TPU v7x, 32 devices: a whole 2x2x4 slice. The times are simulated.
32 devices in a mesh: member: 4 (over y, x), shard: 8 (over z, core).
Axes of the slice: x: 2, y: 2, z: 4, core: 2. Of those that a mesh axis runs over, the one named last changes fastest.
Arguments:
- trunk_out: bfloat16 [128, 8192], P('shard', 'member'), may hold values from -6 to 6
- segment_ids: int32 [128], replicated, may hold values from 0 to 7, never falling along the last dimension, each value on 1 to 32 neighbouring positions
- pair_order: int32 [8], replicated, may hold values from 0 to 7, each once
- w_query: bfloat16 [4, 8, 4096, 128], P('member', 'shard'), may hold values from -0.25 to 0.25
- w_key_value: bfloat16 [4, 8, 1024, 256], P('member', 'shard'), may hold values from -0.0625 to 0.0625
- w_out: bfloat16 [4, 512, 8192], P('member', 'shard'), may hold values from -0.25 to 0.25
- norm_gain: float32 [4, 8192], P('member'), may hold values from 0.1 to 1.9
- reward_weight: float32 [4, 8192], P('member'), may hold values from -0.0625 to 0.0625
Outputs:
- trunk_grad: float32 [128, 8192], P('member', 'shard')
- rewards: float32 [4, 8], P('member')
Inputs may be any that keep to these rules, and one draw needn't show every extreme that they name: `segment_ids`: segment numbers never fall along the tokens; every sequence 0 to 7 has 1 to 32 tokens, and one has exactly 32. Each sequence appears once; sequence pair_order[2 * i] is preferred to sequence pair_order[2 * i + 1].
All inputs are finite; a program needn't handle non-finite values.
Results may differ from a plain program's by a relative error of at most 0.011.
Values may be sent and summed in bfloat16 or wider, within the bound.
No kernel may reach another device: no remote copies, remote signals or barrier semaphores. Data moves between devices by JAX's collectives and lax.ppermute only.
A program may use at most 64 MiB of HBM per device.

v0:
```python
import math

import jax
import jax.numpy as jnp
from jax import lax
from jax.experimental import pallas as pl
from jax.experimental.pallas import tpu as pltpu
from jax.sharding import PartitionSpec as P


HD = 128
SEQS = 8


KERNEL_VMEM = 8 << 20
softcap_limit = 20.0
loss_scale = 256.0
norm_eps = 1e-05


def from_partner(block, axis, stride):
    count = lax.axis_size(axis)
    route = []
    for low in range(count):
        high = low | 1 << stride
        if high != low and high < count:
            route += [(low, high), (high, low)]
    return lax.ppermute(block, axis, route)


def partner_swap(values, bit_number):
    return from_partner(values, "shard", bit_number)


def group_total(values, bit_list):
    for bit_number in bit_list:
        values = values + partner_swap(values, bit_number)
    return values


def pair_join(own_part, other_part, pair_side, join_axis):
    first_part = jnp.where(pair_side == 0, own_part, other_part)
    second_part = jnp.where(pair_side == 0, other_part, own_part)
    return jnp.concatenate([first_part, second_part], axis=join_axis)


def general_device(
    trunk_out, segment_ids, pair_order, w_query, w_key_value, w_out, norm_gain, reward_weight
):
    n_shard = lax.axis_size("shard")
    query_heads = n_shard // 2
    kv_count = max(1, query_heads // 8)
    group_size = query_heads // kv_count
    shard_index = lax.axis_index("shard")
    pair_side = shard_index % 2
    head_index = shard_index // 2
    block_index = shard_index % (2 * group_size) // 2
    local_rows, _ = trunk_out.shape
    features = lax.all_gather(trunk_out, "member", axis=1, tiled=True)
    gathered = lax.all_gather(features, "shard", axis=0, tiled=True)
    tok_count, model_width = gathered.shape
    half_width = model_width // 2
    half_rows = tok_count // 2
    half_head = HD // 2
    row_block = half_width // group_size
    scale_factor = 1.0 / math.sqrt(HD)
    group_bits = list(range((2 * group_size).bit_length() - 1))
    query_piece = w_query[0, 0]
    kv_piece = w_key_value[0, 0]
    out_rows = w_out[0]
    gain_vector = norm_gain[0]
    head_weight = reward_weight[0]
    positions = jnp.arange(tok_count)
    own_start = pair_side * half_rows
    own_positions = own_start + jnp.arange(half_rows)
    own_segments = lax.dynamic_slice_in_dim(segment_ids, own_start, half_rows, 0)
    allowed = (own_segments[:, None] == segment_ids[None, :]) & (
        positions[None, :] <= own_positions[:, None]
    )
    member_of = jnp.arange(SEQS)[:, None] == segment_ids[None, :]
    pooling = member_of.astype(jnp.bfloat16)
    lengths = jnp.sum(member_of.astype(jnp.float32), axis=1)
    own_pooling = lax.dynamic_slice_in_dim(pooling, own_start, half_rows, 1)
    half_features = lax.dynamic_slice_in_dim(gathered, pair_side * half_width, half_width, 1)
    query_partial = jnp.dot(half_features, query_piece, preferred_element_type=jnp.float32)
    kept_rows = lax.dynamic_slice_in_dim(query_partial, own_start, half_rows, 0)
    sent_rows = lax.dynamic_slice_in_dim(query_partial, half_rows - own_start, half_rows, 0)
    queries = (kept_rows + partner_swap(sent_rows, 0)).astype(jnp.bfloat16)
    kv_features = lax.dynamic_slice_in_dim(half_features, block_index * row_block, row_block, 1)
    kv_values = group_total(
        jnp.dot(kv_features, kv_piece, preferred_element_type=jnp.float32), group_bits
    ).astype(jnp.bfloat16)
    key_full = kv_values[:, :HD]
    value_full = kv_values[:, HD:]
    raw_scores = (
        jnp.einsum("td,sd->ts", queries, key_full, preferred_element_type=jnp.float32)
        * scale_factor
    )
    capped = softcap_limit * jnp.tanh(raw_scores / softcap_limit)
    weights_exp = jnp.where(allowed, jnp.exp(capped), 0.0)
    attention = weights_exp / jnp.sum(weights_exp, axis=1, keepdims=True)
    attention_low = attention.astype(jnp.bfloat16)
    attended = jnp.dot(attention_low, value_full, preferred_element_type=jnp.float32).astype(
        jnp.bfloat16
    )
    seq_part = jnp.dot(own_pooling, attended, preferred_element_type=jnp.float32)
    seq_total = seq_part + partner_swap(seq_part, 0)
    seq_mean = (seq_total / lengths[:, None]).astype(jnp.bfloat16)
    own_dims = lax.dynamic_slice_in_dim(seq_mean, pair_side * half_head, half_head, 1)
    head_part = jnp.dot(own_dims, out_rows, preferred_element_type=jnp.float32)
    pooled_attn = lax.psum(head_part, "shard")
    pooled_input = jnp.dot(pooling, gathered, preferred_element_type=jnp.float32) / lengths[:, None]
    hidden = pooled_input + pooled_attn
    inverse_rms = lax.rsqrt(jnp.mean(hidden * hidden, axis=1) + norm_eps)
    normed = hidden * inverse_rms[:, None] * gain_vector
    rewards = jnp.sum(normed * head_weight, axis=1)
    seq_ids = jnp.arange(SEQS)
    chosen = (pair_order[0::2][:, None] == seq_ids[None, :]).astype(jnp.float32)
    rejected = (pair_order[1::2][:, None] == seq_ids[None, :]).astype(jnp.float32)
    margin = jnp.sum(chosen * rewards, axis=1) - jnp.sum(rejected * rewards, axis=1)
    pair_slope = loss_scale * jax.nn.sigmoid(-margin)
    reward_grad = jnp.sum(rejected * pair_slope[:, None], axis=0) - jnp.sum(
        chosen * pair_slope[:, None], axis=0
    )
    scaled_grad = reward_grad[:, None] * head_weight * gain_vector
    hidden_grad = inverse_rms[:, None] * (
        scaled_grad
        - hidden * (inverse_rms**2)[:, None] * jnp.mean(hidden * scaled_grad, axis=1, keepdims=True)
    )
    per_token = hidden_grad / lengths[:, None]
    grad_low = hidden_grad.astype(jnp.bfloat16)
    grad_dims = (
        jnp.einsum("jd,ed->je", grad_low, out_rows, preferred_element_type=jnp.float32)
        / lengths[:, None]
    )
    mean_grad = pair_join(grad_dims, partner_swap(grad_dims, 0), pair_side, 1)
    out_grad = jnp.take(mean_grad, own_segments, axis=0).astype(jnp.bfloat16)
    prob_grad = jnp.einsum("td,sd->ts", out_grad, value_full, preferred_element_type=jnp.float32)
    score_grad = attention * (prob_grad - jnp.sum(attention * prob_grad, axis=1, keepdims=True))
    raw_grad = (score_grad * (1.0 - (capped / softcap_limit) ** 2) * scale_factor).astype(
        jnp.bfloat16
    )
    query_grad = jnp.dot(raw_grad, key_full, preferred_element_type=jnp.float32).astype(
        jnp.bfloat16
    )
    key_grad = jnp.einsum("ts,td->sd", raw_grad, queries, preferred_element_type=jnp.float32)
    value_grad = jnp.einsum(
        "ts,td->sd", attention_low, out_grad, preferred_element_type=jnp.float32
    )
    kv_grad = group_total(jnp.concatenate([key_grad, value_grad], axis=1), group_bits).astype(
        jnp.bfloat16
    )
    query_wire = lax.optimization_barrier(query_grad).astype(jnp.float32)
    query_all = pair_join(
        query_grad, partner_swap(query_wire, 0).astype(jnp.bfloat16), pair_side, 0
    )
    grad_half = jnp.einsum("td,rd->tr", query_all, query_piece, preferred_element_type=jnp.float32)
    kv_term = jnp.einsum("te,re->tr", kv_grad, kv_piece, preferred_element_type=jnp.float32)
    start_col = block_index * row_block
    grad_half = lax.dynamic_update_slice_in_dim(
        grad_half,
        lax.dynamic_slice_in_dim(grad_half, start_col, row_block, 1) + kv_term,
        start_col,
        1,
    )
    pair_rows = 2 * local_rows
    start_row = head_index * pair_rows
    pair_segments = lax.dynamic_slice_in_dim(segment_ids, start_row, pair_rows, 0)
    token_half = lax.dynamic_slice_in_dim(per_token, pair_side * half_width, half_width, 1)
    direct = jnp.take(token_half, pair_segments, axis=0)
    grad_half = lax.dynamic_update_slice_in_dim(
        grad_half,
        lax.dynamic_slice_in_dim(grad_half, start_row, pair_rows, 0) + direct,
        start_row,
        0,
    )
    by_member = lax.psum_scatter(grad_half, "member", scatter_dimension=0, tiled=True)
    member_rows = by_member.shape[0]
    placed = lax.dynamic_update_slice_in_dim(
        jnp.zeros((member_rows, model_width), jnp.float32), by_member, pair_side * half_width, 1
    )
    trunk_grad = lax.psum_scatter(placed, "shard", scatter_dimension=1, tiled=True)
    return (trunk_grad, rewards[None])


def route_pairs(target):
    pairs = []
    for member in range(4):
        for height in range(4):
            for core in range(2):
                to = target(member, height, core)
                if to is not None:
                    pairs.append((member * 8 + height * 2 + core, to[0] * 8 + to[1] * 2 + to[2]))
    return pairs


def send(block, target):
    return lax.ppermute(block, ("member", "shard"), route_pairs(target))


def core_swap(block):
    return send(block, lambda m, z, k: (m, z, 1 - k))


def matmul(left, right):
    return jnp.dot(left, right, preferred_element_type=jnp.float32)


def matmul_nt(left, right):
    return lax.dot_general(
        left, right, (((1,), (1,)), ((), ())), preferred_element_type=jnp.float32
    )


def matmul_tn(left, right):
    return lax.dot_general(
        left, right, (((0,), (0,)), ((), ())), preferred_element_type=jnp.float32
    )


def height_total(block, core, wire):
    sent = block.astype(wire)
    near = send(sent, lambda m, z, k: (m, z ^ (1 + k), k))
    half = jnp.where(core == 0, sent[:, :HD], sent[:, HD:])
    far = send(half, lambda m, z, k: (m, z ^ 3, k)).astype(jnp.float32)
    zero = jnp.zeros_like(far)
    spread = jnp.concatenate(
        [jnp.where(core == 0, far, zero), jnp.where(core == 0, zero, far)], axis=1
    )
    mine = jnp.where(core == 0, sent.astype(jnp.float32), 0.0) + near.astype(jnp.float32) + spread
    return mine, core_swap(mine)


def split_high_low(value):
    high = value.astype(jnp.bfloat16)
    return high, (value - high.astype(jnp.float32)).astype(jnp.bfloat16)


def iota(shape, dimension):
    return lax.broadcasted_iota(jnp.int32, shape, dimension)


def one_hot(condition):
    return condition.astype(jnp.float32).astype(jnp.bfloat16)


def pooling_of(segments):
    return one_hot(iota((SEQS, segments.shape[1]), 0) == segments)


def lengths_of(segments):
    return jnp.sum(
        (iota((SEQS, segments.shape[1]), 0) == segments).astype(jnp.float32), axis=1, keepdims=True
    )


def local_call(kernel, outputs, *operands):
    vmem = pl.BlockSpec(memory_space=pltpu.VMEM)
    smem = pl.BlockSpec(memory_space=pltpu.SMEM)
    return pl.pallas_call(
        kernel,
        out_shape=[jax.ShapeDtypeStruct(shape, dtype) for shape, dtype in outputs],
        in_specs=[smem] + [vmem] * (len(operands) - 1),
        out_specs=[vmem] * len(outputs),
        compiler_params=pltpu.CompilerParams(vmem_limit_bytes=KERNEL_VMEM),
    )(*operands)


def prepare_kernel(
    place, segment_ids, norm_gain, reward_weight, weight,
    segments_out, gain_out, weight_out, head_weight, sems,
):
    width = gain_out.shape[1]
    start = pl.multiple_of(place[1] % 2 * width, width)
    copies = [
        pltpu.make_async_copy(weight, weight_out, sems.at[0]),
        pltpu.make_async_copy(segment_ids, segments_out, sems.at[1]),
        pltpu.make_async_copy(norm_gain.at[:, pl.ds(start, width)], gain_out, sems.at[2]),
        pltpu.make_async_copy(reward_weight.at[:, pl.ds(start, width)], head_weight, sems.at[3]),
    ]
    for copy in copies:
        copy.start()
    for copy in copies:
        copy.wait()
    gain_out[...] = gain_out[...] * head_weight[...]


def prepare(place, segments, norm_gain, reward_weight, weight):
    width = norm_gain.shape[1] // 2
    return pl.pallas_call(
        prepare_kernel,
        out_shape=[
            jax.ShapeDtypeStruct(segments.shape, segments.dtype),
            jax.ShapeDtypeStruct((1, width), norm_gain.dtype),
            jax.ShapeDtypeStruct(weight.shape, weight.dtype),
        ],
        in_specs=[pl.BlockSpec(memory_space=pltpu.SMEM)]
        + [pl.BlockSpec(memory_space=pl.ANY)] * 4,
        out_specs=[pl.BlockSpec(memory_space=pltpu.VMEM)] * 3,
        scratch_shapes=[
            pltpu.VMEM((1, width), reward_weight.dtype),
            pltpu.SemaphoreType.DMA((4,)),
        ],
        compiler_params=pltpu.CompilerParams(vmem_limit_bytes=KERNEL_VMEM),
    )(place, segments, norm_gain, reward_weight, weight)


def stack_kernel(place, *refs):
    pieces, out, sems = refs[:-2], refs[-2], refs[-1]
    rows = pieces[0].shape[0]
    copies = []
    for step, ref in enumerate(pieces):
        start = pl.multiple_of(((place[1] // 2) ^ step) * rows, rows)
        copies.append(pltpu.make_async_copy(ref, out.at[pl.ds(start, rows), :], sems.at[step]))
    for copy in copies:
        copy.start()
    for copy in copies:
        copy.wait()


def stack_rows(place, blocks):
    rows, width = blocks[0].shape
    return pl.pallas_call(
        stack_kernel,
        out_shape=jax.ShapeDtypeStruct((len(blocks) * rows, width), blocks[0].dtype),
        in_specs=[pl.BlockSpec(memory_space=pltpu.SMEM)]
        + [pl.BlockSpec(memory_space=pl.ANY)] * len(blocks),
        out_specs=pl.BlockSpec(memory_space=pltpu.VMEM),
        scratch_shapes=[pltpu.SemaphoreType.DMA((len(blocks),))],
        compiler_params=pltpu.CompilerParams(vmem_limit_bytes=KERNEL_VMEM),
    )(place, *blocks)


def kv_columns_kernel(place, own, other, out):
    width = out.shape[1]
    rows = own.shape[0] // 4
    core = place[1] % 2
    start = pl.multiple_of(place[1] // 2 % 2 * width, width)
    for source, side in ((own, core), (other, 1 - core)):
        for step in range(4):
            to = pl.multiple_of((2 * step + side) * rows, rows)
            out[pl.ds(to, rows), :] = source[step * rows : (step + 1) * rows, pl.ds(start, width)]


def query_kernel(place, own, other, first, second, out_first, out_second):
    rows = own.shape[0] // 4
    core = place[1] % 2
    for weight, out in ((first, out_first), (second, out_second)):
        for source, side in ((own, core), (other, 1 - core)):
            part = matmul(source[...], weight[...])
            for step in range(4):
                to = pl.multiple_of((2 * step + side) * rows, rows)
                out[pl.ds(to, rows), :] = part[step * rows : (step + 1) * rows]


def kv_kernel(place, segments, first, second, weight, out, pooled):
    far = (place[1] // 4) ^ (place[0] % 2)
    columns = jnp.where(far == 0, first[...], second[...])
    out[...] = matmul(columns, weight[...])
    pooled[...] = matmul(pooling_of(segments[...]), columns) / lengths_of(segments[...])


def forward_kernel(
    place, segments, mine, swapped, kv_mine, kv_swapped, pooled, out_own, out_other, gain,
    queries_out, kv_out, attention_out, capped_out, message,
):
    bf16 = jnp.bfloat16
    core, height = place[1] % 2, place[1] // 2
    queries = (mine[:, :HD] + swapped[:, :HD]).astype(bf16)
    kv_values = (kv_mine[...] + kv_swapped[...]).astype(bf16)
    queries_out[...] = queries
    kv_out[...] = kv_values
    keys, values = kv_values[:, :HD], kv_values[:, HD:]
    pooling = pooling_of(segments[...])
    lengths = lengths_of(segments[...])
    tokens = pooling.shape[1]
    same = matmul_tn(pooling, pooling) > 0.5
    allowed = same & (iota((tokens, tokens), 1) <= iota((tokens, tokens), 0))
    raw_scores = matmul_nt(queries, keys) * (1.0 / math.sqrt(HD))
    capped = softcap_limit * jnp.tanh(raw_scores / softcap_limit)
    weights_exp = jnp.where(allowed, jnp.exp(capped), 0.0)
    attention = weights_exp / jnp.sum(weights_exp, axis=1, keepdims=True)
    attention_out[...] = attention
    capped_out[...] = capped
    attended = matmul(attention.astype(bf16), values).astype(bf16)
    seq_mean = (matmul(pooling, attended) / lengths).astype(bf16)
    half = out_own.shape[0]
    low, high = seq_mean[:, :half], seq_mean[:, half:]
    part = matmul(jnp.where(core == 0, low, high), out_own[...]) + matmul(
        jnp.where(core == 0, high, low), out_other[...]
    )
    width = pooled.shape[1]
    part = jnp.concatenate(
        [
            part[:, n * width : (n + 1) * width] + jnp.where(height == n, pooled[...], 0.0)
            for n in range(part.shape[1] // width)
        ],
        axis=1,
    )
    product_high, product_low = split_high_low(jnp.sum(part * gain[...], axis=1, keepdims=True))
    lane = iota((SEQS, HD), 1)
    message[:, : part.shape[1]] = part.astype(bf16)
    message[:, part.shape[1] :] = jnp.where(
        lane == 0,
        product_high.astype(jnp.float32),
        jnp.where(lane == 1, product_low.astype(jnp.float32), 0.0),
    ).astype(bf16)


def stats_kernel(
    place, first, second, third, fourth, out_own, out_other, gain, hidden_out, report
):
    core = place[1] % 2
    half_width = hidden_out.shape[1]
    f32 = jnp.float32
    total = (first[...].astype(f32) + second[...].astype(f32)) + (
        third[...].astype(f32) + fourth[...].astype(f32)
    )
    hidden = total[:, :half_width]
    hidden_out[...] = hidden
    stacked = jnp.concatenate([hidden, jnp.broadcast_to(gain[...], hidden.shape)], axis=0)
    stacked = stacked.astype(jnp.bfloat16)
    along_own = matmul_nt(stacked, out_own[...])
    along_other = matmul_nt(stacked, out_other[...])
    half = along_own.shape[1]
    report[: 2 * SEQS, :half] = jnp.where(core == 0, along_own, along_other)
    report[: 2 * SEQS, half:] = jnp.where(core == 0, along_other, along_own)
    squares = jnp.sum(hidden * hidden, axis=1, keepdims=True)
    products = total[:, half_width : half_width + 1] + total[:, half_width + 1 : half_width + 2]
    lane = iota((SEQS, HD), 1)
    report[2 * SEQS :, :] = jnp.where(lane == 0, squares, jnp.where(lane == 1, products, 0.0))


def member_order(place, tokens):
    rows = tokens // 4
    position = iota((tokens, tokens), 0)
    token = rows * (place[0] ^ (position // rows)) + position % rows
    return one_hot(iota((tokens, tokens), 1) == token)


def backward_kernel(
    place, pairs, segments, mine, swapped, queries, kv_values, attention, capped,
    query_grad, kv_grad, rewards_out, factors,
):
    bf16, f32 = jnp.bfloat16, jnp.float32
    width = place[2].astype(f32)
    report = mine[...] + swapped[...]
    hidden_along, gain_along = report[:SEQS], report[SEQS : 2 * SEQS]
    square_sum, product_sum = report[2 * SEQS :, 0:1], report[2 * SEQS :, 1:2]
    pooling = pooling_of(segments[...])
    lengths = lengths_of(segments[...])
    inverse_rms = lax.rsqrt(square_sum / width + norm_eps)
    rewards = product_sum * inverse_rms
    diagonal = iota((SEQS, SEQS), 0) == iota((SEQS, SEQS), 1)
    rewards_row = jnp.sum(jnp.where(diagonal, rewards, 0.0), axis=0, keepdims=True)
    rewards_out[...] = rewards_row
    signs = pairs[...]
    margin = jnp.sum(signs * rewards_row, axis=1, keepdims=True)
    pair_slope = loss_scale / (1.0 + jnp.exp(margin))
    grad_row = -jnp.sum(signs * pair_slope, axis=0, keepdims=True)
    reward_grad = jnp.sum(jnp.where(diagonal, grad_row, 0.0), axis=1, keepdims=True)
    gain_factor = inverse_rms * reward_grad / lengths
    hidden_factor = inverse_rms * inverse_rms * inverse_rms * (
        reward_grad * product_sum / width
    ) / lengths
    factors[0] = jnp.broadcast_to(gain_factor, (SEQS, HD))
    factors[1] = jnp.broadcast_to(hidden_factor, (SEQS, HD))
    mean_grad = (gain_factor * gain_along - hidden_factor * hidden_along).astype(bf16)
    out_grad = matmul_tn(pooling, mean_grad).astype(bf16)
    keys, values = kv_values[:, :HD], kv_values[:, HD:]
    attn = attention[...]
    prob_grad = matmul_nt(out_grad, values)
    score_grad = attn * (prob_grad - jnp.sum(attn * prob_grad, axis=1, keepdims=True))
    ratio = capped[...] / softcap_limit
    raw_grad = (score_grad * (1.0 - ratio * ratio) * (1.0 / math.sqrt(HD))).astype(bf16)
    order = member_order(place, attn.shape[0])
    query_grad[...] = matmul(order, matmul(raw_grad, keys).astype(bf16)).astype(bf16)
    kv_grad[:, :HD] = matmul_tn(raw_grad, queries[...])
    kv_grad[:, HD:] = matmul_tn(attn.astype(bf16), out_grad)


def far_kernel(place, grad, weight, far):
    width = far.shape[1] // 3
    for step in (1, 2, 3):
        start = pl.multiple_of(((place[1] // 2) ^ step) * width, width)
        far[:, (step - 1) * width : step * width] = matmul_nt(
            grad[...], weight[pl.ds(start, width), :]
        ).astype(far.dtype)


def near_kernel(
    place, segments, grad, weight, kv_mine, kv_swapped, kv_weight, hidden, gain, factors, near
):
    bf16 = jnp.bfloat16
    width = near.shape[1]
    start = pl.multiple_of(place[1] // 2 * width, width)
    order = member_order(place, near.shape[0])
    kv_grad = (kv_mine[...] + kv_swapped[...]).astype(bf16)
    kv_turned = matmul(order, kv_grad).astype(bf16)
    seq_turned = matmul_nt(order, pooling_of(segments[...])).astype(bf16)
    gain_block = gain[:, pl.ds(start, width)]
    high, low = split_high_low(
        factors[0][:, 0:1] * gain_block - factors[1][:, 0:1] * hidden[:, pl.ds(start, width)]
    )
    near[...] = (
        matmul_nt(grad[...], weight[pl.ds(start, width), :])
        + matmul_nt(kv_turned, kv_weight[...])
        + matmul(seq_turned, high)
        + matmul(seq_turned, low)
    ).astype(bf16)


def member_sum_kernel(place, own, first, second, third, out):
    f32 = jnp.float32
    rows = out.shape[0]
    out[...] = (
        (own[:rows, :].astype(f32) + first[...].astype(f32))
        + (second[...].astype(f32) + third[...].astype(f32))
    ).astype(out.dtype)


def fast_device(
    trunk_out, segment_ids, pair_order, w_query, w_key_value, w_out, norm_gain, reward_weight
):
    bf16, f32 = jnp.bfloat16, jnp.float32
    member = lax.axis_index("member")
    shard = lax.axis_index("shard")
    core = shard % 2
    col = member % 2
    local_width = trunk_out.shape[1]
    tokens = segment_ids.shape[0]
    half_width = w_query.shape[2]
    block_width = w_key_value.shape[2]
    member_rows = tokens // 4
    query_piece = w_query[0, 0]
    kv_piece = w_key_value[0, 0]
    place = jnp.stack([member, shard, jnp.int32(2 * half_width)])

    stack = [trunk_out] + [send(trunk_out, lambda m, z, k, d=d: (m, z ^ d, k)) for d in (1, 2, 3)]

    cuts = [
        lax.dynamic_slice_in_dim(query_piece, (col ^ r) * local_width, local_width, 0)
        for r in (0, 1)
    ]
    weights = [
        send(cuts[r], lambda m, z, k, r=r: (2 * k + ((m % 2) ^ r), z, m // 2))
        for r in (0, 1)
    ]

    segments, gain, kv_weight = prepare(
        place, segment_ids[None, :], norm_gain, reward_weight, kv_piece
    )
    column_own = stack_rows(place, stack)
    column_other = core_swap(column_own)
    block_shape = ((tokens, block_width), bf16)
    (kv_sent,) = local_call(kv_columns_kernel, [block_shape], place, column_own, column_other)
    kv_got = [
        send(
            kv_sent,
            lambda m, z, k, r=r: (2 * k + ((m % 2) ^ r), z, m // 2) if m % 2 == z // 2 else None,
        )
        for r in (0, 1)
    ]
    head_shape = ((tokens, HD), f32)
    query_parts = local_call(
        query_kernel, [head_shape] * 2, place, column_own, column_other, *weights
    )
    query_got = [
        send(part, lambda m, z, k, r=r: (2 * k + ((m % 2) ^ r), z, m // 2))
        for r, part in enumerate(query_parts)
    ]
    kv_part, pooled = local_call(
        kv_kernel,
        [((tokens, 2 * HD), f32), ((SEQS, block_width), f32)],
        place,
        segments,
        *kv_got,
        kv_weight,
    )
    mixed = jnp.concatenate([query_got[0] + query_got[1], kv_part], axis=1)
    swapped = core_swap(mixed)
    kv_mine, kv_swapped = height_total(mixed[:, HD:] + swapped[:, HD:], core, jnp.float16)

    out_rows, _ = lax.optimization_barrier((w_out[0], mixed))
    out_own = lax.dynamic_slice_in_dim(out_rows, core * half_width, half_width, 1)
    out_other = core_swap(
        lax.dynamic_slice_in_dim(out_rows, (1 - core) * half_width, half_width, 1)
    )

    queries, kv_values, attention, capped, message = local_call(
        forward_kernel,
        [
            ((tokens, HD), bf16),
            ((tokens, 2 * HD), bf16),
            ((tokens, tokens), f32),
            ((tokens, tokens), f32),
            ((SEQS, half_width + HD), bf16),
        ],
        place, segments, mixed, swapped, kv_mine, kv_swapped, pooled, out_own, out_other, gain,
    )
    others = [send(message, lambda m, z, k, d=d: (m, z ^ d, k)) for d in (1, 2, 3)]
    hidden, report = local_call(
        stats_kernel,
        [((SEQS, half_width), f32), ((3 * SEQS, HD), f32)],
        place, message, *others, out_own, out_other, gain,
    )
    seq_ids = jnp.arange(SEQS)[None, :]
    pairs = (pair_order[0::2][:, None] == seq_ids).astype(f32) - (
        pair_order[1::2][:, None] == seq_ids
    ).astype(f32)
    pairs = jnp.concatenate([pairs, jnp.zeros_like(pairs)], axis=0)
    query_grad, kv_grad, rewards, factors = local_call(
        backward_kernel,
        [
            ((tokens, HD), bf16),
            ((tokens, 2 * HD), f32),
            ((1, SEQS), f32),
            ((2, SEQS, HD), f32),
        ],
        place, pairs, segments, report, core_swap(report), queries, kv_values, attention, capped,
    )

    kv_mine, kv_swapped = height_total(kv_grad, core, bf16)
    (far_grad,) = local_call(
        far_kernel, [((tokens, 3 * block_width), bf16)], place, query_grad, query_piece
    )
    far_got = [
        send(far_grad[d * member_rows : (d + 1) * member_rows], lambda m, z, k, d=d: (m ^ d, z, k))
        for d in (1, 2, 3)
    ]
    (near_grad,) = local_call(
        near_kernel,
        [block_shape],
        place, segments, query_grad, query_piece, kv_mine, kv_swapped, kv_weight, hidden, gain,
        factors,
    )
    near_got = [
        send(near_grad[d * member_rows : (d + 1) * member_rows], lambda m, z, k, d=d: (m ^ d, z, k))
        for d in (1, 2, 3)
    ]
    (far_sum,) = local_call(
        member_sum_kernel, [((member_rows, 3 * block_width), bf16)], place, far_grad, *far_got
    )
    (near_sum,) = local_call(
        member_sum_kernel, [((member_rows, block_width), bf16)], place, near_grad, *near_got
    )
    pieces = [near_sum] + [far_sum[:, e * block_width : (e + 1) * block_width] for e in range(3)]
    total = 0.0
    for d in (1, 2, 3, 0):
        got = send(pieces[d], lambda m, z, k, d=d: (m, (4 * k + (z ^ d)) // 2, z % 2 ^ d % 2))
        total = total + got.astype(f32)
    return (total, rewards)


def solution(mesh):
    fast = dict(mesh.shape) == {"member": 4, "shard": 8}
    placed = (
        P("shard", "member"),
        P(),
        P(),
        P("member", "shard", None, None),
        P("member", "shard", None, None),
        P("member", "shard", None),
        P("member", None),
        P("member", None),
    )
    return jax.shard_map(
        fast_device if fast else general_device,
        mesh=mesh,
        in_specs=placed,
        out_specs=(P("member", "shard"), P("member", None)),
        check_vma=False,
    )
```

profile of v0, /device:TPU:0, one launch (start us, length us, event | category | flops | bytes accessed | tf_op | source)
XLA Modules:
  0.0 91.9 jit_solution(15063664672352526880)
XLA Ops:
  0.6 3.1 %collective-permute-start = (bf16[16,2048]{1,0:T(8,128)(2,1)}, bf16[16,2048]{1,0:T(8,128)(2,1)S(1)}, u32[]{:S(2)}, u32[]{:S(2)}) collective-permute-start(bf16[16,2048]{1,0:T(8,128)(2,1)} %refs_0_.1), channel_id=1, source_target_pairs={{0,2},{1,3},{2,0},{3,1},{4,6},{5,7},{6,4},{7,5},{8,10},{9,11},{10,... | collective-permute-start | bytes 196616 | tf_op jit(solution)/shard_map/ppermute | solution.py:198
  3.7 2.6 %collective-permute-start.1 = (bf16[16,2048]{1,0:T(8,128)(2,1)}, bf16[16,2048]{1,0:T(8,128)(2,1)S(1)}, u32[]{:S(2)}, u32[]{:S(2)}) collective-permute-start(bf16[16,2048]{1,0:T(8,128)(2,1)} %refs_0_.1), channel_id=1, source_target_pairs={{0,4},{1,5},{2,6},{3,7},{4,0},{5,1},{6,2},{7,3},{8,12},{9,13},{10,... | collective-permute-start | bytes 196616 | tf_op jit(solution)/shard_map/ppermute | solution.py:198
  8.3 1.8 %collective-permute-start.5 = (bf16[2048,128]{1,0:T(8,128)(2,1)S(1)}, bf16[2048,128]{1,0:T(8,128)(2,1)S(1)}, u32[]{:S(2)}, u32[]{:S(2)}) collective-permute-start(bf16[2048,128]{1,0:T(8,128)(2,1)S(1)} %get-tuple-element.42), channel_id=1, source_target_pairs={{0,8},{1,24},{2,10},{3,26},{4,12},{5,28},{6,14},{7,30},{8,0},{9,16... | collective-permute-start | bytes 1572872 | tf_op jit(solution)/shard_map/ppermute | solution.py:198
  13.7 1.5 %collective-permute-done.3.other = bf16[64,2048]{1,0:T(8,128)(2,1)S(1)} collective-permute-done((bf16[64,2048]{1,0:T(8,128)(2,1)S(1)}, bf16[64,2048]{1,0:T(8,128)(2,1)S(1)}, u32[]{:S(2)}, u32[]{:S(2)}) %collective-permute-start.3) | collective-permute-done | bytes 262176 | tf_op jit(solution)/shard_map/ppermute | solution.py:198
  16.6 3.4 %collective-permute-start.9 = (bf16[128,1024]{1,0:T(8,128)(2,1)S(1)}, bf16[128,1024]{1,0:T(8,128)(2,1)S(1)}, u32[]{:S(2)}, u32[]{:S(2)}) collective-permute-start(bf16[128,1024]{1,0:T(8,128)(2,1)S(1)} %shard_map.98), channel_id=1, source_target_pairs={{0,8},{1,24},{2,10},{3,26},{12,4},{13,20},{14,6},{15,22},{16,9},{1... | collective-permute-start | bytes 786440 | tf_op jit(solution)/shard_map/ppermute | solution.py:198
  23.1 2.0 %collective-permute-start.7 = (f32[128,128]{1,0:T(8,128)S(1)}, f32[128,128]{1,0:T(8,128)S(1)}, u32[]{:S(2)}, u32[]{:S(2)}) collective-permute-start(f32[128,128]{1,0:T(8,128)S(1)} %get-tuple-element.23), channel_id=1, source_target_pairs={{0,8},{1,24},{2,10},{3,26},{4,12},{5,28},{6,14},{7,30},{8,0},{9,16... | collective-permute-start | bytes 196616 | tf_op jit(solution)/shard_map/ppermute | solution.py:198
  26.4 1.7 %collective-permute-done.7 = f32[128,128]{1,0:T(8,128)S(1)} collective-permute-done((f32[128,128]{1,0:T(8,128)S(1)}, f32[128,128]{1,0:T(8,128)S(1)}, u32[]{:S(2)}, u32[]{:S(2)}) %collective-permute-start.7) | collective-permute-done | bytes 65568 | tf_op jit(solution)/shard_map/ppermute | solution.py:198
  29.0 5.2 %collective-permute-start.10 = (f32[128,384]{1,0:T(8,128)S(1)}, f32[128,384]{1,0:T(8,128)S(1)}, u32[]{:S(2)}, u32[]{:S(2)}) collective-permute-start(f32[128,384]{1,0:T(8,128)S(1)} %pad_maximum_fusion.mine), channel_id=1, source_target_pairs={{0,1},{1,0},{2,3},{3,2},{4,5},{5,4},{6,7},{7,6},{8,9},{9,8},{10,11... | collective-permute-start | bytes 589832 | tf_op jit(solution)/shard_map/ppermute | solution.py:198
  35.3 4.7 %collective-permute-start.12 = (f16[128,128]{1,0:T(8,128)(2,1)S(1)}, f16[128,128]{1,0:T(8,128)(2,1)S(1)}, u32[]{:S(2)}, u32[]{:S(2)}) collective-permute-start(f16[128,128]{1,0:T(8,128)(2,1)S(1)} %slice_select_fusion.1), channel_id=1, source_target_pairs={{0,6},{1,7},{2,4},{3,5},{4,2},{5,3},{6,0},{7,1},{8,14},{9,15},{10,... | collective-permute-start | bytes 98312 | tf_op jit(solution)/shard_map/ppermute | solution.py:198
  40.2 1.7 %collective-permute-done.12 = f16[128,128]{1,0:T(8,128)(2,1)S(1)} collective-permute-done((f16[128,128]{1,0:T(8,128)(2,1)S(1)}, f16[128,128]{1,0:T(8,128)(2,1)S(1)}, u32[]{:S(2)}, u32[]{:S(2)}) %collective-permute-start.12) | collective-permute-done | bytes 32800 | tf_op jit(solution)/shard_map/ppermute | solution.py:198
  41.9 3.3 %collective-permute-done.11 = f16[128,256]{1,0:T(8,128)(2,1)S(1)} collective-permute-done((f16[128,256]{1,0:T(8,128)(2,1)S(1)}, f16[128,256]{1,0:T(8,128)(2,1)S(1)}, u32[]{:S(2)}, u32[]{:S(2)}) %collective-permute-start.11) | collective-permute-done | bytes 65568 | tf_op jit(solution)/shard_map/ppermute | solution.py:198
  46.6 1.5 %shard_map.100 = (bf16[128,128]{1,0:T(8,128)(2,1)S(1)}, bf16[128,256]{1,0:T(8,128)(2,1)S(1)}, f32[128,128]{1,0:T(8,128)S(1)}, f32[128,128]{1,0:T(8,128)S(1)}, bf16[8,4224]{1,0:T(8,128)(2,1)S(1)}) custom-call(s32[3]{0:T(128)S(1)} %pad_add_fusion.place, s32[1,128]{1,0:T(1,128)S(1)} %get-tuple-element.21.segments, f32[128,384]{1,0:T(8,128)S(1)} %pad_maximum_fusion.mine, ...), custom_call_target="tpu_custom_call" | custom-call | tf_op jit(solution)/shard_map/pallas_call | solution.py:260
  48.2 1.5 %collective-permute-start.16 = (bf16[8,4224]{1,0:T(8,128)(2,1)S(1)}, bf16[8,4224]{1,0:T(8,128)(2,1)S(1)}, u32[]{:S(2)}, u32[]{:S(2)}) collective-permute-start(bf16[8,4224]{1,0:T(8,128)(2,1)S(1)} %get-tuple-element.29.first), channel_id=1, source_target_pairs={{0,4},{1,5},{2,6},{3,7},{4,0},{5,1},{6,2},{7,3},{8,12},{9,13},{10,... | collective-permute-start | bytes 202760 | tf_op jit(solution)/shard_map/ppermute | solution.py:198
  49.7 2.8 %collective-permute-start.17 = (bf16[8,4224]{1,0:T(8,128)(2,1)S(1)}, bf16[8,4224]{1,0:T(8,128)(2,1)S(1)}, u32[]{:S(2)}, u32[]{:S(2)}) collective-permute-start(bf16[8,4224]{1,0:T(8,128)(2,1)S(1)} %get-tuple-element.29.first), channel_id=1, source_target_pairs={{0,6},{1,7},{2,4},{3,5},{4,2},{5,3},{6,0},{7,1},{8,14},{9,15},{10,... | collective-permute-start | bytes 202760 | tf_op jit(solution)/shard_map/ppermute | solution.py:198
  53.4 3.6 %collective-permute-done.16.third = bf16[8,4224]{1,0:T(8,128)(2,1)S(1)} collective-permute-done((bf16[8,4224]{1,0:T(8,128)(2,1)S(1)}, bf16[8,4224]{1,0:T(8,128)(2,1)S(1)}, u32[]{:S(2)}, u32[]{:S(2)}) %collective-permute-start.16) | collective-permute-done | bytes 67616 | tf_op jit(solution)/shard_map/ppermute | solution.py:198
  59.1 1.7 %shard_map.102 = (bf16[128,128]{1,0:T(8,128)(2,1)S(1)}, f32[128,256]{1,0:T(8,128)S(1)}, f32[1,8]{1,0:T(1,128)}, f32[2,8,128]{2,1,0:T(8,128)S(1)}) custom-call(s32[3]{0:T(128)S(1)} %pad_add_fusion.place, f32[8,8]{1,0:T(8,128)S(1)} %concatenate.12.pairs, s32[1,128]{1,0:T(1,128)S(1)} %get-tuple-element.21.segments, f32[24,128]{1,0:T(8,128)S(1)} %get-tuple-element.30.mine, ...), custom_call_target="tpu_custom_call" | custom-call | tf_op jit(solution)/shard_map/pallas_call | solution.py:260
  60.8 1.8 %collective-permute-start.26 = (bf16[128,128]{1,0:T(8,128)(2,1)S(1)}, bf16[128,128]{1,0:T(8,128)(2,1)S(1)}, u32[]{:S(2)}, u32[]{:S(2)}) collective-permute-start(bf16[128,128]{1,0:T(8,128)(2,1)S(1)} %slice_select_fusion), channel_id=1, source_target_pairs={{0,6},{1,7},{2,4},{3,5},{4,2},{5,3},{6,0},{7,1},{8,14},{9,15},{10,... | collective-permute-start | bytes 98312 | tf_op jit(solution)/shard_map/ppermute | solution.py:198
  63.7 3.4 %collective-permute-done.26 = bf16[128,128]{1,0:T(8,128)(2,1)S(1)} collective-permute-done((bf16[128,128]{1,0:T(8,128)(2,1)S(1)}, bf16[128,128]{1,0:T(8,128)(2,1)S(1)}, u32[]{:S(2)}, u32[]{:S(2)}) %collective-permute-start.26) | collective-permute-done | bytes 32800 | tf_op jit(solution)/shard_map/ppermute | solution.py:198
  69.2 2.5 %collective-permute-start.21 = (bf16[32,3072]{1,0:T(8,128)(2,1)S(1)}, bf16[32,3072]{1,0:T(8,128)(2,1)S(1)}, u32[]{:S(2)}, u32[]{:S(2)}) collective-permute-start(bf16[32,3072]{1,0:T(8,128)(2,1)S(1)} %get-tuple-element.44), channel_id=1, source_target_pairs={{0,24},{1,25},{2,26},{3,27},{4,28},{5,29},{6,30},{7,31},{8,16},{9,... | collective-permute-start | bytes 589832 | tf_op jit(solution)/shard_map/ppermute | solution.py:198
  73.9 2.1 %collective-permute-done.19.first = bf16[32,3072]{1,0:T(8,128)(2,1)S(1)} collective-permute-done((bf16[32,3072]{1,0:T(8,128)(2,1)S(1)}, bf16[32,3072]{1,0:T(8,128)(2,1)S(1)}, u32[]{:S(2)}, u32[]{:S(2)}) %collective-permute-start.19) | collective-permute-done | bytes 196640 | tf_op jit(solution)/shard_map/ppermute | solution.py:198
  76.4 3.6 %collective-permute-done.20.second = bf16[32,3072]{1,0:T(8,128)(2,1)S(1)} collective-permute-done((bf16[32,3072]{1,0:T(8,128)(2,1)S(1)}, bf16[32,3072]{1,0:T(8,128)(2,1)S(1)}, u32[]{:S(2)}, u32[]{:S(2)}) %collective-permute-start.20) | collective-permute-done | bytes 196640 | tf_op jit(solution)/shard_map/ppermute | solution.py:198
  81.3 2.0 %collective-permute-start.23 = (bf16[32,1024]{1,0:T(8,128)(2,1)S(1)}, bf16[32,1024]{1,0:T(8,128)(2,1)S(1)}, u32[]{:S(2)}, u32[]{:S(2)}) collective-permute-start(bf16[32,1024]{1,0:T(8,128)(2,1)S(1)} %get-tuple-element.52), channel_id=1, source_target_pairs={{0,2},{1,6},{2,3},{3,7},{4,0},{5,4},{6,1},{7,5},{8,10},{9,14},{10,... | collective-permute-start | bytes 196616 | tf_op jit(solution)/shard_map/ppermute | solution.py:198
  83.3 2.2 %collective-permute-start.24 = (bf16[32,1024]{1,0:T(8,128)(2,1)S(1)}, bf16[32,1024]{1,0:T(8,128)(2,1)S(1)}, u32[]{:S(2)}, u32[]{:S(2)}) collective-permute-start(bf16[32,1024]{1,0:T(8,128)(2,1)S(1)} %get-tuple-element.51), channel_id=1, source_target_pairs={{0,3},{1,7},{2,2},{3,6},{4,1},{5,5},{6,0},{7,4},{8,11},{9,15},{10,... | collective-permute-start | bytes 196616 | tf_op jit(solution)/shard_map/ppermute | solution.py:198
  87.5 3.8 %collective-permute-done.24 = bf16[32,1024]{1,0:T(8,128)(2,1)S(1)} collective-permute-done((bf16[32,1024]{1,0:T(8,128)(2,1)S(1)}, bf16[32,1024]{1,0:T(8,128)(2,1)S(1)}, u32[]{:S(2)}, u32[]{:S(2)}) %collective-permute-start.24) | collective-permute-done | bytes 65568 | tf_op jit(solution)/shard_map/ppermute | solution.py:198
  (89 shorter events, 27.6 us)
Async XLA Ops:
  0.6 9.6 %collective-permute-start = (bf16[16,2048]{1,0:T(8,128)(2,1)}, bf16[16,2048]{1,0:T(8,128)(2,1)S(1)}, u32[]{:S(2)}, u32[]{:S(2)}) collective-permute-start(bf16[16,2048]{1,0:T(8,128)(2,1)} %refs_0_.1), channel_id=1, source_target_pairs={{0,2},{1,3},{2,0},{3,1},{4,6},{5,7},{6,4},{7,5},{8,10},{9,11},{10,... | collective-permute-start | bytes 196616 | tf_op jit(solution)/shard_map/ppermute | solution.py:198
  3.7 7.5 %collective-permute-start.1 = (bf16[16,2048]{1,0:T(8,128)(2,1)}, bf16[16,2048]{1,0:T(8,128)(2,1)S(1)}, u32[]{:S(2)}, u32[]{:S(2)}) collective-permute-start(bf16[16,2048]{1,0:T(8,128)(2,1)} %refs_0_.1), channel_id=1, source_target_pairs={{0,4},{1,5},{2,6},{3,7},{4,0},{5,1},{6,2},{7,3},{8,12},{9,13},{10,... | collective-permute-start | bytes 196616 | tf_op jit(solution)/shard_map/ppermute | solution.py:198
  6.3 6.3 %collective-permute-start.2 = (bf16[16,2048]{1,0:T(8,128)(2,1)}, bf16[16,2048]{1,0:T(8,128)(2,1)S(1)}, u32[]{:S(2)}, u32[]{:S(2)}) collective-permute-start(bf16[16,2048]{1,0:T(8,128)(2,1)} %refs_0_.1), channel_id=1, source_target_pairs={{0,6},{1,7},{2,4},{3,5},{4,2},{5,3},{6,0},{7,1},{8,14},{9,15},{10,... | collective-permute-start | bytes 196616 | tf_op jit(solution)/shard_map/ppermute | solution.py:198
  7.6 12.4 %collective-permute-start.4 = (bf16[2048,128]{1,0:T(8,128)(2,1)S(1)}, bf16[2048,128]{1,0:T(8,128)(2,1)S(1)}, u32[]{:S(2)}, u32[]{:S(2)}) collective-permute-start(bf16[2048,128]{1,0:T(8,128)(2,1)S(1)} %get-tuple-element.43), channel_id=1, source_target_pairs={{0,0},{1,16},{2,2},{3,18},{4,4},{5,20},{6,6},{7,22},{8,8},{9,24},{... | collective-permute-start | bytes 1572872 | tf_op jit(solution)/shard_map/ppermute | solution.py:198
  8.3 13.0 %collective-permute-start.5 = (bf16[2048,128]{1,0:T(8,128)(2,1)S(1)}, bf16[2048,128]{1,0:T(8,128)(2,1)S(1)}, u32[]{:S(2)}, u32[]{:S(2)}) collective-permute-start(bf16[2048,128]{1,0:T(8,128)(2,1)S(1)} %get-tuple-element.42), channel_id=1, source_target_pairs={{0,8},{1,24},{2,10},{3,26},{4,12},{5,28},{6,14},{7,30},{8,0},{9,16... | collective-permute-start | bytes 1572872 | tf_op jit(solution)/shard_map/ppermute | solution.py:198
  15.8 12.3 %collective-permute-start.8 = (bf16[128,1024]{1,0:T(8,128)(2,1)S(1)}, bf16[128,1024]{1,0:T(8,128)(2,1)S(1)}, u32[]{:S(2)}, u32[]{:S(2)}) collective-permute-start(bf16[128,1024]{1,0:T(8,128)(2,1)S(1)} %shard_map.98), channel_id=1, source_target_pairs={{0,0},{1,16},{2,2},{3,18},{12,12},{13,28},{14,14},{15,30},{16,1},{... | collective-permute-start | bytes 786440 | tf_op jit(solution)/shard_map/ppermute | solution.py:198
  16.6 11.5 %collective-permute-start.9 = (bf16[128,1024]{1,0:T(8,128)(2,1)S(1)}, bf16[128,1024]{1,0:T(8,128)(2,1)S(1)}, u32[]{:S(2)}, u32[]{:S(2)}) collective-permute-start(bf16[128,1024]{1,0:T(8,128)(2,1)S(1)} %shard_map.98), channel_id=1, source_target_pairs={{0,8},{1,24},{2,10},{3,26},{12,4},{13,20},{14,6},{15,22},{16,9},{1... | collective-permute-start | bytes 786440 | tf_op jit(solution)/shard_map/ppermute | solution.py:198
  29.0 6.3 %collective-permute-start.10 = (f32[128,384]{1,0:T(8,128)S(1)}, f32[128,384]{1,0:T(8,128)S(1)}, u32[]{:S(2)}, u32[]{:S(2)}) collective-permute-start(f32[128,384]{1,0:T(8,128)S(1)} %pad_maximum_fusion.mine), channel_id=1, source_target_pairs={{0,1},{1,0},{2,3},{3,2},{4,5},{5,4},{6,7},{7,6},{8,9},{9,8},{10,11... | collective-permute-start | bytes 589832 | tf_op jit(solution)/shard_map/ppermute | solution.py:198
  35.3 6.6 %collective-permute-start.12 = (f16[128,128]{1,0:T(8,128)(2,1)S(1)}, f16[128,128]{1,0:T(8,128)(2,1)S(1)}, u32[]{:S(2)}, u32[]{:S(2)}) collective-permute-start(f16[128,128]{1,0:T(8,128)(2,1)S(1)} %slice_select_fusion.1), channel_id=1, source_target_pairs={{0,6},{1,7},{2,4},{3,5},{4,2},{5,3},{6,0},{7,1},{8,14},{9,15},{10,... | collective-permute-start | bytes 98312 | tf_op jit(solution)/shard_map/ppermute | solution.py:198
  40.1 6.6 %collective-permute-start.14 = (bf16[64,4096]{1,0:T(8,128)(2,1)S(1)}, bf16[64,4096]{1,0:T(8,128)(2,1)S(1)}, u32[]{:S(2)}, u32[]{:S(2)}) collective-permute-start(bf16[64,4096]{1,0:T(8,128)(2,1)S(1)} %get-tuple-element.40), channel_id=1, source_target_pairs={{0,1},{1,0},{2,3},{3,2},{4,5},{5,4},{6,7},{7,6},{8,9},{9,8},{10,11... | collective-permute-start | bytes 1572872 | tf_op jit(solution)/shard_map/ppermute | solution.py:198
  48.2 5.2 %collective-permute-start.15 = (bf16[8,4224]{1,0:T(8,128)(2,1)S(1)}, bf16[8,4224]{1,0:T(8,128)(2,1)S(1)}, u32[]{:S(2)}, u32[]{:S(2)}) collective-permute-start(bf16[8,4224]{1,0:T(8,128)(2,1)S(1)} %get-tuple-element.29.first), channel_id=1, source_target_pairs={{0,2},{1,3},{2,0},{3,1},{4,6},{5,7},{6,4},{7,5},{8,10},{9,11},{10,... | collective-permute-start | bytes 202760 | tf_op jit(solution)/shard_map/ppermute | solution.py:198
  48.2 8.7 %collective-permute-start.16 = (bf16[8,4224]{1,0:T(8,128)(2,1)S(1)}, bf16[8,4224]{1,0:T(8,128)(2,1)S(1)}, u32[]{:S(2)}, u32[]{:S(2)}) collective-permute-start(bf16[8,4224]{1,0:T(8,128)(2,1)S(1)} %get-tuple-element.29.first), channel_id=1, source_target_pairs={{0,4},{1,5},{2,6},{3,7},{4,0},{5,1},{6,2},{7,3},{8,12},{9,13},{10,... | collective-permute-start | bytes 202760 | tf_op jit(solution)/shard_map/ppermute | solution.py:198
  49.7 7.2 %collective-permute-start.17 = (bf16[8,4224]{1,0:T(8,128)(2,1)S(1)}, bf16[8,4224]{1,0:T(8,128)(2,1)S(1)}, u32[]{:S(2)}, u32[]{:S(2)}) collective-permute-start(bf16[8,4224]{1,0:T(8,128)(2,1)S(1)} %get-tuple-element.29.first), channel_id=1, source_target_pairs={{0,6},{1,7},{2,4},{3,5},{4,2},{5,3},{6,0},{7,1},{8,14},{9,15},{10,... | collective-permute-start | bytes 202760 | tf_op jit(solution)/shard_map/ppermute | solution.py:198
  60.8 6.2 %collective-permute-start.26 = (bf16[128,128]{1,0:T(8,128)(2,1)S(1)}, bf16[128,128]{1,0:T(8,128)(2,1)S(1)}, u32[]{:S(2)}, u32[]{:S(2)}) collective-permute-start(bf16[128,128]{1,0:T(8,128)(2,1)S(1)} %slice_select_fusion), channel_id=1, source_target_pairs={{0,6},{1,7},{2,4},{3,5},{4,2},{5,3},{6,0},{7,1},{8,14},{9,15},{10,... | collective-permute-start | bytes 98312 | tf_op jit(solution)/shard_map/ppermute | solution.py:198
  62.7 5.3 %collective-permute-start.25 = (bf16[128,256]{1,0:T(8,128)(2,1)S(1)}, bf16[128,256]{1,0:T(8,128)(2,1)S(1)}, u32[]{:S(2)}, u32[]{:S(2)}) collective-permute-start(bf16[128,256]{1,0:T(8,128)(2,1)S(1)} %convert_element_type.51), channel_id=1, source_target_pairs={{0,2},{1,5},{2,0},{3,7},{4,6},{5,1},{6,4},{7,3},{8,10},{9,13},{10,... | collective-permute-start | bytes 196616 | tf_op jit(solution)/shard_map/ppermute | solution.py:198
  68.1 7.8 %collective-permute-start.19 = (bf16[32,3072]{1,0:T(8,128)(2,1)S(1)}, bf16[32,3072]{1,0:T(8,128)(2,1)S(1)}, u32[]{:S(2)}, u32[]{:S(2)}) collective-permute-start(bf16[32,3072]{1,0:T(8,128)(2,1)S(1)} %get-tuple-element.46), channel_id=1, source_target_pairs={{0,8},{1,9},{2,10},{3,11},{4,12},{5,13},{6,14},{7,15},{8,0},{9,1},... | collective-permute-start | bytes 589832 | tf_op jit(solution)/shard_map/ppermute | solution.py:198
  68.7 11.3 %collective-permute-start.20 = (bf16[32,3072]{1,0:T(8,128)(2,1)S(1)}, bf16[32,3072]{1,0:T(8,128)(2,1)S(1)}, u32[]{:S(2)}, u32[]{:S(2)}) collective-permute-start(bf16[32,3072]{1,0:T(8,128)(2,1)S(1)} %get-tuple-element.45), channel_id=1, source_target_pairs={{0,16},{1,17},{2,18},{3,19},{4,20},{5,21},{6,22},{7,23},{8,24},{9,... | collective-permute-start | bytes 589832 | tf_op jit(solution)/shard_map/ppermute | solution.py:198
  69.2 11.4 %collective-permute-start.21 = (bf16[32,3072]{1,0:T(8,128)(2,1)S(1)}, bf16[32,3072]{1,0:T(8,128)(2,1)S(1)}, u32[]{:S(2)}, u32[]{:S(2)}) collective-permute-start(bf16[32,3072]{1,0:T(8,128)(2,1)S(1)} %get-tuple-element.44), channel_id=1, source_target_pairs={{0,24},{1,25},{2,26},{3,27},{4,28},{5,29},{6,30},{7,31},{8,16},{9,... | collective-permute-start | bytes 589832 | tf_op jit(solution)/shard_map/ppermute | solution.py:198
  72.9 10.4 %collective-permute-start.28 = (bf16[32,1024]{1,0:T(8,128)(2,1)S(1)}, bf16[32,1024]{1,0:T(8,128)(2,1)S(1)}, u32[]{:S(2)}, u32[]{:S(2)}) collective-permute-start(bf16[32,1024]{1,0:T(8,128)(2,1)S(1)} %get-tuple-element.49), channel_id=1, source_target_pairs={{0,8},{1,9},{2,10},{3,11},{4,12},{5,13},{6,14},{7,15},{8,0},{9,1},... | collective-permute-start | bytes 196616 | tf_op jit(solution)/shard_map/ppermute | solution.py:198
  73.4 12.1 %collective-permute-start.29 = (bf16[32,1024]{1,0:T(8,128)(2,1)S(1)}, bf16[32,1024]{1,0:T(8,128)(2,1)S(1)}, u32[]{:S(2)}, u32[]{:S(2)}) collective-permute-start(bf16[32,1024]{1,0:T(8,128)(2,1)S(1)} %get-tuple-element.48), channel_id=1, source_target_pairs={{0,16},{1,17},{2,18},{3,19},{4,20},{5,21},{6,22},{7,23},{8,24},{9,... | collective-permute-start | bytes 196616 | tf_op jit(solution)/shard_map/ppermute | solution.py:198
  76.0 9.5 %collective-permute-start.30 = (bf16[32,1024]{1,0:T(8,128)(2,1)S(1)}, bf16[32,1024]{1,0:T(8,128)(2,1)S(1)}, u32[]{:S(2)}, u32[]{:S(2)}) collective-permute-start(bf16[32,1024]{1,0:T(8,128)(2,1)S(1)} %get-tuple-element.47), channel_id=1, source_target_pairs={{0,24},{1,25},{2,26},{3,27},{4,28},{5,29},{6,30},{7,31},{8,16},{9,... | collective-permute-start | bytes 196616 | tf_op jit(solution)/shard_map/ppermute | solution.py:198
  81.2 5.6 %collective-permute-start.22 = (bf16[32,1024]{1,0:T(8,128)(2,1)S(1)}, bf16[32,1024]{1,0:T(8,128)(2,1)S(1)}, u32[]{:S(2)}, u32[]{:S(2)}) collective-permute-start(bf16[32,1024]{1,0:T(8,128)(2,1)S(1)} %get-tuple-element.50), channel_id=1, source_target_pairs={{0,1},{1,5},{2,0},{3,4},{4,3},{5,7},{6,2},{7,6},{8,9},{9,13},{10,8... | collective-permute-start | bytes 196616 | tf_op jit(solution)/shard_map/ppermute | solution.py:198
  81.3 6.2 %collective-permute-start.23 = (bf16[32,1024]{1,0:T(8,128)(2,1)S(1)}, bf16[32,1024]{1,0:T(8,128)(2,1)S(1)}, u32[]{:S(2)}, u32[]{:S(2)}) collective-permute-start(bf16[32,1024]{1,0:T(8,128)(2,1)S(1)} %get-tuple-element.52), channel_id=1, source_target_pairs={{0,2},{1,6},{2,3},{3,7},{4,0},{5,4},{6,1},{7,5},{8,10},{9,14},{10,... | collective-permute-start | bytes 196616 | tf_op jit(solution)/shard_map/ppermute | solution.py:198
  83.3 7.9 %collective-permute-start.24 = (bf16[32,1024]{1,0:T(8,128)(2,1)S(1)}, bf16[32,1024]{1,0:T(8,128)(2,1)S(1)}, u32[]{:S(2)}, u32[]{:S(2)}) collective-permute-start(bf16[32,1024]{1,0:T(8,128)(2,1)S(1)} %get-tuple-element.51), channel_id=1, source_target_pairs={{0,3},{1,7},{2,2},{3,6},{4,1},{5,5},{6,0},{7,4},{8,11},{9,15},{10,... | collective-permute-start | bytes 196616 | tf_op jit(solution)/shard_map/ppermute | solution.py:198
  (16 other events, 96.0 us)
where the time goes:
time: 93.8 us; the launch traced here: 91.9 us
  starting transfers between devices  41.6 us (44%)
  waiting for transfers between devices  34.6 us (37%)
  Pallas kernels  11.4 us (12%)
  local copies, waits for them, and re-layouts  2.34 us (2%)
  other arithmetic  0.99 us (1%)
  between operations  0.98 us (1%)
    ppermute x32, starting transfers between devices, send(): return lax.ppermute(block, ('member', 'shard'), route_pairs(target))  41.6 us
    ppermute x32, waiting for transfers between devices, send(): return lax.ppermute(block, ('member', 'shard'), route_pairs(target))  34.6 us
    pallas_call x10, Pallas kernels, local_call(): pl.pallas_call(kernel, out_shape=[jax.ShapeDtypeStruct(shape, dtype) for...  9.84 us
  transfers between devices with their start and end apart: 32, of which 19 were waited for; matrix products, arithmetic and copies ran while one was open for 2% of the time, Pallas kernels for 7%

commit v1 on v0

--- a/solution.py
+++ b/solution.py
@@ -1,3 +1,4 @@
+import functools
 import math
 
 import jax
@@ -254,22 +255,26 @@
     )
 
 
+def here():
+    return lax.axis_index("member"), lax.axis_index("shard")
+
+
 def local_call(kernel, outputs, *operands):
     vmem = pl.BlockSpec(memory_space=pltpu.VMEM)
-    smem = pl.BlockSpec(memory_space=pltpu.SMEM)
     return pl.pallas_call(
         kernel,
         out_shape=[jax.ShapeDtypeStruct(shape, dtype) for shape, dtype in outputs],
-        in_specs=[smem] + [vmem] * (len(operands) - 1),
+        in_specs=[vmem] * len(operands),
         out_specs=[vmem] * len(outputs),
         compiler_params=pltpu.CompilerParams(vmem_limit_bytes=KERNEL_VMEM),
     )(*operands)
 
 
 def prepare_kernel(
-    place, segment_ids, norm_gain, reward_weight, weight,
-    segments_out, gain_out, weight_out, head_weight, sems,
+    segment_ids, norm_gain, reward_weight, weight, trunk,
+    segments_out, gain_out, weight_out, trunk_out, head_weight, sems,
 ):
+    place = here()
     width = gain_out.shape[1]
     start = pl.multiple_of(place[1] % 2 * width, width)
     copies = [
@@ -277,6 +282,7 @@
         pltpu.make_async_copy(segment_ids, segments_out, sems.at[1]),
         pltpu.make_async_copy(norm_gain.at[:, pl.ds(start, width)], gain_out, sems.at[2]),
         pltpu.make_async_copy(reward_weight.at[:, pl.ds(start, width)], head_weight, sems.at[3]),
+        pltpu.make_async_copy(trunk, trunk_out, sems.at[4]),
     ]
     for copy in copies:
         copy.start()
@@ -285,7 +291,7 @@
     gain_out[...] = gain_out[...] * head_weight[...]
 
 
-def prepare(place, segments, norm_gain, reward_weight, weight):
+def prepare(segments, norm_gain, reward_weight, weight, trunk):
     width = norm_gain.shape[1] // 2
     return pl.pallas_call(
         prepare_kernel,
@@ -293,19 +299,20 @@
             jax.ShapeDtypeStruct(segments.shape, segments.dtype),
             jax.ShapeDtypeStruct((1, width), norm_gain.dtype),
             jax.ShapeDtypeStruct(weight.shape, weight.dtype),
+            jax.ShapeDtypeStruct(trunk.shape, trunk.dtype),
         ],
-        in_specs=[pl.BlockSpec(memory_space=pltpu.SMEM)]
-        + [pl.BlockSpec(memory_space=pl.ANY)] * 4,
-        out_specs=[pl.BlockSpec(memory_space=pltpu.VMEM)] * 3,
+        in_specs=[pl.BlockSpec(memory_space=pl.ANY)] * 5,
+        out_specs=[pl.BlockSpec(memory_space=pltpu.VMEM)] * 4,
         scratch_shapes=[
             pltpu.VMEM((1, width), reward_weight.dtype),
-            pltpu.SemaphoreType.DMA((4,)),
+            pltpu.SemaphoreType.DMA((5,)),
         ],
         compiler_params=pltpu.CompilerParams(vmem_limit_bytes=KERNEL_VMEM),
-    )(place, segments, norm_gain, reward_weight, weight)
-
-
-def stack_kernel(place, *refs):
+    )(segments, norm_gain, reward_weight, weight, trunk)
+
+
+def stack_kernel(*refs):
+    place = here()
     pieces, out, sems = refs[:-2], refs[-2], refs[-1]
     rows = pieces[0].shape[0]
     copies = []
@@ -318,20 +325,20 @@
         copy.wait()
 
 
-def stack_rows(place, blocks):
+def stack_rows(blocks):
     rows, width = blocks[0].shape
     return pl.pallas_call(
         stack_kernel,
         out_shape=jax.ShapeDtypeStruct((len(blocks) * rows, width), blocks[0].dtype),
-        in_specs=[pl.BlockSpec(memory_space=pltpu.SMEM)]
-        + [pl.BlockSpec(memory_space=pl.ANY)] * len(blocks),
+        in_specs=[pl.BlockSpec(memory_space=pl.ANY)] * len(blocks),
         out_specs=pl.BlockSpec(memory_space=pltpu.VMEM),
         scratch_shapes=[pltpu.SemaphoreType.DMA((len(blocks),))],
         compiler_params=pltpu.CompilerParams(vmem_limit_bytes=KERNEL_VMEM),
-    )(place, *blocks)
-
-
-def kv_columns_kernel(place, own, other, out):
+    )(*blocks)
+
+
+def kv_columns_kernel(own, other, out):
+    place = here()
     width = out.shape[1]
     rows = own.shape[0] // 4
     core = place[1] % 2
@@ -342,18 +349,19 @@
             out[pl.ds(to, rows), :] = source[step * rows : (step + 1) * rows, pl.ds(start, width)]
 
 
-def query_kernel(place, own, other, first, second, out_first, out_second):
+def query_kernel(own, other, weight, out):
+    place = here()
     rows = own.shape[0] // 4
     core = place[1] % 2
-    for weight, out in ((first, out_first), (second, out_second)):
-        for source, side in ((own, core), (other, 1 - core)):
-            part = matmul(source[...], weight[...])
-            for step in range(4):
-                to = pl.multiple_of((2 * step + side) * rows, rows)
-                out[pl.ds(to, rows), :] = part[step * rows : (step + 1) * rows]
-
-
-def kv_kernel(place, segments, first, second, weight, out, pooled):
+    for source, side in ((own, core), (other, 1 - core)):
+        part = matmul(source[...], weight[...])
+        for step in range(4):
+            to = pl.multiple_of((2 * step + side) * rows, rows)
+            out[pl.ds(to, rows), :] = part[step * rows : (step + 1) * rows]
+
+
+def kv_kernel(segments, first, second, weight, out, pooled):
+    place = here()
     far = (place[1] // 4) ^ (place[0] % 2)
     columns = jnp.where(far == 0, first[...], second[...])
     out[...] = matmul(columns, weight[...])
@@ -361,10 +369,11 @@
 
 
 def forward_kernel(
-    place, segments, mine, swapped, kv_mine, kv_swapped, pooled, out_own, out_other, gain,
+    segments, mine, swapped, kv_mine, kv_swapped, pooled, out_own, out_other, gain,
     queries_out, kv_out, attention_out, capped_out, message,
 ):
     bf16 = jnp.bfloat16
+    place = here()
     core, height = place[1] % 2, place[1] // 2
     queries = (mine[:, :HD] + swapped[:, :HD]).astype(bf16)
     kv_values = (kv_mine[...] + kv_swapped[...]).astype(bf16)
@@ -408,9 +417,9 @@
 
 
 def stats_kernel(
-    place, first, second, third, fourth, out_own, out_other, gain, hidden_out, report
+    first, second, third, fourth, out_own, out_other, gain, hidden_out, report
 ):
-    core = place[1] % 2
+    core = here()[1] % 2
     half_width = hidden_out.shape[1]
     f32 = jnp.float32
     total = (first[...].astype(f32) + second[...].astype(f32)) + (
@@ -439,11 +448,11 @@
 
 
 def backward_kernel(
-    place, pairs, segments, mine, swapped, queries, kv_values, attention, capped,
-    query_grad, kv_grad, rewards_out, factors,
+    pairs, segments, mine, swapped, queries, kv_values, attention, capped,
+    query_grad, kv_grad, rewards_out, factors, *, full_width,
 ):
-    bf16, f32 = jnp.bfloat16, jnp.float32
-    width = place[2].astype(f32)
+    bf16 = jnp.bfloat16
+    width = full_width
     report = mine[...] + swapped[...]
     hidden_along, gain_along = report[:SEQS], report[SEQS : 2 * SEQS]
     square_sum, product_sum = report[2 * SEQS :, 0:1], report[2 * SEQS :, 1:2]
@@ -473,13 +482,14 @@
     score_grad = attn * (prob_grad - jnp.sum(attn * prob_grad, axis=1, keepdims=True))
     ratio = capped[...] / softcap_limit
     raw_grad = (score_grad * (1.0 - ratio * ratio) * (1.0 / math.sqrt(HD))).astype(bf16)
-    order = member_order(place, attn.shape[0])
+    order = member_order(here(), attn.shape[0])
     query_grad[...] = matmul(order, matmul(raw_grad, keys).astype(bf16)).astype(bf16)
     kv_grad[:, :HD] = matmul_tn(raw_grad, queries[...])
     kv_grad[:, HD:] = matmul_tn(attn.astype(bf16), out_grad)
 
 
-def far_kernel(place, grad, weight, far):
+def far_kernel(grad, weight, far):
+    place = here()
     width = far.shape[1] // 3
     for step in (1, 2, 3):
         start = pl.multiple_of(((place[1] // 2) ^ step) * width, width)
@@ -489,9 +499,10 @@
 
 
 def near_kernel(
-    place, segments, grad, weight, kv_mine, kv_swapped, kv_weight, hidden, gain, factors, near
+    segments, grad, weight, kv_mine, kv_swapped, kv_weight, hidden, gain, factors, near
 ):
     bf16 = jnp.bfloat16
+    place = here()
     width = near.shape[1]
     start = pl.multiple_of(place[1] // 2 * width, width)
     order = member_order(place, near.shape[0])
@@ -510,7 +521,7 @@
     ).astype(bf16)
 
 
-def member_sum_kernel(place, own, first, second, third, out):
+def member_sum_kernel(own, first, second, third, out):
     f32 = jnp.float32
     rows = out.shape[0]
     out[...] = (
@@ -534,9 +545,8 @@
     member_rows = tokens // 4
     query_piece = w_query[0, 0]
     kv_piece = w_key_value[0, 0]
-    place = jnp.stack([member, shard, jnp.int32(2 * half_width)])
-
-    stack = [trunk_out] + [send(trunk_out, lambda m, z, k, d=d: (m, z ^ d, k)) for d in (1, 2, 3)]
+
+    stack = [send(trunk_out, lambda m, z, k, d=d: (m, z ^ d, k)) for d in (1, 2, 3)]
 
     cuts = [
         lax.dynamic_slice_in_dim(query_piece, (col ^ r) * local_width, local_width, 0)
@@ -547,13 +557,13 @@
         for r in (0, 1)
     ]
 
-    segments, gain, kv_weight = prepare(
-        place, segment_ids[None, :], norm_gain, reward_weight, kv_piece
-    )
-    column_own = stack_rows(place, stack)
+    segments, gain, kv_weight, trunk_near = prepare(
+        segment_ids[None, :], norm_gain, reward_weight, kv_piece, trunk_out
+    )
+    column_own = stack_rows([trunk_near] + stack)
     column_other = core_swap(column_own)
     block_shape = ((tokens, block_width), bf16)
-    (kv_sent,) = local_call(kv_columns_kernel, [block_shape], place, column_own, column_other)
+    (kv_sent,) = local_call(kv_columns_kernel, [block_shape], column_own, column_other)
     kv_got = [
         send(
             kv_sent,
@@ -562,9 +572,10 @@
         for r in (0, 1)
     ]
     head_shape = ((tokens, HD), f32)
-    query_parts = local_call(
-        query_kernel, [head_shape] * 2, place, column_own, column_other, *weights
-    )
+    query_parts = [
+        local_call(query_kernel, [head_shape], column_own, column_other, weights[r])[0]
+        for r in (0, 1)
+    ]
     query_got = [
         send(part, lambda m, z, k, r=r: (2 * k + ((m % 2) ^ r), z, m // 2))
         for r, part in enumerate(query_parts)
@@ -572,7 +583,6 @@
     kv_part, pooled = local_call(
         kv_kernel,
         [((tokens, 2 * HD), f32), ((SEQS, block_width), f32)],
-        place,
         segments,
         *kv_got,
         kv_weight,
@@ -596,13 +606,13 @@
             ((tokens, tokens), f32),
             ((SEQS, half_width + HD), bf16),
         ],
-        place, segments, mixed, swapped, kv_mine, kv_swapped, pooled, out_own, out_other, gain,
+        segments, mixed, swapped, kv_mine, kv_swapped, pooled, out_own, out_other, gain,
     )
     others = [send(message, lambda m, z, k, d=d: (m, z ^ d, k)) for d in (1, 2, 3)]
     hidden, report = local_call(
         stats_kernel,
         [((SEQS, half_width), f32), ((3 * SEQS, HD), f32)],
-        place, message, *others, out_own, out_other, gain,
+        message, *others, out_own, out_other, gain,
     )
     seq_ids = jnp.arange(SEQS)[None, :]
     pairs = (pair_order[0::2][:, None] == seq_ids).astype(f32) - (
@@ -610,19 +620,19 @@
     ).astype(f32)
     pairs = jnp.concatenate([pairs, jnp.zeros_like(pairs)], axis=0)
     query_grad, kv_grad, rewards, factors = local_call(
-        backward_kernel,
+        functools.partial(backward_kernel, full_width=float(2 * half_width)),
         [
             ((tokens, HD), bf16),
             ((tokens, 2 * HD), f32),
             ((1, SEQS), f32),
             ((2, SEQS, HD), f32),
         ],
-        place, pairs, segments, report, core_swap(report), queries, kv_values, attention, capped,
+        pairs, segments, report, core_swap(report), queries, kv_values, attention, capped,
     )
 
     kv_mine, kv_swapped = height_total(kv_grad, core, bf16)
     (far_grad,) = local_call(
-        far_kernel, [((tokens, 3 * block_width), bf16)], place, query_grad, query_piece
+        far_kernel, [((tokens, 3 * block_width), bf16)], query_grad, query_piece
     )
     far_got = [
         send(far_grad[d * member_rows : (d + 1) * member_rows], lambda m, z, k, d=d: (m ^ d, z, k))
@@ -631,7 +641,7 @@
     (near_grad,) = local_call(
         near_kernel,
         [block_shape],
-        place, segments, query_grad, query_piece, kv_mine, kv_swapped, kv_weight, hidden, gain,
+        segments, query_grad, query_piece, kv_mine, kv_swapped, kv_weight, hidden, gain,
         factors,
     )
     near_got = [
@@ -639,10 +649,10 @@
         for d in (1, 2, 3)
     ]
     (far_sum,) = local_call(
-        member_sum_kernel, [((member_rows, 3 * block_width), bf16)], place, far_grad, *far_got
+        member_sum_kernel, [((member_rows, 3 * block_width), bf16)], far_grad, *far_got
     )
     (near_sum,) = local_call(
-        member_sum_kernel, [((member_rows, block_width), bf16)], place, near_grad, *near_got
+        member_sum_kernel, [((member_rows, block_width), bf16)], near_grad, *near_got
     )
     pieces = [near_sum] + [far_sum[:, e * block_width : (e + 1) * block_width] for e in range(3)]
     total = 0.0

time: 93.8 us -> 85.9 us (0.916); the launches traced: 91.9 us -> 85.6 us
  Pallas kernels: 11.4 us -> 5.3 us
  starting transfers between devices: 41.6 us -> 38.5 us
  waiting for transfers between devices: 34.6 us -> 37.5 us
    pallas_call x10 -> x11, Pallas kernels: 9.84 us -> 4.73 us  [local_call(): pl.pallas_call(kernel, out_shape=[jax.ShapeDtypeStruct(shape, dtype) for...]
    ppermute x32, starting transfers between devices: 41.6 us -> 38.5 us  [send(): return lax.ppermute(block, ('member', 'shard'), route_pairs(target))]
    ppermute x32, waiting for transfers between devices: 34.6 us -> 37.5 us  [send(): return lax.ppermute(block, ('member', 'shard'), route_pairs(target))]
  transfers between devices with their start and end apart: 32 -> 32, of which waited for: 19 -> 17; matrix products, arithmetic and copies ran while one was open for 2% -> 2% of each run, Pallas kernels for 7% -> 3%
where the time goes in v1:
time: 85.9 us; the launch traced here: 85.6 us
  starting transfers between devices  38.5 us (45%)
  waiting for transfers between devices  37.5 us (44%)
  Pallas kernels  5.3 us (6%)
  local copies, waits for them, and re-layouts  2.34 us (3%)
  between operations  0.99 us (1%)
  other arithmetic  0.91 us (1%)
    ppermute x32, starting transfers between devices, send(): return lax.ppermute(block, ('member', 'shard'), route_pairs(target))  38.5 us
    ppermute x32, waiting for transfers between devices, send(): return lax.ppermute(block, ('member', 'shard'), route_pairs(target))  37.5 us
    pallas_call x11, Pallas kernels, local_call(): pl.pallas_call(kernel, out_shape=[jax.ShapeDtypeStruct(shape, dtype) for...  4.73 us
  transfers between devices with their start and end apart: 32, of which 17 were waited for; matrix products, arithmetic and copies ran while one was open for 2% of the time, Pallas kernels for 3%

profile of v1, /device:TPU:0, one launch (start us, length us, event | category | flops | bytes accessed | tf_op | source)
XLA Modules:
  0.0 85.6 jit_solution(11498604923618818974)
XLA Ops:
  0.6 3.1 %collective-permute-start = (bf16[16,2048]{1,0:T(8,128)(2,1)}, bf16[16,2048]{1,0:T(8,128)(2,1)S(1)}, u32[]{:S(2)}, u32[]{:S(2)}) collective-permute-start(bf16[16,2048]{1,0:T(8,128)(2,1)} %trunk.1), channel_id=1, source_target_pairs={{0,2},{1,3},{2,0},{3,1},{4,6},{5,7},{6,4},{7,5},{8,10},{9,11},{10,... | collective-permute-start | bytes 196616 | tf_op jit(solution)/shard_map/ppermute | solution.py:199
  3.7 2.6 %collective-permute-start.1 = (bf16[16,2048]{1,0:T(8,128)(2,1)}, bf16[16,2048]{1,0:T(8,128)(2,1)S(1)}, u32[]{:S(2)}, u32[]{:S(2)}) collective-permute-start(bf16[16,2048]{1,0:T(8,128)(2,1)} %trunk.1), channel_id=1, source_target_pairs={{0,4},{1,5},{2,6},{3,7},{4,0},{5,1},{6,2},{7,3},{8,12},{9,13},{10,... | collective-permute-start | bytes 196616 | tf_op jit(solution)/shard_map/ppermute | solution.py:199
  7.7 1.6 %collective-permute-start.6 = (bf16[2048,128]{1,0:T(8,128)(2,1)S(1)}, bf16[2048,128]{1,0:T(8,128)(2,1)S(1)}, u32[]{:S(2)}, u32[]{:S(2)}) collective-permute-start(bf16[2048,128]{1,0:T(8,128)(2,1)S(1)} %get-tuple-element.40), channel_id=1, source_target_pairs={{0,8},{1,24},{2,10},{3,26},{4,12},{5,28},{6,14},{7,30},{8,0},{9,16... | collective-permute-start | bytes 1572872 | tf_op jit(solution)/shard_map/ppermute | solution.py:199
  11.1 4.8 %collective-permute-done.2.refs_3_ = bf16[16,2048]{1,0:T(8,128)(2,1)S(1)} collective-permute-done((bf16[16,2048]{1,0:T(8,128)(2,1)S(1)}, bf16[16,2048]{1,0:T(8,128)(2,1)S(1)}, u32[]{:S(2)}, u32[]{:S(2)}) %collective-permute-start.2) | collective-permute-done | bytes 65568 | tf_op jit(solution)/shard_map/ppermute | solution.py:199
  16.4 1.4 %collective-permute-done.3.other = bf16[64,2048]{1,0:T(8,128)(2,1)S(1)} collective-permute-done((bf16[64,2048]{1,0:T(8,128)(2,1)S(1)}, bf16[64,2048]{1,0:T(8,128)(2,1)S(1)}, u32[]{:S(2)}, u32[]{:S(2)}) %collective-permute-start.3) | collective-permute-done | bytes 262176 | tf_op jit(solution)/shard_map/ppermute | solution.py:199
  18.6 2.5 %collective-permute-start.9 = (bf16[128,1024]{1,0:T(8,128)(2,1)S(1)}, bf16[128,1024]{1,0:T(8,128)(2,1)S(1)}, u32[]{:S(2)}, u32[]{:S(2)}) collective-permute-start(bf16[128,1024]{1,0:T(8,128)(2,1)S(1)} %shard_map.99), channel_id=1, source_target_pairs={{0,8},{1,24},{2,10},{3,26},{12,4},{13,20},{14,6},{15,22},{16,9},{1... | collective-permute-start | bytes 786440 | tf_op jit(solution)/shard_map/ppermute | solution.py:199
  22.5 1.6 %collective-permute-start.7 = (f32[128,128]{1,0:T(8,128)S(1)}, f32[128,128]{1,0:T(8,128)S(1)}, u32[]{:S(2)}, u32[]{:S(2)}) collective-permute-start(f32[128,128]{1,0:T(8,128)S(1)} %shard_map.98), channel_id=1, source_target_pairs={{0,8},{1,24},{2,10},{3,26},{4,12},{5,28},{6,14},{7,30},{8,0},{9,16... | collective-permute-start | bytes 196616 | tf_op jit(solution)/shard_map/ppermute | solution.py:199
  25.2 3.5 %collective-permute-done.7 = f32[128,128]{1,0:T(8,128)S(1)} collective-permute-done((f32[128,128]{1,0:T(8,128)S(1)}, f32[128,128]{1,0:T(8,128)S(1)}, u32[]{:S(2)}, u32[]{:S(2)}) %collective-permute-start.7) | collective-permute-done | bytes 65568 | tf_op jit(solution)/shard_map/ppermute | solution.py:199
  29.0 3.0 %collective-permute-start.10 = (f32[128,384]{1,0:T(8,128)S(1)}, f32[128,384]{1,0:T(8,128)S(1)}, u32[]{:S(2)}, u32[]{:S(2)}) collective-permute-start(f32[128,384]{1,0:T(8,128)S(1)} %pad_maximum_fusion.mine), channel_id=1, source_target_pairs={{0,1},{1,0},{2,3},{3,2},{4,5},{5,4},{6,7},{7,6},{8,9},{9,8},{10,11... | collective-permute-start | bytes 589832 | tf_op jit(solution)/shard_map/ppermute | solution.py:199
  33.1 2.6 %collective-permute-start.12 = (f16[128,128]{1,0:T(8,128)(2,1)S(1)}, f16[128,128]{1,0:T(8,128)(2,1)S(1)}, u32[]{:S(2)}, u32[]{:S(2)}) collective-permute-start(f16[128,128]{1,0:T(8,128)(2,1)S(1)} %slice_select_fusion.1), channel_id=1, source_target_pairs={{0,6},{1,7},{2,4},{3,5},{4,2},{5,3},{6,0},{7,1},{8,14},{9,15},{10,... | collective-permute-start | bytes 98312 | tf_op jit(solution)/shard_map/ppermute | solution.py:199
  35.9 3.1 %collective-permute-done.12 = f16[128,128]{1,0:T(8,128)(2,1)S(1)} collective-permute-done((f16[128,128]{1,0:T(8,128)(2,1)S(1)}, f16[128,128]{1,0:T(8,128)(2,1)S(1)}, u32[]{:S(2)}, u32[]{:S(2)}) %collective-permute-start.12) | collective-permute-done | bytes 32800 | tf_op jit(solution)/shard_map/ppermute | solution.py:199
  39.0 1.9 %collective-permute-done.11 = f16[128,256]{1,0:T(8,128)(2,1)S(1)} collective-permute-done((f16[128,256]{1,0:T(8,128)(2,1)S(1)}, f16[128,256]{1,0:T(8,128)(2,1)S(1)}, u32[]{:S(2)}, u32[]{:S(2)}) %collective-permute-start.11) | collective-permute-done | bytes 65568 | tf_op jit(solution)/shard_map/ppermute | solution.py:199
  43.4 1.8 %collective-permute-start.16 = (bf16[8,4224]{1,0:T(8,128)(2,1)S(1)}, bf16[8,4224]{1,0:T(8,128)(2,1)S(1)}, u32[]{:S(2)}, u32[]{:S(2)}) collective-permute-start(bf16[8,4224]{1,0:T(8,128)(2,1)S(1)} %get-tuple-element.27.first), channel_id=1, source_target_pairs={{0,4},{1,5},{2,6},{3,7},{4,0},{5,1},{6,2},{7,3},{8,12},{9,13},{10,... | collective-permute-start | bytes 202760 | tf_op jit(solution)/shard_map/ppermute | solution.py:199
  45.2 2.5 %collective-permute-start.17 = (bf16[8,4224]{1,0:T(8,128)(2,1)S(1)}, bf16[8,4224]{1,0:T(8,128)(2,1)S(1)}, u32[]{:S(2)}, u32[]{:S(2)}) collective-permute-start(bf16[8,4224]{1,0:T(8,128)(2,1)S(1)} %get-tuple-element.27.first), channel_id=1, source_target_pairs={{0,6},{1,7},{2,4},{3,5},{4,2},{5,3},{6,0},{7,1},{8,14},{9,15},{10,... | collective-permute-start | bytes 202760 | tf_op jit(solution)/shard_map/ppermute | solution.py:199
  48.5 3.6 %collective-permute-done.16.third = bf16[8,4224]{1,0:T(8,128)(2,1)S(1)} collective-permute-done((bf16[8,4224]{1,0:T(8,128)(2,1)S(1)}, bf16[8,4224]{1,0:T(8,128)(2,1)S(1)}, u32[]{:S(2)}, u32[]{:S(2)}) %collective-permute-start.16) | collective-permute-done | bytes 67616 | tf_op jit(solution)/shard_map/ppermute | solution.py:199
  55.1 1.8 %collective-permute-start.26 = (bf16[128,128]{1,0:T(8,128)(2,1)S(1)}, bf16[128,128]{1,0:T(8,128)(2,1)S(1)}, u32[]{:S(2)}, u32[]{:S(2)}) collective-permute-start(bf16[128,128]{1,0:T(8,128)(2,1)S(1)} %slice_select_fusion), channel_id=1, source_target_pairs={{0,6},{1,7},{2,4},{3,5},{4,2},{5,3},{6,0},{7,1},{8,14},{9,15},{10,... | collective-permute-start | bytes 98312 | tf_op jit(solution)/shard_map/ppermute | solution.py:199
  57.5 3.8 %collective-permute-done.26 = bf16[128,128]{1,0:T(8,128)(2,1)S(1)} collective-permute-done((bf16[128,128]{1,0:T(8,128)(2,1)S(1)}, bf16[128,128]{1,0:T(8,128)(2,1)S(1)}, u32[]{:S(2)}, u32[]{:S(2)}) %collective-permute-start.26) | collective-permute-done | bytes 32800 | tf_op jit(solution)/shard_map/ppermute | solution.py:199
  62.5 2.2 %collective-permute-start.20 = (bf16[32,3072]{1,0:T(8,128)(2,1)S(1)}, bf16[32,3072]{1,0:T(8,128)(2,1)S(1)}, u32[]{:S(2)}, u32[]{:S(2)}) collective-permute-start(bf16[32,3072]{1,0:T(8,128)(2,1)S(1)} %get-tuple-element.43), channel_id=1, source_target_pairs={{0,16},{1,17},{2,18},{3,19},{4,20},{5,21},{6,22},{7,23},{8,24},{9,... | collective-permute-start | bytes 589832 | tf_op jit(solution)/shard_map/ppermute | solution.py:199
  66.8 2.0 %collective-permute-start.29 = (bf16[32,1024]{1,0:T(8,128)(2,1)S(1)}, bf16[32,1024]{1,0:T(8,128)(2,1)S(1)}, u32[]{:S(2)}, u32[]{:S(2)}) collective-permute-start(bf16[32,1024]{1,0:T(8,128)(2,1)S(1)} %get-tuple-element.46), channel_id=1, source_target_pairs={{0,16},{1,17},{2,18},{3,19},{4,20},{5,21},{6,22},{7,23},{8,24},{9,... | collective-permute-start | bytes 196616 | tf_op jit(solution)/shard_map/ppermute | solution.py:199
  70.2 1.6 %collective-permute-start.30 = (bf16[32,1024]{1,0:T(8,128)(2,1)S(1)}, bf16[32,1024]{1,0:T(8,128)(2,1)S(1)}, u32[]{:S(2)}, u32[]{:S(2)}) collective-permute-start(bf16[32,1024]{1,0:T(8,128)(2,1)S(1)} %get-tuple-element.45), channel_id=1, source_target_pairs={{0,24},{1,25},{2,26},{3,27},{4,28},{5,29},{6,30},{7,31},{8,16},{9,... | collective-permute-start | bytes 196616 | tf_op jit(solution)/shard_map/ppermute | solution.py:199
  71.9 2.8 %collective-permute-done.20.second = bf16[32,3072]{1,0:T(8,128)(2,1)S(1)} collective-permute-done((bf16[32,3072]{1,0:T(8,128)(2,1)S(1)}, bf16[32,3072]{1,0:T(8,128)(2,1)S(1)}, u32[]{:S(2)}, u32[]{:S(2)}) %collective-permute-start.20) | collective-permute-done | bytes 196640 | tf_op jit(solution)/shard_map/ppermute | solution.py:199
  74.8 2.0 %collective-permute-start.23 = (bf16[32,1024]{1,0:T(8,128)(2,1)S(1)}, bf16[32,1024]{1,0:T(8,128)(2,1)S(1)}, u32[]{:S(2)}, u32[]{:S(2)}) collective-permute-start(bf16[32,1024]{1,0:T(8,128)(2,1)S(1)} %get-tuple-element.50), channel_id=1, source_target_pairs={{0,2},{1,6},{2,3},{3,7},{4,0},{5,4},{6,1},{7,5},{8,10},{9,14},{10,... | collective-permute-start | bytes 196616 | tf_op jit(solution)/shard_map/ppermute | solution.py:199
  76.9 2.2 %collective-permute-start.24 = (bf16[32,1024]{1,0:T(8,128)(2,1)S(1)}, bf16[32,1024]{1,0:T(8,128)(2,1)S(1)}, u32[]{:S(2)}, u32[]{:S(2)}) collective-permute-start(bf16[32,1024]{1,0:T(8,128)(2,1)S(1)} %get-tuple-element.49), channel_id=1, source_target_pairs={{0,3},{1,7},{2,2},{3,6},{4,1},{5,5},{6,0},{7,4},{8,11},{9,15},{10,... | collective-permute-start | bytes 196616 | tf_op jit(solution)/shard_map/ppermute | solution.py:199
  81.0 3.8 %collective-permute-done.24 = bf16[32,1024]{1,0:T(8,128)(2,1)S(1)} collective-permute-done((bf16[32,1024]{1,0:T(8,128)(2,1)S(1)}, bf16[32,1024]{1,0:T(8,128)(2,1)S(1)}, u32[]{:S(2)}, u32[]{:S(2)}) %collective-permute-start.24) | collective-permute-done | bytes 65568 | tf_op jit(solution)/shard_map/ppermute | solution.py:199
  (89 shorter events, 22.9 us)
Async XLA Ops:
  0.6 10.4 %collective-permute-start = (bf16[16,2048]{1,0:T(8,128)(2,1)}, bf16[16,2048]{1,0:T(8,128)(2,1)S(1)}, u32[]{:S(2)}, u32[]{:S(2)}) collective-permute-start(bf16[16,2048]{1,0:T(8,128)(2,1)} %trunk.1), channel_id=1, source_target_pairs={{0,2},{1,3},{2,0},{3,1},{4,6},{5,7},{6,4},{7,5},{8,10},{9,11},{10,... | collective-permute-start | bytes 196616 | tf_op jit(solution)/shard_map/ppermute | solution.py:199
  3.7 7.3 %collective-permute-start.1 = (bf16[16,2048]{1,0:T(8,128)(2,1)}, bf16[16,2048]{1,0:T(8,128)(2,1)S(1)}, u32[]{:S(2)}, u32[]{:S(2)}) collective-permute-start(bf16[16,2048]{1,0:T(8,128)(2,1)} %trunk.1), channel_id=1, source_target_pairs={{0,4},{1,5},{2,6},{3,7},{4,0},{5,1},{6,2},{7,3},{8,12},{9,13},{10,... | collective-permute-start | bytes 196616 | tf_op jit(solution)/shard_map/ppermute | solution.py:199
  7.7 14.5 %collective-permute-start.6 = (bf16[2048,128]{1,0:T(8,128)(2,1)S(1)}, bf16[2048,128]{1,0:T(8,128)(2,1)S(1)}, u32[]{:S(2)}, u32[]{:S(2)}) collective-permute-start(bf16[2048,128]{1,0:T(8,128)(2,1)S(1)} %get-tuple-element.40), channel_id=1, source_target_pairs={{0,8},{1,24},{2,10},{3,26},{4,12},{5,28},{6,14},{7,30},{8,0},{9,16... | collective-permute-start | bytes 1572872 | tf_op jit(solution)/shard_map/ppermute | solution.py:199
  9.2 6.7 %collective-permute-start.2 = (bf16[16,2048]{1,0:T(8,128)(2,1)S(1)}, bf16[16,2048]{1,0:T(8,128)(2,1)S(1)}, u32[]{:S(2)}, u32[]{:S(2)}) collective-permute-start(bf16[16,2048]{1,0:T(8,128)(2,1)S(1)} %copy-done.2), channel_id=1, source_target_pairs={{0,6},{1,7},{2,4},{3,5},{4,2},{5,3},{6,0},{7,1},{8,14},{9,15},{10,... | collective-permute-start | bytes 196616 | tf_op jit(solution)/shard_map/ppermute | solution.py:199
  9.5 14.6 %collective-permute-start.4 = (bf16[2048,128]{1,0:T(8,128)(2,1)S(1)}, bf16[2048,128]{1,0:T(8,128)(2,1)S(1)}, u32[]{:S(2)}, u32[]{:S(2)}) collective-permute-start(bf16[2048,128]{1,0:T(8,128)(2,1)S(1)} %get-tuple-element.41), channel_id=1, source_target_pairs={{0,0},{1,16},{2,2},{3,18},{4,4},{5,20},{6,6},{7,22},{8,8},{9,24},{... | collective-permute-start | bytes 1572872 | tf_op jit(solution)/shard_map/ppermute | solution.py:199
  17.9 10.8 %collective-permute-start.8 = (bf16[128,1024]{1,0:T(8,128)(2,1)S(1)}, bf16[128,1024]{1,0:T(8,128)(2,1)S(1)}, u32[]{:S(2)}, u32[]{:S(2)}) collective-permute-start(bf16[128,1024]{1,0:T(8,128)(2,1)S(1)} %shard_map.99), channel_id=1, source_target_pairs={{0,0},{1,16},{2,2},{3,18},{12,12},{13,28},{14,14},{15,30},{16,1},{... | collective-permute-start | bytes 786440 | tf_op jit(solution)/shard_map/ppermute | solution.py:199
  18.6 10.1 %collective-permute-start.9 = (bf16[128,1024]{1,0:T(8,128)(2,1)S(1)}, bf16[128,1024]{1,0:T(8,128)(2,1)S(1)}, u32[]{:S(2)}, u32[]{:S(2)}) collective-permute-start(bf16[128,1024]{1,0:T(8,128)(2,1)S(1)} %shard_map.99), channel_id=1, source_target_pairs={{0,8},{1,24},{2,10},{3,26},{12,4},{13,20},{14,6},{15,22},{16,9},{1... | collective-permute-start | bytes 786440 | tf_op jit(solution)/shard_map/ppermute | solution.py:199
  22.5 6.2 %collective-permute-start.7 = (f32[128,128]{1,0:T(8,128)S(1)}, f32[128,128]{1,0:T(8,128)S(1)}, u32[]{:S(2)}, u32[]{:S(2)}) collective-permute-start(f32[128,128]{1,0:T(8,128)S(1)} %shard_map.98), channel_id=1, source_target_pairs={{0,8},{1,24},{2,10},{3,26},{4,12},{5,28},{6,14},{7,30},{8,0},{9,16... | collective-permute-start | bytes 196616 | tf_op jit(solution)/shard_map/ppermute | solution.py:199
  33.1 5.9 %collective-permute-start.12 = (f16[128,128]{1,0:T(8,128)(2,1)S(1)}, f16[128,128]{1,0:T(8,128)(2,1)S(1)}, u32[]{:S(2)}, u32[]{:S(2)}) collective-permute-start(f16[128,128]{1,0:T(8,128)(2,1)S(1)} %slice_select_fusion.1), channel_id=1, source_target_pairs={{0,6},{1,7},{2,4},{3,5},{4,2},{5,3},{6,0},{7,1},{8,14},{9,15},{10,... | collective-permute-start | bytes 98312 | tf_op jit(solution)/shard_map/ppermute | solution.py:199
  35.7 6.6 %collective-permute-start.14 = (bf16[64,4096]{1,0:T(8,128)(2,1)S(1)}, bf16[64,4096]{1,0:T(8,128)(2,1)S(1)}, u32[]{:S(2)}, u32[]{:S(2)}) collective-permute-start(bf16[64,4096]{1,0:T(8,128)(2,1)S(1)} %get-tuple-element.38), channel_id=1, source_target_pairs={{0,1},{1,0},{2,3},{3,2},{4,5},{5,4},{6,7},{7,6},{8,9},{9,8},{10,11... | collective-permute-start | bytes 1572872 | tf_op jit(solution)/shard_map/ppermute | solution.py:199
  43.3 5.2 %collective-permute-start.15 = (bf16[8,4224]{1,0:T(8,128)(2,1)S(1)}, bf16[8,4224]{1,0:T(8,128)(2,1)S(1)}, u32[]{:S(2)}, u32[]{:S(2)}) collective-permute-start(bf16[8,4224]{1,0:T(8,128)(2,1)S(1)} %get-tuple-element.27.first), channel_id=1, source_target_pairs={{0,2},{1,3},{2,0},{3,1},{4,6},{5,7},{6,4},{7,5},{8,10},{9,11},{10,... | collective-permute-start | bytes 202760 | tf_op jit(solution)/shard_map/ppermute | solution.py:199
  43.4 8.7 %collective-permute-start.16 = (bf16[8,4224]{1,0:T(8,128)(2,1)S(1)}, bf16[8,4224]{1,0:T(8,128)(2,1)S(1)}, u32[]{:S(2)}, u32[]{:S(2)}) collective-permute-start(bf16[8,4224]{1,0:T(8,128)(2,1)S(1)} %get-tuple-element.27.first), channel_id=1, source_target_pairs={{0,4},{1,5},{2,6},{3,7},{4,0},{5,1},{6,2},{7,3},{8,12},{9,13},{10,... | collective-permute-start | bytes 202760 | tf_op jit(solution)/shard_map/ppermute | solution.py:199
  45.2 6.9 %collective-permute-start.17 = (bf16[8,4224]{1,0:T(8,128)(2,1)S(1)}, bf16[8,4224]{1,0:T(8,128)(2,1)S(1)}, u32[]{:S(2)}, u32[]{:S(2)}) collective-permute-start(bf16[8,4224]{1,0:T(8,128)(2,1)S(1)} %get-tuple-element.27.first), channel_id=1, source_target_pairs={{0,6},{1,7},{2,4},{3,5},{4,2},{5,3},{6,0},{7,1},{8,14},{9,15},{10,... | collective-permute-start | bytes 202760 | tf_op jit(solution)/shard_map/ppermute | solution.py:199
  55.1 6.2 %collective-permute-start.26 = (bf16[128,128]{1,0:T(8,128)(2,1)S(1)}, bf16[128,128]{1,0:T(8,128)(2,1)S(1)}, u32[]{:S(2)}, u32[]{:S(2)}) collective-permute-start(bf16[128,128]{1,0:T(8,128)(2,1)S(1)} %slice_select_fusion), channel_id=1, source_target_pairs={{0,6},{1,7},{2,4},{3,5},{4,2},{5,3},{6,0},{7,1},{8,14},{9,15},{10,... | collective-permute-start | bytes 98312 | tf_op jit(solution)/shard_map/ppermute | solution.py:199
  56.9 5.3 %collective-permute-start.25 = (bf16[128,256]{1,0:T(8,128)(2,1)S(1)}, bf16[128,256]{1,0:T(8,128)(2,1)S(1)}, u32[]{:S(2)}, u32[]{:S(2)}) collective-permute-start(bf16[128,256]{1,0:T(8,128)(2,1)S(1)} %convert_element_type.51), channel_id=1, source_target_pairs={{0,2},{1,5},{2,0},{3,7},{4,6},{5,1},{6,4},{7,3},{8,10},{9,13},{10,... | collective-permute-start | bytes 196616 | tf_op jit(solution)/shard_map/ppermute | solution.py:199
  62.4 7.8 %collective-permute-start.19 = (bf16[32,3072]{1,0:T(8,128)(2,1)S(1)}, bf16[32,3072]{1,0:T(8,128)(2,1)S(1)}, u32[]{:S(2)}, u32[]{:S(2)}) collective-permute-start(bf16[32,3072]{1,0:T(8,128)(2,1)S(1)} %get-tuple-element.44), channel_id=1, source_target_pairs={{0,8},{1,9},{2,10},{3,11},{4,12},{5,13},{6,14},{7,15},{8,0},{9,1},... | collective-permute-start | bytes 589832 | tf_op jit(solution)/shard_map/ppermute | solution.py:199
  62.5 12.2 %collective-permute-start.20 = (bf16[32,3072]{1,0:T(8,128)(2,1)S(1)}, bf16[32,3072]{1,0:T(8,128)(2,1)S(1)}, u32[]{:S(2)}, u32[]{:S(2)}) collective-permute-start(bf16[32,3072]{1,0:T(8,128)(2,1)S(1)} %get-tuple-element.43), channel_id=1, source_target_pairs={{0,16},{1,17},{2,18},{3,19},{4,20},{5,21},{6,22},{7,23},{8,24},{9,... | collective-permute-start | bytes 589832 | tf_op jit(solution)/shard_map/ppermute | solution.py:199
  64.7 10.0 %collective-permute-start.21 = (bf16[32,3072]{1,0:T(8,128)(2,1)S(1)}, bf16[32,3072]{1,0:T(8,128)(2,1)S(1)}, u32[]{:S(2)}, u32[]{:S(2)}) collective-permute-start(bf16[32,3072]{1,0:T(8,128)(2,1)S(1)} %get-tuple-element.42), channel_id=1, source_target_pairs={{0,24},{1,25},{2,26},{3,27},{4,28},{5,29},{6,30},{7,31},{8,16},{9,... | collective-permute-start | bytes 589832 | tf_op jit(solution)/shard_map/ppermute | solution.py:199
  66.6 10.3 %collective-permute-start.28 = (bf16[32,1024]{1,0:T(8,128)(2,1)S(1)}, bf16[32,1024]{1,0:T(8,128)(2,1)S(1)}, u32[]{:S(2)}, u32[]{:S(2)}) collective-permute-start(bf16[32,1024]{1,0:T(8,128)(2,1)S(1)} %get-tuple-element.47), channel_id=1, source_target_pairs={{0,8},{1,9},{2,10},{3,11},{4,12},{5,13},{6,14},{7,15},{8,0},{9,1},... | collective-permute-start | bytes 196616 | tf_op jit(solution)/shard_map/ppermute | solution.py:199
  66.8 12.2 %collective-permute-start.29 = (bf16[32,1024]{1,0:T(8,128)(2,1)S(1)}, bf16[32,1024]{1,0:T(8,128)(2,1)S(1)}, u32[]{:S(2)}, u32[]{:S(2)}) collective-permute-start(bf16[32,1024]{1,0:T(8,128)(2,1)S(1)} %get-tuple-element.46), channel_id=1, source_target_pairs={{0,16},{1,17},{2,18},{3,19},{4,20},{5,21},{6,22},{7,23},{8,24},{9,... | collective-permute-start | bytes 196616 | tf_op jit(solution)/shard_map/ppermute | solution.py:199
  70.2 8.8 %collective-permute-start.30 = (bf16[32,1024]{1,0:T(8,128)(2,1)S(1)}, bf16[32,1024]{1,0:T(8,128)(2,1)S(1)}, u32[]{:S(2)}, u32[]{:S(2)}) collective-permute-start(bf16[32,1024]{1,0:T(8,128)(2,1)S(1)} %get-tuple-element.45), channel_id=1, source_target_pairs={{0,24},{1,25},{2,26},{3,27},{4,28},{5,29},{6,30},{7,31},{8,16},{9,... | collective-permute-start | bytes 196616 | tf_op jit(solution)/shard_map/ppermute | solution.py:199
  74.8 6.2 %collective-permute-start.23 = (bf16[32,1024]{1,0:T(8,128)(2,1)S(1)}, bf16[32,1024]{1,0:T(8,128)(2,1)S(1)}, u32[]{:S(2)}, u32[]{:S(2)}) collective-permute-start(bf16[32,1024]{1,0:T(8,128)(2,1)S(1)} %get-tuple-element.50), channel_id=1, source_target_pairs={{0,2},{1,6},{2,3},{3,7},{4,0},{5,4},{6,1},{7,5},{8,10},{9,14},{10,... | collective-permute-start | bytes 196616 | tf_op jit(solution)/shard_map/ppermute | solution.py:199
  76.9 8.0 %collective-permute-start.24 = (bf16[32,1024]{1,0:T(8,128)(2,1)S(1)}, bf16[32,1024]{1,0:T(8,128)(2,1)S(1)}, u32[]{:S(2)}, u32[]{:S(2)}) collective-permute-start(bf16[32,1024]{1,0:T(8,128)(2,1)S(1)} %get-tuple-element.49), channel_id=1, source_target_pairs={{0,3},{1,7},{2,2},{3,6},{4,1},{5,5},{6,0},{7,4},{8,11},{9,15},{10,... | collective-permute-start | bytes 196616 | tf_op jit(solution)/shard_map/ppermute | solution.py:199
  79.1 5.8 %collective-permute-start.31 = (bf16[32,1024]{1,0:T(8,128)(2,1)S(1)}, bf16[32,1024]{1,0:T(8,128)(2,1)S(1)}, u32[]{:S(2)}, u32[]{:S(2)}) collective-permute-start(bf16[32,1024]{1,0:T(8,128)(2,1)S(1)} %shard_map.107), channel_id=1, source_target_pairs={{0,0},{1,4},{2,1},{3,5},{4,2},{5,6},{6,3},{7,7},{8,8},{9,12},{10,9... | collective-permute-start | bytes 196616 | tf_op jit(solution)/shard_map/ppermute | solution.py:199
  (16 other events, 71.9 us)

commit v2 on v1

--- a/solution.py
+++ b/solution.py
@@ -219,7 +219,7 @@
     )
 
 
-def height_total(block, core, wire):
+def height_total(block, core, wire, beside=None):
     sent = block.astype(wire)
     near = send(sent, lambda m, z, k: (m, z ^ (1 + k), k))
     half = jnp.where(core == 0, sent[:, :HD], sent[:, HD:])
@@ -229,6 +229,8 @@
         [jnp.where(core == 0, far, zero), jnp.where(core == 0, zero, far)], axis=1
     )
     mine = jnp.where(core == 0, sent.astype(jnp.float32), 0.0) + near.astype(jnp.float32) + spread
+    if beside is not None:
+        mine = jnp.concatenate([mine, beside], axis=1)
     return mine, core_swap(mine)
 
 
@@ -369,14 +371,14 @@
 
 
 def forward_kernel(
-    segments, mine, swapped, kv_mine, kv_swapped, pooled, out_own, out_other, gain,
+    segments, mine, swapped, pooled, out_own, out_other, gain,
     queries_out, kv_out, attention_out, capped_out, message,
 ):
     bf16 = jnp.bfloat16
     place = here()
     core, height = place[1] % 2, place[1] // 2
-    queries = (mine[:, :HD] + swapped[:, :HD]).astype(bf16)
-    kv_values = (kv_mine[...] + kv_swapped[...]).astype(bf16)
+    queries = (mine[:, 2 * HD :] + swapped[:, 2 * HD :]).astype(bf16)
+    kv_values = (mine[:, : 2 * HD] + swapped[:, : 2 * HD]).astype(bf16)
     queries_out[...] = queries
     kv_out[...] = kv_values
     keys, values = kv_values[:, :HD], kv_values[:, HD:]
@@ -521,13 +523,43 @@
     ).astype(bf16)
 
 
-def member_sum_kernel(own, first, second, third, out):
+def sum_of(own, first, second, third, start, width):
     f32 = jnp.float32
-    rows = out.shape[0]
-    out[...] = (
-        (own[:rows, :].astype(f32) + first[...].astype(f32))
-        + (second[...].astype(f32) + third[...].astype(f32))
-    ).astype(out.dtype)
+    rows = first.shape[0]
+    return (
+        (own[:rows, start : start + width].astype(f32) + first[:, start : start + width].astype(f32))
+        + (
+            second[:, start : start + width].astype(f32)
+            + third[:, start : start + width].astype(f32)
+        )
+    ).astype(own.dtype)
+
+
+def place_of(step, width):
+    return pl.multiple_of(((here()[1] // 2) ^ step) % 2 * width, width)
+
+
+def far_sum_kernel(own, first, second, third, one, two):
+    width = one.shape[1]
+    one[...] = sum_of(own, first, second, third, 0, width)
+    for step in (2, 3):
+        two[:, pl.ds(place_of(step, width), width)] = sum_of(
+            own, first, second, third, (step - 1) * width, width
+        )
+
+
+def near_sum_kernel(own, first, second, third, one, two):
+    width = one.shape[1]
+    two[:, pl.ds(place_of(0, width), width)] = sum_of(own, first, second, third, 0, width)
+    two[:, pl.ds(place_of(1, width), width)] = one[...]
+
+
+def merge_kernel(first, second, kept, given):
+    width = kept.shape[1]
+    core = here()[1] % 2
+    for out, side in ((kept, core), (given, 1 - core)):
+        columns = pl.ds(pl.multiple_of(side * width, width), width)
+        out[...] = first[:, columns].astype(jnp.float32) + second[:, columns].astype(jnp.float32)
 
 
 def fast_device(
@@ -587,11 +619,10 @@
         *kv_got,
         kv_weight,
     )
-    mixed = jnp.concatenate([query_got[0] + query_got[1], kv_part], axis=1)
-    swapped = core_swap(mixed)
-    kv_mine, kv_swapped = height_total(mixed[:, HD:] + swapped[:, HD:], core, jnp.float16)
-
-    out_rows, _ = lax.optimization_barrier((w_out[0], mixed))
+    kv_part = kv_part + core_swap(kv_part)
+    mine, swapped = height_total(kv_part, core, jnp.float16, query_got[0] + query_got[1])
+
+    out_rows, _ = lax.optimization_barrier((w_out[0], kv_part))
     out_own = lax.dynamic_slice_in_dim(out_rows, core * half_width, half_width, 1)
     out_other = core_swap(
         lax.dynamic_slice_in_dim(out_rows, (1 - core) * half_width, half_width, 1)
@@ -606,7 +637,7 @@
             ((tokens, tokens), f32),
             ((SEQS, half_width + HD), bf16),
         ],
-        segments, mixed, swapped, kv_mine, kv_swapped, pooled, out_own, out_other, gain,
+        segments, mine, swapped, pooled, out_own, out_other, gain,
     )
     others = [send(message, lambda m, z, k, d=d: (m, z ^ d, k)) for d in (1, 2, 3)]
     hidden, report = local_call(
@@ -648,17 +679,16 @@
         send(near_grad[d * member_rows : (d + 1) * member_rows], lambda m, z, k, d=d: (m ^ d, z, k))
         for d in (1, 2, 3)
     ]
-    (far_sum,) = local_call(
-        member_sum_kernel, [((member_rows, 3 * block_width), bf16)], far_grad, *far_got
-    )
-    (near_sum,) = local_call(
-        member_sum_kernel, [((member_rows, block_width), bf16)], near_grad, *near_got
-    )
-    pieces = [near_sum] + [far_sum[:, e * block_width : (e + 1) * block_width] for e in range(3)]
-    total = 0.0
-    for d in (1, 2, 3, 0):
-        got = send(pieces[d], lambda m, z, k, d=d: (m, (4 * k + (z ^ d)) // 2, z % 2 ^ d % 2))
-        total = total + got.astype(f32)
+    sum_shape = ((member_rows, block_width), bf16)
+    pair_shape = ((member_rows, 2 * block_width), bf16)
+    far_one, far_pair = local_call(far_sum_kernel, [sum_shape, pair_shape], far_grad, *far_got)
+    far_part = send(far_pair, lambda m, z, k: (m, 2 * k + 1 - z // 2, z % 2))
+    (near_pair,) = local_call(near_sum_kernel, [pair_shape], near_grad, *near_got, far_one)
+    near_part = send(near_pair, lambda m, z, k: (m, 2 * k + z // 2, z % 2))
+    kept, given = local_call(
+        merge_kernel, [((member_rows, block_width), f32)] * 2, far_part, near_part
+    )
+    total = kept + core_swap(given)
     return (total, rewards)
 
 

time: 85.9 us -> 95.1 us (1.11)
  waiting for transfers between devices: 37.5 us -> 41.4 us
  starting transfers between devices: 38.5 us -> 41.5 us
  local copies, waits for them, and re-layouts: 2.34 us -> 4.48 us
    ppermute x32 -> x31, waiting for transfers between devices: 37.5 us -> 41.4 us  [send(): return lax.ppermute(block, ('member', 'shard'), route_pairs(target))]
    unnamed x16, local copies, waits for them, and re-layouts: 0.65 us -> 4.06 us
    ppermute x32 -> x31, starting transfers between devices: 38.5 us -> 41.5 us  [send(): return lax.ppermute(block, ('member', 'shard'), route_pairs(target))]
    dynamic_slice x1, local copies, waits for them, and re-layouts: 1.34 us -> 0.08 us  [fast_device(): lax.dynamic_slice_in_dim(query_piece, (col ^ r) * local_width, local_widt...]
    pallas_call x11 -> x12, Pallas kernels: 4.73 us -> 4.75 us  [local_call(): pl.pallas_call(kernel, out_shape=[jax.ShapeDtypeStruct(shape, dtype) for...]
  transfers between devices with their start and end apart: 32 -> 31, of which waited for: 17 -> 18; matrix products, arithmetic and copies ran while one was open for 2% -> 1% of each run, Pallas kernels for 3% -> 2%
where the time goes in v2:
time: 95.1 us; the launch traced here: 94.5 us
  starting transfers between devices  41.5 us (44%)
  waiting for transfers between devices  41.4 us (44%)
  Pallas kernels  5.31 us (6%)
  local copies, waits for them, and re-layouts  4.48 us (5%)
  between operations  0.96 us (1%)
    ppermute x31, starting transfers between devices, send(): return lax.ppermute(block, ('member', 'shard'), route_pairs(target))  41.5 us
    ppermute x31, waiting for transfers between devices, send(): return lax.ppermute(block, ('member', 'shard'), route_pairs(target))  41.4 us
    pallas_call x12, Pallas kernels, local_call(): pl.pallas_call(kernel, out_shape=[jax.ShapeDtypeStruct(shape, dtype) for...  4.75 us
    unnamed x16, local copies, waits for them, and re-layouts  4.06 us
  transfers between devices with their start and end apart: 31, of which 18 were waited for; matrix products, arithmetic and copies ran while one was open for 1% of the time, Pallas kernels for 2%

profile of v2, /device:TPU:0, one launch (start us, length us, event | category | flops | bytes accessed | tf_op | source)
XLA Modules:
  0.0 94.5 jit_solution(6592557853124221516)
XLA Ops:
  0.6 3.1 %collective-permute-start = (bf16[16,2048]{1,0:T(8,128)(2,1)}, bf16[16,2048]{1,0:T(8,128)(2,1)S(1)}, u32[]{:S(2)}, u32[]{:S(2)}) collective-permute-start(bf16[16,2048]{1,0:T(8,128)(2,1)} %trunk.1), channel_id=1, source_target_pairs={{0,2},{1,3},{2,0},{3,1},{4,6},{5,7},{6,4},{7,5},{8,10},{9,11},{10,... | collective-permute-start | bytes 196616 | tf_op jit(solution)/shard_map/ppermute | solution.py:199
  3.8 2.6 %collective-permute-start.1 = (bf16[16,2048]{1,0:T(8,128)(2,1)}, bf16[16,2048]{1,0:T(8,128)(2,1)S(1)}, u32[]{:S(2)}, u32[]{:S(2)}) collective-permute-start(bf16[16,2048]{1,0:T(8,128)(2,1)} %trunk.1), channel_id=1, source_target_pairs={{0,4},{1,5},{2,6},{3,7},{4,0},{5,1},{6,2},{7,3},{8,12},{9,13},{10,... | collective-permute-start | bytes 196616 | tf_op jit(solution)/shard_map/ppermute | solution.py:199
  11.2 1.4 %collective-permute-done.2.refs_3_ = bf16[16,2048]{1,0:T(8,128)(2,1)S(1)} collective-permute-done((bf16[16,2048]{1,0:T(8,128)(2,1)}, bf16[16,2048]{1,0:T(8,128)(2,1)S(1)}, u32[]{:S(2)}, u32[]{:S(2)}) %collective-permute-start.2) | collective-permute-done | bytes 65568 | tf_op jit(solution)/shard_map/ppermute | solution.py:199
  13.9 1.6 %collective-permute-start.11 = (bf16[2048,128]{1,0:T(8,128)(2,1)S(1)}, bf16[2048,128]{1,0:T(8,128)(2,1)S(1)}, u32[]{:S(2)}, u32[]{:S(2)}) collective-permute-start(bf16[2048,128]{1,0:T(8,128)(2,1)S(1)} %get-tuple-element.50), channel_id=1, source_target_pairs={{0,8},{1,24},{2,10},{3,26},{4,12},{5,28},{6,14},{7,30},{8,0},{9,16... | collective-permute-start | bytes 1572872 | tf_op jit(solution)/shard_map/ppermute | solution.py:199
  16.2 2.6 %collective-permute-start.5 = (bf16[128,1024]{1,0:T(8,128)(2,1)S(1)}, bf16[128,1024]{1,0:T(8,128)(2,1)S(1)}, u32[]{:S(2)}, u32[]{:S(2)}) collective-permute-start(bf16[128,1024]{1,0:T(8,128)(2,1)S(1)} %shard_map.97), channel_id=1, source_target_pairs={{0,8},{1,24},{2,10},{3,26},{12,4},{13,20},{14,6},{15,22},{16,9},{1... | collective-permute-start | bytes 786440 | tf_op jit(solution)/shard_map/ppermute | solution.py:199
  18.7 12.4 %collective-permute-done.5.second = bf16[128,1024]{1,0:T(8,128)(2,1)S(1)} collective-permute-done((bf16[128,1024]{1,0:T(8,128)(2,1)S(1)}, bf16[128,1024]{1,0:T(8,128)(2,1)S(1)}, u32[]{:S(2)}, u32[]{:S(2)}) %collective-permute-start.5) | collective-permute-done | bytes 262176 | tf_op jit(solution)/shard_map/ppermute | solution.py:199
  31.5 2.4 %collective-permute-start.6 = (f32[128,256]{1,0:T(8,128)S(1)}, f32[128,256]{1,0:T(8,128)S(1)}, u32[]{:S(2)}, u32[]{:S(2)}) collective-permute-start(f32[128,256]{1,0:T(8,128)S(1)} %get-tuple-element.27), channel_id=1, source_target_pairs={{0,1},{1,0},{2,3},{3,2},{4,5},{5,4},{6,7},{7,6},{8,9},{9,8},{10,11... | collective-permute-start | bytes 393224 | tf_op jit(solution)/shard_map/ppermute | solution.py:199
  35.3 2.7 %collective-permute-start.12 = (f32[128,128]{1,0:T(8,128)S(1)}, f32[128,128]{1,0:T(8,128)S(1)}, u32[]{:S(2)}, u32[]{:S(2)}) collective-permute-start(f32[128,128]{1,0:T(8,128)S(1)} %shard_map.100), channel_id=1, source_target_pairs={{0,8},{1,24},{2,10},{3,26},{4,12},{5,28},{6,14},{7,30},{8,0},{9,16... | collective-permute-start | bytes 196616 | tf_op jit(solution)/shard_map/ppermute | solution.py:199
  38.0 2.2 %collective-permute-done.12 = f32[128,128]{1,0:T(8,128)S(1)} collective-permute-done((f32[128,128]{1,0:T(8,128)S(1)}, f32[128,128]{1,0:T(8,128)S(1)}, u32[]{:S(2)}, u32[]{:S(2)}) %collective-permute-start.12) | collective-permute-done | bytes 65568 | tf_op jit(solution)/shard_map/ppermute | solution.py:199
  40.4 3.6 %collective-permute-start.8 = (f16[128,128]{1,0:T(8,128)(2,1)S(1)}, f16[128,128]{1,0:T(8,128)(2,1)S(1)}, u32[]{:S(2)}, u32[]{:S(2)}) collective-permute-start(f16[128,128]{1,0:T(8,128)(2,1)S(1)} %slice_select_fusion.1), channel_id=1, source_target_pairs={{0,6},{1,7},{2,4},{3,5},{4,2},{5,3},{6,0},{7,1},{8,14},{9,15},{10,... | collective-permute-start | bytes 98312 | tf_op jit(solution)/shard_map/ppermute | solution.py:199
  44.1 1.5 %collective-permute-start.14 = (bf16[64,4096]{1,0:T(8,128)(2,1)S(1)}, bf16[64,4096]{1,0:T(8,128)(2,1)S(1)}, u32[]{:S(2)}, u32[]{:S(2)}) collective-permute-start(bf16[64,4096]{1,0:T(8,128)(2,1)S(1)} %get-tuple-element.48), channel_id=1, source_target_pairs={{0,1},{1,0},{2,3},{3,2},{4,5},{5,4},{6,7},{7,6},{8,9},{9,8},{10,11... | collective-permute-start | bytes 1572872 | tf_op jit(solution)/shard_map/ppermute | solution.py:199
  46.6 3.2 %collective-permute-start.13 = (f32[128,384]{1,0:T(8,128)S(1)}, f32[128,384]{1,0:T(8,128)S(1)}, u32[]{:S(2)}, u32[]{:S(2)}) collective-permute-start(f32[128,384]{1,0:T(8,128)S(1)} %pad_maximum_fusion.mine), channel_id=1, source_target_pairs={{0,1},{1,0},{2,3},{3,2},{4,5},{5,4},{6,7},{7,6},{8,9},{9,8},{10,11... | collective-permute-start | bytes 589832 | tf_op jit(solution)/shard_map/ppermute | solution.py:199
  51.9 1.9 %collective-permute-start.16 = (bf16[8,4224]{1,0:T(8,128)(2,1)S(1)}, bf16[8,4224]{1,0:T(8,128)(2,1)S(1)}, u32[]{:S(2)}, u32[]{:S(2)}) collective-permute-start(bf16[8,4224]{1,0:T(8,128)(2,1)S(1)} %get-tuple-element.31.first), channel_id=1, source_target_pairs={{0,4},{1,5},{2,6},{3,7},{4,0},{5,1},{6,2},{7,3},{8,12},{9,13},{10,... | collective-permute-start | bytes 202760 | tf_op jit(solution)/shard_map/ppermute | solution.py:199
  53.8 2.5 %collective-permute-start.17 = (bf16[8,4224]{1,0:T(8,128)(2,1)S(1)}, bf16[8,4224]{1,0:T(8,128)(2,1)S(1)}, u32[]{:S(2)}, u32[]{:S(2)}) collective-permute-start(bf16[8,4224]{1,0:T(8,128)(2,1)S(1)} %get-tuple-element.31.first), channel_id=1, source_target_pairs={{0,6},{1,7},{2,4},{3,5},{4,2},{5,3},{6,0},{7,1},{8,14},{9,15},{10,... | collective-permute-start | bytes 202760 | tf_op jit(solution)/shard_map/ppermute | solution.py:199
  57.4 3.4 %collective-permute-done.16.third = bf16[8,4224]{1,0:T(8,128)(2,1)S(1)} collective-permute-done((bf16[8,4224]{1,0:T(8,128)(2,1)S(1)}, bf16[8,4224]{1,0:T(8,128)(2,1)S(1)}, u32[]{:S(2)}, u32[]{:S(2)}) %collective-permute-start.16) | collective-permute-done | bytes 67616 | tf_op jit(solution)/shard_map/ppermute | solution.py:199
  62.5 1.3 %shard_map.103 = (bf16[128,128]{1,0:T(8,128)(2,1)S(1)}, f32[128,256]{1,0:T(8,128)S(1)}, f32[1,8]{1,0:T(1,128)}, f32[2,8,128]{2,1,0:T(8,128)S(1)}) custom-call(f32[8,8]{1,0:T(8,128)S(1)} %concatenate.12.pairs, s32[1,128]{1,0:T(1,128)S(1)} %get-tuple-element.24.segments, f32[24,128]{1,0:T(8,128)S(1)} %get-tuple-element.32.mine, ...), custom_call_target="tpu_custom_call" | custom-call | tf_op jit(solution)/shard_map/pallas_call | solution.py:266
  63.8 2.1 %collective-permute-start.24 = (bf16[128,128]{1,0:T(8,128)(2,1)S(1)}, bf16[128,128]{1,0:T(8,128)(2,1)S(1)}, u32[]{:S(2)}, u32[]{:S(2)}) collective-permute-start(bf16[128,128]{1,0:T(8,128)(2,1)S(1)} %slice_select_fusion), channel_id=1, source_target_pairs={{0,6},{1,7},{2,4},{3,5},{4,2},{5,3},{6,0},{7,1},{8,14},{9,15},{10,... | collective-permute-start | bytes 98312 | tf_op jit(solution)/shard_map/ppermute | solution.py:199
  66.7 3.3 %collective-permute-done.24 = bf16[128,128]{1,0:T(8,128)(2,1)S(1)} collective-permute-done((bf16[128,128]{1,0:T(8,128)(2,1)S(1)}, bf16[128,128]{1,0:T(8,128)(2,1)S(1)}, u32[]{:S(2)}, u32[]{:S(2)}) %collective-permute-start.24) | collective-permute-done | bytes 32800 | tf_op jit(solution)/shard_map/ppermute | solution.py:199
  73.2 1.7 %collective-permute-start.21 = (bf16[32,3072]{1,0:T(8,128)(2,1)S(1)}, bf16[32,3072]{1,0:T(8,128)(2,1)S(1)}, u32[]{:S(2)}, u32[]{:S(2)}) collective-permute-start(bf16[32,3072]{1,0:T(8,128)(2,1)S(1)} %get-tuple-element.52), channel_id=1, source_target_pairs={{0,24},{1,25},{2,26},{3,27},{4,28},{5,29},{6,30},{7,31},{8,16},{9,... | collective-permute-start | bytes 589832 | tf_op jit(solution)/shard_map/ppermute | solution.py:199
  77.3 1.8 %collective-permute-done.19.first = bf16[32,3072]{1,0:T(8,128)(2,1)S(1)} collective-permute-done((bf16[32,3072]{1,0:T(8,128)(2,1)S(1)}, bf16[32,3072]{1,0:T(8,128)(2,1)S(1)}, u32[]{:S(2)}, u32[]{:S(2)}) %collective-permute-start.19) | collective-permute-done | bytes 196640 | tf_op jit(solution)/shard_map/ppermute | solution.py:199
  80.4 3.3 %collective-permute-done.20.second = bf16[32,3072]{1,0:T(8,128)(2,1)S(1)} collective-permute-done((bf16[32,3072]{1,0:T(8,128)(2,1)S(1)}, bf16[32,3072]{1,0:T(8,128)(2,1)S(1)}, u32[]{:S(2)}, u32[]{:S(2)}) %collective-permute-start.20) | collective-permute-done | bytes 196640 | tf_op jit(solution)/shard_map/ppermute | solution.py:199
  84.8 1.8 %collective-permute-done.28.third = bf16[32,1024]{1,0:T(8,128)(2,1)S(1)} collective-permute-done((bf16[32,1024]{1,0:T(8,128)(2,1)S(1)}, bf16[32,1024]{1,0:T(8,128)(2,1)S(1)}, u32[]{:S(2)}, u32[]{:S(2)}) %collective-permute-start.28) | collective-permute-done | bytes 65568 | tf_op jit(solution)/shard_map/ppermute | solution.py:199
  87.3 4.0 %collective-permute-done.22.first = bf16[32,2048]{1,0:T(8,128)(2,1)S(1)} collective-permute-done((bf16[32,2048]{1,0:T(8,128)(2,1)S(1)}, bf16[32,2048]{1,0:T(8,128)(2,1)S(1)}, u32[]{:S(2)}, u32[]{:S(2)}) %collective-permute-start.22) | collective-permute-done | bytes 131104 | tf_op jit(solution)/shard_map/ppermute | solution.py:199
  91.4 1.5 %collective-permute-start.30 = (f32[32,1024]{1,0:T(8,128)S(1)}, f32[32,1024]{1,0:T(8,128)S(1)}, u32[]{:S(2)}, u32[]{:S(2)}) collective-permute-start(f32[32,1024]{1,0:T(8,128)S(1)} %get-tuple-element.44), channel_id=1, source_target_pairs={{0,1},{1,0},{2,3},{3,2},{4,5},{5,4},{6,7},{7,6},{8,9},{9,8},{10,11... | collective-permute-start | bytes 393224 | tf_op jit(solution)/shard_map/ppermute | solution.py:199
  (87 shorter events, 25.7 us)
Async XLA Ops:
  0.6 10.0 %collective-permute-start = (bf16[16,2048]{1,0:T(8,128)(2,1)}, bf16[16,2048]{1,0:T(8,128)(2,1)S(1)}, u32[]{:S(2)}, u32[]{:S(2)}) collective-permute-start(bf16[16,2048]{1,0:T(8,128)(2,1)} %trunk.1), channel_id=1, source_target_pairs={{0,2},{1,3},{2,0},{3,1},{4,6},{5,7},{6,4},{7,5},{8,10},{9,11},{10,... | collective-permute-start | bytes 196616 | tf_op jit(solution)/shard_map/ppermute | solution.py:199
  3.8 7.5 %collective-permute-start.1 = (bf16[16,2048]{1,0:T(8,128)(2,1)}, bf16[16,2048]{1,0:T(8,128)(2,1)S(1)}, u32[]{:S(2)}, u32[]{:S(2)}) collective-permute-start(bf16[16,2048]{1,0:T(8,128)(2,1)} %trunk.1), channel_id=1, source_target_pairs={{0,4},{1,5},{2,6},{3,7},{4,0},{5,1},{6,2},{7,3},{8,12},{9,13},{10,... | collective-permute-start | bytes 196616 | tf_op jit(solution)/shard_map/ppermute | solution.py:199
  6.3 6.3 %collective-permute-start.2 = (bf16[16,2048]{1,0:T(8,128)(2,1)}, bf16[16,2048]{1,0:T(8,128)(2,1)S(1)}, u32[]{:S(2)}, u32[]{:S(2)}) collective-permute-start(bf16[16,2048]{1,0:T(8,128)(2,1)} %trunk.1), channel_id=1, source_target_pairs={{0,6},{1,7},{2,4},{3,5},{4,2},{5,3},{6,0},{7,1},{8,14},{9,15},{10,... | collective-permute-start | bytes 196616 | tf_op jit(solution)/shard_map/ppermute | solution.py:199
  13.2 20.7 %collective-permute-start.9 = (bf16[2048,128]{1,0:T(8,128)(2,1)S(1)}, bf16[2048,128]{1,0:T(8,128)(2,1)S(1)}, u32[]{:S(2)}, u32[]{:S(2)}) collective-permute-start(bf16[2048,128]{1,0:T(8,128)(2,1)S(1)} %get-tuple-element.51), channel_id=1, source_target_pairs={{0,0},{1,16},{2,2},{3,18},{4,4},{5,20},{6,6},{7,22},{8,8},{9,24},{... | collective-permute-start | bytes 1572872 | tf_op jit(solution)/shard_map/ppermute | solution.py:199
  13.9 21.1 %collective-permute-start.11 = (bf16[2048,128]{1,0:T(8,128)(2,1)S(1)}, bf16[2048,128]{1,0:T(8,128)(2,1)S(1)}, u32[]{:S(2)}, u32[]{:S(2)}) collective-permute-start(bf16[2048,128]{1,0:T(8,128)(2,1)S(1)} %get-tuple-element.50), channel_id=1, source_target_pairs={{0,8},{1,24},{2,10},{3,26},{4,12},{5,28},{6,14},{7,30},{8,0},{9,16... | collective-permute-start | bytes 1572872 | tf_op jit(solution)/shard_map/ppermute | solution.py:199
  16.2 15.0 %collective-permute-start.5 = (bf16[128,1024]{1,0:T(8,128)(2,1)S(1)}, bf16[128,1024]{1,0:T(8,128)(2,1)S(1)}, u32[]{:S(2)}, u32[]{:S(2)}) collective-permute-start(bf16[128,1024]{1,0:T(8,128)(2,1)S(1)} %shard_map.97), channel_id=1, source_target_pairs={{0,8},{1,24},{2,10},{3,26},{12,4},{13,20},{14,6},{15,22},{16,9},{1... | collective-permute-start | bytes 786440 | tf_op jit(solution)/shard_map/ppermute | solution.py:199
  31.5 8.8 %collective-permute-start.6 = (f32[128,256]{1,0:T(8,128)S(1)}, f32[128,256]{1,0:T(8,128)S(1)}, u32[]{:S(2)}, u32[]{:S(2)}) collective-permute-start(f32[128,256]{1,0:T(8,128)S(1)} %get-tuple-element.27), channel_id=1, source_target_pairs={{0,1},{1,0},{2,3},{3,2},{4,5},{5,4},{6,7},{7,6},{8,9},{9,8},{10,11... | collective-permute-start | bytes 393224 | tf_op jit(solution)/shard_map/ppermute | solution.py:199
  35.3 5.0 %collective-permute-start.12 = (f32[128,128]{1,0:T(8,128)S(1)}, f32[128,128]{1,0:T(8,128)S(1)}, u32[]{:S(2)}, u32[]{:S(2)}) collective-permute-start(f32[128,128]{1,0:T(8,128)S(1)} %shard_map.100), channel_id=1, source_target_pairs={{0,8},{1,24},{2,10},{3,26},{4,12},{5,28},{6,14},{7,30},{8,0},{9,16... | collective-permute-start | bytes 196616 | tf_op jit(solution)/shard_map/ppermute | solution.py:199
  40.3 6.3 %collective-permute-start.7 = (f16[128,256]{1,0:T(8,128)(2,1)S(1)}, f16[128,256]{1,0:T(8,128)(2,1)S(1)}, u32[]{:S(2)}, u32[]{:S(2)}) collective-permute-start(f16[128,256]{1,0:T(8,128)(2,1)S(1)} %fusion), channel_id=1, source_target_pairs={{0,2},{1,5},{2,0},{3,7},{4,6},{5,1},{6,4},{7,3},{8,10},{9,13},{10,... | collective-permute-start | bytes 196616 | tf_op jit(solution)/shard_map/ppermute | solution.py:199
  40.4 6.1 %collective-permute-start.8 = (f16[128,128]{1,0:T(8,128)(2,1)S(1)}, f16[128,128]{1,0:T(8,128)(2,1)S(1)}, u32[]{:S(2)}, u32[]{:S(2)}) collective-permute-start(f16[128,128]{1,0:T(8,128)(2,1)S(1)} %slice_select_fusion.1), channel_id=1, source_target_pairs={{0,6},{1,7},{2,4},{3,5},{4,2},{5,3},{6,0},{7,1},{8,14},{9,15},{10,... | collective-permute-start | bytes 98312 | tf_op jit(solution)/shard_map/ppermute | solution.py:199
  44.1 6.8 %collective-permute-start.14 = (bf16[64,4096]{1,0:T(8,128)(2,1)S(1)}, bf16[64,4096]{1,0:T(8,128)(2,1)S(1)}, u32[]{:S(2)}, u32[]{:S(2)}) collective-permute-start(bf16[64,4096]{1,0:T(8,128)(2,1)S(1)} %get-tuple-element.48), channel_id=1, source_target_pairs={{0,1},{1,0},{2,3},{3,2},{4,5},{5,4},{6,7},{7,6},{8,9},{9,8},{10,11... | collective-permute-start | bytes 1572872 | tf_op jit(solution)/shard_map/ppermute | solution.py:199
  51.9 5.4 %collective-permute-start.15 = (bf16[8,4224]{1,0:T(8,128)(2,1)S(1)}, bf16[8,4224]{1,0:T(8,128)(2,1)S(1)}, u32[]{:S(2)}, u32[]{:S(2)}) collective-permute-start(bf16[8,4224]{1,0:T(8,128)(2,1)S(1)} %get-tuple-element.31.first), channel_id=1, source_target_pairs={{0,2},{1,3},{2,0},{3,1},{4,6},{5,7},{6,4},{7,5},{8,10},{9,11},{10,... | collective-permute-start | bytes 202760 | tf_op jit(solution)/shard_map/ppermute | solution.py:199
  51.9 8.9 %collective-permute-start.16 = (bf16[8,4224]{1,0:T(8,128)(2,1)S(1)}, bf16[8,4224]{1,0:T(8,128)(2,1)S(1)}, u32[]{:S(2)}, u32[]{:S(2)}) collective-permute-start(bf16[8,4224]{1,0:T(8,128)(2,1)S(1)} %get-tuple-element.31.first), channel_id=1, source_target_pairs={{0,4},{1,5},{2,6},{3,7},{4,0},{5,1},{6,2},{7,3},{8,12},{9,13},{10,... | collective-permute-start | bytes 202760 | tf_op jit(solution)/shard_map/ppermute | solution.py:199
  53.8 7.0 %collective-permute-start.17 = (bf16[8,4224]{1,0:T(8,128)(2,1)S(1)}, bf16[8,4224]{1,0:T(8,128)(2,1)S(1)}, u32[]{:S(2)}, u32[]{:S(2)}) collective-permute-start(bf16[8,4224]{1,0:T(8,128)(2,1)S(1)} %get-tuple-element.31.first), channel_id=1, source_target_pairs={{0,6},{1,7},{2,4},{3,5},{4,2},{5,3},{6,0},{7,1},{8,14},{9,15},{10,... | collective-permute-start | bytes 202760 | tf_op jit(solution)/shard_map/ppermute | solution.py:199
  63.8 6.1 %collective-permute-start.24 = (bf16[128,128]{1,0:T(8,128)(2,1)S(1)}, bf16[128,128]{1,0:T(8,128)(2,1)S(1)}, u32[]{:S(2)}, u32[]{:S(2)}) collective-permute-start(bf16[128,128]{1,0:T(8,128)(2,1)S(1)} %slice_select_fusion), channel_id=1, source_target_pairs={{0,6},{1,7},{2,4},{3,5},{4,2},{5,3},{6,0},{7,1},{8,14},{9,15},{10,... | collective-permute-start | bytes 98312 | tf_op jit(solution)/shard_map/ppermute | solution.py:199
  65.9 5.2 %collective-permute-start.23 = (bf16[128,256]{1,0:T(8,128)(2,1)S(1)}, bf16[128,256]{1,0:T(8,128)(2,1)S(1)}, u32[]{:S(2)}, u32[]{:S(2)}) collective-permute-start(bf16[128,256]{1,0:T(8,128)(2,1)S(1)} %convert_element_type.36), channel_id=1, source_target_pairs={{0,2},{1,5},{2,0},{3,7},{4,6},{5,1},{6,4},{7,3},{8,10},{9,13},{10,... | collective-permute-start | bytes 196616 | tf_op jit(solution)/shard_map/ppermute | solution.py:199
  71.3 7.8 %collective-permute-start.19 = (bf16[32,3072]{1,0:T(8,128)(2,1)S(1)}, bf16[32,3072]{1,0:T(8,128)(2,1)S(1)}, u32[]{:S(2)}, u32[]{:S(2)}) collective-permute-start(bf16[32,3072]{1,0:T(8,128)(2,1)S(1)} %get-tuple-element.54), channel_id=1, source_target_pairs={{0,8},{1,9},{2,10},{3,11},{4,12},{5,13},{6,14},{7,15},{8,0},{9,1},... | collective-permute-start | bytes 589832 | tf_op jit(solution)/shard_map/ppermute | solution.py:199
  72.0 11.6 %collective-permute-start.20 = (bf16[32,3072]{1,0:T(8,128)(2,1)S(1)}, bf16[32,3072]{1,0:T(8,128)(2,1)S(1)}, u32[]{:S(2)}, u32[]{:S(2)}) collective-permute-start(bf16[32,3072]{1,0:T(8,128)(2,1)S(1)} %get-tuple-element.53), channel_id=1, source_target_pairs={{0,16},{1,17},{2,18},{3,19},{4,20},{5,21},{6,22},{7,23},{8,24},{9,... | collective-permute-start | bytes 589832 | tf_op jit(solution)/shard_map/ppermute | solution.py:199
  73.2 11.1 %collective-permute-start.21 = (bf16[32,3072]{1,0:T(8,128)(2,1)S(1)}, bf16[32,3072]{1,0:T(8,128)(2,1)S(1)}, u32[]{:S(2)}, u32[]{:S(2)}) collective-permute-start(bf16[32,3072]{1,0:T(8,128)(2,1)S(1)} %get-tuple-element.52), channel_id=1, source_target_pairs={{0,24},{1,25},{2,26},{3,27},{4,28},{5,29},{6,30},{7,31},{8,16},{9,... | collective-permute-start | bytes 589832 | tf_op jit(solution)/shard_map/ppermute | solution.py:199
  75.4 9.3 %collective-permute-start.26 = (bf16[32,1024]{1,0:T(8,128)(2,1)S(1)}, bf16[32,1024]{1,0:T(8,128)(2,1)S(1)}, u32[]{:S(2)}, u32[]{:S(2)}) collective-permute-start(bf16[32,1024]{1,0:T(8,128)(2,1)S(1)} %get-tuple-element.57), channel_id=1, source_target_pairs={{0,8},{1,9},{2,10},{3,11},{4,12},{5,13},{6,14},{7,15},{8,0},{9,1},... | collective-permute-start | bytes 196616 | tf_op jit(solution)/shard_map/ppermute | solution.py:199
  76.2 8.6 %collective-permute-start.27 = (bf16[32,1024]{1,0:T(8,128)(2,1)S(1)}, bf16[32,1024]{1,0:T(8,128)(2,1)S(1)}, u32[]{:S(2)}, u32[]{:S(2)}) collective-permute-start(bf16[32,1024]{1,0:T(8,128)(2,1)S(1)} %get-tuple-element.56), channel_id=1, source_target_pairs={{0,16},{1,17},{2,18},{3,19},{4,20},{5,21},{6,22},{7,23},{8,24},{9,... | collective-permute-start | bytes 196616 | tf_op jit(solution)/shard_map/ppermute | solution.py:199
  79.1 7.5 %collective-permute-start.28 = (bf16[32,1024]{1,0:T(8,128)(2,1)S(1)}, bf16[32,1024]{1,0:T(8,128)(2,1)S(1)}, u32[]{:S(2)}, u32[]{:S(2)}) collective-permute-start(bf16[32,1024]{1,0:T(8,128)(2,1)S(1)} %get-tuple-element.55), channel_id=1, source_target_pairs={{0,24},{1,25},{2,26},{3,27},{4,28},{5,29},{6,30},{7,31},{8,16},{9,... | collective-permute-start | bytes 196616 | tf_op jit(solution)/shard_map/ppermute | solution.py:199
  84.3 7.0 %collective-permute-start.22 = (bf16[32,2048]{1,0:T(8,128)(2,1)S(1)}, bf16[32,2048]{1,0:T(8,128)(2,1)S(1)}, u32[]{:S(2)}, u32[]{:S(2)}) collective-permute-start(bf16[32,2048]{1,0:T(8,128)(2,1)S(1)} %get-tuple-element.38), channel_id=1, source_target_pairs={{0,2},{1,6},{2,3},{3,7},{4,0},{5,4},{6,1},{7,5},{8,10},{9,14},{10,... | collective-permute-start | bytes 393224 | tf_op jit(solution)/shard_map/ppermute | solution.py:199
  86.6 4.7 %collective-permute-start.29 = (bf16[32,2048]{1,0:T(8,128)(2,1)S(1)}, bf16[32,2048]{1,0:T(8,128)(2,1)S(1)}, u32[]{:S(2)}, u32[]{:S(2)}) collective-permute-start(bf16[32,2048]{1,0:T(8,128)(2,1)S(1)} %shard_map.107), channel_id=1, source_target_pairs={{0,0},{1,4},{2,1},{3,5},{4,2},{5,6},{6,3},{7,7},{8,8},{9,12},{10,9... | collective-permute-start | bytes 393224 | tf_op jit(solution)/shard_map/ppermute | solution.py:199
  (15 other events, 52.0 us)

commit v3 on v2

--- a/solution.py
+++ b/solution.py
@@ -559,7 +559,9 @@
     core = here()[1] % 2
     for out, side in ((kept, core), (given, 1 - core)):
         columns = pl.ds(pl.multiple_of(side * width, width), width)
-        out[...] = first[:, columns].astype(jnp.float32) + second[:, columns].astype(jnp.float32)
+        out[...] = (
+            first[:, columns].astype(jnp.float32) + second[:, columns].astype(jnp.float32)
+        ).astype(out.dtype)
 
 
 def fast_device(
@@ -686,9 +688,12 @@
     (near_pair,) = local_call(near_sum_kernel, [pair_shape], near_grad, *near_got, far_one)
     near_part = send(near_pair, lambda m, z, k: (m, 2 * k + z // 2, z % 2))
     kept, given = local_call(
-        merge_kernel, [((member_rows, block_width), f32)] * 2, far_part, near_part
-    )
-    total = kept + core_swap(given)
+        merge_kernel,
+        [((member_rows, block_width), f32), ((member_rows, block_width), bf16)],
+        far_part,
+        near_part,
+    )
+    total = kept + core_swap(given).astype(f32)
     return (total, rewards)
 
 

time: 95.1 us -> 95 us (level)
  no operation moved by 1% of the time
where the time goes in v3:
time: 95 us; the launch traced here: 94.4 us
  starting transfers between devices  41.5 us (44%)
  waiting for transfers between devices  41.3 us (43%)
  Pallas kernels  5.32 us (6%)
  local copies, waits for them, and re-layouts  4.48 us (5%)
    ppermute x31, starting transfers between devices, send(): return lax.ppermute(block, ('member', 'shard'), route_pairs(target))  41.5 us
    ppermute x31, waiting for transfers between devices, send(): return lax.ppermute(block, ('member', 'shard'), route_pairs(target))  41.3 us
    pallas_call x12, Pallas kernels, local_call(): pl.pallas_call(kernel, out_shape=[jax.ShapeDtypeStruct(shape, dtype) for...  4.75 us
    unnamed x16, local copies, waits for them, and re-layouts  4.06 us
  transfers between devices with their start and end apart: 31, of which 18 were waited for; matrix products, arithmetic and copies ran while one was open for 1% of the time, Pallas kernels for 2%

profile of v3, /device:TPU:0, one launch (start us, length us, event | category | flops | bytes accessed | tf_op | source)
XLA Modules:
  0.0 94.4 jit_solution(18281796457588437594)
XLA Ops:
  0.6 3.1 %collective-permute-start = (bf16[16,2048]{1,0:T(8,128)(2,1)}, bf16[16,2048]{1,0:T(8,128)(2,1)S(1)}, u32[]{:S(2)}, u32[]{:S(2)}) collective-permute-start(bf16[16,2048]{1,0:T(8,128)(2,1)} %trunk.1), channel_id=1, source_target_pairs={{0,2},{1,3},{2,0},{3,1},{4,6},{5,7},{6,4},{7,5},{8,10},{9,11},{10,... | collective-permute-start | bytes 196616 | tf_op jit(solution)/shard_map/ppermute | solution.py:199
  3.8 2.6 %collective-permute-start.1 = (bf16[16,2048]{1,0:T(8,128)(2,1)}, bf16[16,2048]{1,0:T(8,128)(2,1)S(1)}, u32[]{:S(2)}, u32[]{:S(2)}) collective-permute-start(bf16[16,2048]{1,0:T(8,128)(2,1)} %trunk.1), channel_id=1, source_target_pairs={{0,4},{1,5},{2,6},{3,7},{4,0},{5,1},{6,2},{7,3},{8,12},{9,13},{10,... | collective-permute-start | bytes 196616 | tf_op jit(solution)/shard_map/ppermute | solution.py:199
  11.2 1.4 %collective-permute-done.2.refs_3_ = bf16[16,2048]{1,0:T(8,128)(2,1)S(1)} collective-permute-done((bf16[16,2048]{1,0:T(8,128)(2,1)}, bf16[16,2048]{1,0:T(8,128)(2,1)S(1)}, u32[]{:S(2)}, u32[]{:S(2)}) %collective-permute-start.2) | collective-permute-done | bytes 65568 | tf_op jit(solution)/shard_map/ppermute | solution.py:199
  13.9 1.6 %collective-permute-start.11 = (bf16[2048,128]{1,0:T(8,128)(2,1)S(1)}, bf16[2048,128]{1,0:T(8,128)(2,1)S(1)}, u32[]{:S(2)}, u32[]{:S(2)}) collective-permute-start(bf16[2048,128]{1,0:T(8,128)(2,1)S(1)} %get-tuple-element.50), channel_id=1, source_target_pairs={{0,8},{1,24},{2,10},{3,26},{4,12},{5,28},{6,14},{7,30},{8,0},{9,16... | collective-permute-start | bytes 1572872 | tf_op jit(solution)/shard_map/ppermute | solution.py:199
  16.2 2.6 %collective-permute-start.5 = (bf16[128,1024]{1,0:T(8,128)(2,1)S(1)}, bf16[128,1024]{1,0:T(8,128)(2,1)S(1)}, u32[]{:S(2)}, u32[]{:S(2)}) collective-permute-start(bf16[128,1024]{1,0:T(8,128)(2,1)S(1)} %shard_map.97), channel_id=1, source_target_pairs={{0,8},{1,24},{2,10},{3,26},{12,4},{13,20},{14,6},{15,22},{16,9},{1... | collective-permute-start | bytes 786440 | tf_op jit(solution)/shard_map/ppermute | solution.py:199
  18.7 12.4 %collective-permute-done.5.second = bf16[128,1024]{1,0:T(8,128)(2,1)S(1)} collective-permute-done((bf16[128,1024]{1,0:T(8,128)(2,1)S(1)}, bf16[128,1024]{1,0:T(8,128)(2,1)S(1)}, u32[]{:S(2)}, u32[]{:S(2)}) %collective-permute-start.5) | collective-permute-done | bytes 262176 | tf_op jit(solution)/shard_map/ppermute | solution.py:199
  31.5 2.4 %collective-permute-start.6 = (f32[128,256]{1,0:T(8,128)S(1)}, f32[128,256]{1,0:T(8,128)S(1)}, u32[]{:S(2)}, u32[]{:S(2)}) collective-permute-start(f32[128,256]{1,0:T(8,128)S(1)} %get-tuple-element.27), channel_id=1, source_target_pairs={{0,1},{1,0},{2,3},{3,2},{4,5},{5,4},{6,7},{7,6},{8,9},{9,8},{10,11... | collective-permute-start | bytes 393224 | tf_op jit(solution)/shard_map/ppermute | solution.py:199
  35.3 2.7 %collective-permute-start.12 = (f32[128,128]{1,0:T(8,128)S(1)}, f32[128,128]{1,0:T(8,128)S(1)}, u32[]{:S(2)}, u32[]{:S(2)}) collective-permute-start(f32[128,128]{1,0:T(8,128)S(1)} %shard_map.100), channel_id=1, source_target_pairs={{0,8},{1,24},{2,10},{3,26},{4,12},{5,28},{6,14},{7,30},{8,0},{9,16... | collective-permute-start | bytes 196616 | tf_op jit(solution)/shard_map/ppermute | solution.py:199
  38.0 2.2 %collective-permute-done.12 = f32[128,128]{1,0:T(8,128)S(1)} collective-permute-done((f32[128,128]{1,0:T(8,128)S(1)}, f32[128,128]{1,0:T(8,128)S(1)}, u32[]{:S(2)}, u32[]{:S(2)}) %collective-permute-start.12) | collective-permute-done | bytes 65568 | tf_op jit(solution)/shard_map/ppermute | solution.py:199
  40.4 3.6 %collective-permute-start.8 = (f16[128,128]{1,0:T(8,128)(2,1)S(1)}, f16[128,128]{1,0:T(8,128)(2,1)S(1)}, u32[]{:S(2)}, u32[]{:S(2)}) collective-permute-start(f16[128,128]{1,0:T(8,128)(2,1)S(1)} %slice_select_fusion.1), channel_id=1, source_target_pairs={{0,6},{1,7},{2,4},{3,5},{4,2},{5,3},{6,0},{7,1},{8,14},{9,15},{10,... | collective-permute-start | bytes 98312 | tf_op jit(solution)/shard_map/ppermute | solution.py:199
  44.1 1.5 %collective-permute-start.14 = (bf16[64,4096]{1,0:T(8,128)(2,1)S(1)}, bf16[64,4096]{1,0:T(8,128)(2,1)S(1)}, u32[]{:S(2)}, u32[]{:S(2)}) collective-permute-start(bf16[64,4096]{1,0:T(8,128)(2,1)S(1)} %get-tuple-element.48), channel_id=1, source_target_pairs={{0,1},{1,0},{2,3},{3,2},{4,5},{5,4},{6,7},{7,6},{8,9},{9,8},{10,11... | collective-permute-start | bytes 1572872 | tf_op jit(solution)/shard_map/ppermute | solution.py:199
  46.6 3.2 %collective-permute-start.13 = (f32[128,384]{1,0:T(8,128)S(1)}, f32[128,384]{1,0:T(8,128)S(1)}, u32[]{:S(2)}, u32[]{:S(2)}) collective-permute-start(f32[128,384]{1,0:T(8,128)S(1)} %pad_maximum_fusion.mine), channel_id=1, source_target_pairs={{0,1},{1,0},{2,3},{3,2},{4,5},{5,4},{6,7},{7,6},{8,9},{9,8},{10,11... | collective-permute-start | bytes 589832 | tf_op jit(solution)/shard_map/ppermute | solution.py:199
  51.9 1.9 %collective-permute-start.16 = (bf16[8,4224]{1,0:T(8,128)(2,1)S(1)}, bf16[8,4224]{1,0:T(8,128)(2,1)S(1)}, u32[]{:S(2)}, u32[]{:S(2)}) collective-permute-start(bf16[8,4224]{1,0:T(8,128)(2,1)S(1)} %get-tuple-element.31.first), channel_id=1, source_target_pairs={{0,4},{1,5},{2,6},{3,7},{4,0},{5,1},{6,2},{7,3},{8,12},{9,13},{10,... | collective-permute-start | bytes 202760 | tf_op jit(solution)/shard_map/ppermute | solution.py:199
  53.8 2.5 %collective-permute-start.17 = (bf16[8,4224]{1,0:T(8,128)(2,1)S(1)}, bf16[8,4224]{1,0:T(8,128)(2,1)S(1)}, u32[]{:S(2)}, u32[]{:S(2)}) collective-permute-start(bf16[8,4224]{1,0:T(8,128)(2,1)S(1)} %get-tuple-element.31.first), channel_id=1, source_target_pairs={{0,6},{1,7},{2,4},{3,5},{4,2},{5,3},{6,0},{7,1},{8,14},{9,15},{10,... | collective-permute-start | bytes 202760 | tf_op jit(solution)/shard_map/ppermute | solution.py:199
  57.4 3.4 %collective-permute-done.16.third = bf16[8,4224]{1,0:T(8,128)(2,1)S(1)} collective-permute-done((bf16[8,4224]{1,0:T(8,128)(2,1)S(1)}, bf16[8,4224]{1,0:T(8,128)(2,1)S(1)}, u32[]{:S(2)}, u32[]{:S(2)}) %collective-permute-start.16) | collective-permute-done | bytes 67616 | tf_op jit(solution)/shard_map/ppermute | solution.py:199
  62.5 1.3 %shard_map.103 = (bf16[128,128]{1,0:T(8,128)(2,1)S(1)}, f32[128,256]{1,0:T(8,128)S(1)}, f32[1,8]{1,0:T(1,128)}, f32[2,8,128]{2,1,0:T(8,128)S(1)}) custom-call(f32[8,8]{1,0:T(8,128)S(1)} %concatenate.12.pairs, s32[1,128]{1,0:T(1,128)S(1)} %get-tuple-element.24.segments, f32[24,128]{1,0:T(8,128)S(1)} %get-tuple-element.32.mine, ...), custom_call_target="tpu_custom_call" | custom-call | tf_op jit(solution)/shard_map/pallas_call | solution.py:266
  63.8 2.1 %collective-permute-start.24 = (bf16[128,128]{1,0:T(8,128)(2,1)S(1)}, bf16[128,128]{1,0:T(8,128)(2,1)S(1)}, u32[]{:S(2)}, u32[]{:S(2)}) collective-permute-start(bf16[128,128]{1,0:T(8,128)(2,1)S(1)} %slice_select_fusion), channel_id=1, source_target_pairs={{0,6},{1,7},{2,4},{3,5},{4,2},{5,3},{6,0},{7,1},{8,14},{9,15},{10,... | collective-permute-start | bytes 98312 | tf_op jit(solution)/shard_map/ppermute | solution.py:199
  66.7 3.3 %collective-permute-done.24 = bf16[128,128]{1,0:T(8,128)(2,1)S(1)} collective-permute-done((bf16[128,128]{1,0:T(8,128)(2,1)S(1)}, bf16[128,128]{1,0:T(8,128)(2,1)S(1)}, u32[]{:S(2)}, u32[]{:S(2)}) %collective-permute-start.24) | collective-permute-done | bytes 32800 | tf_op jit(solution)/shard_map/ppermute | solution.py:199
  73.2 1.7 %collective-permute-start.21 = (bf16[32,3072]{1,0:T(8,128)(2,1)S(1)}, bf16[32,3072]{1,0:T(8,128)(2,1)S(1)}, u32[]{:S(2)}, u32[]{:S(2)}) collective-permute-start(bf16[32,3072]{1,0:T(8,128)(2,1)S(1)} %get-tuple-element.52), channel_id=1, source_target_pairs={{0,24},{1,25},{2,26},{3,27},{4,28},{5,29},{6,30},{7,31},{8,16},{9,... | collective-permute-start | bytes 589832 | tf_op jit(solution)/shard_map/ppermute | solution.py:199
  77.3 1.8 %collective-permute-done.19.first = bf16[32,3072]{1,0:T(8,128)(2,1)S(1)} collective-permute-done((bf16[32,3072]{1,0:T(8,128)(2,1)S(1)}, bf16[32,3072]{1,0:T(8,128)(2,1)S(1)}, u32[]{:S(2)}, u32[]{:S(2)}) %collective-permute-start.19) | collective-permute-done | bytes 196640 | tf_op jit(solution)/shard_map/ppermute | solution.py:199
  80.4 3.3 %collective-permute-done.20.second = bf16[32,3072]{1,0:T(8,128)(2,1)S(1)} collective-permute-done((bf16[32,3072]{1,0:T(8,128)(2,1)S(1)}, bf16[32,3072]{1,0:T(8,128)(2,1)S(1)}, u32[]{:S(2)}, u32[]{:S(2)}) %collective-permute-start.20) | collective-permute-done | bytes 196640 | tf_op jit(solution)/shard_map/ppermute | solution.py:199
  84.8 1.8 %collective-permute-done.28.third = bf16[32,1024]{1,0:T(8,128)(2,1)S(1)} collective-permute-done((bf16[32,1024]{1,0:T(8,128)(2,1)S(1)}, bf16[32,1024]{1,0:T(8,128)(2,1)S(1)}, u32[]{:S(2)}, u32[]{:S(2)}) %collective-permute-start.28) | collective-permute-done | bytes 65568 | tf_op jit(solution)/shard_map/ppermute | solution.py:199
  87.3 4.0 %collective-permute-done.22.first = bf16[32,2048]{1,0:T(8,128)(2,1)S(1)} collective-permute-done((bf16[32,2048]{1,0:T(8,128)(2,1)S(1)}, bf16[32,2048]{1,0:T(8,128)(2,1)S(1)}, u32[]{:S(2)}, u32[]{:S(2)}) %collective-permute-start.22) | collective-permute-done | bytes 131104 | tf_op jit(solution)/shard_map/ppermute | solution.py:199
  91.4 1.5 %collective-permute-start.30 = (bf16[32,1024]{1,0:T(8,128)(2,1)S(1)}, bf16[32,1024]{1,0:T(8,128)(2,1)S(1)}, u32[]{:S(2)}, u32[]{:S(2)}) collective-permute-start(bf16[32,1024]{1,0:T(8,128)(2,1)S(1)} %get-tuple-element.44), channel_id=1, source_target_pairs={{0,1},{1,0},{2,3},{3,2},{4,5},{5,4},{6,7},{7,6},{8,9},{9,8},{10,11... | collective-permute-start | bytes 196616 | tf_op jit(solution)/shard_map/ppermute | solution.py:199
  (87 shorter events, 25.6 us)
Async XLA Ops:
  0.6 10.0 %collective-permute-start = (bf16[16,2048]{1,0:T(8,128)(2,1)}, bf16[16,2048]{1,0:T(8,128)(2,1)S(1)}, u32[]{:S(2)}, u32[]{:S(2)}) collective-permute-start(bf16[16,2048]{1,0:T(8,128)(2,1)} %trunk.1), channel_id=1, source_target_pairs={{0,2},{1,3},{2,0},{3,1},{4,6},{5,7},{6,4},{7,5},{8,10},{9,11},{10,... | collective-permute-start | bytes 196616 | tf_op jit(solution)/shard_map/ppermute | solution.py:199
  3.8 7.5 %collective-permute-start.1 = (bf16[16,2048]{1,0:T(8,128)(2,1)}, bf16[16,2048]{1,0:T(8,128)(2,1)S(1)}, u32[]{:S(2)}, u32[]{:S(2)}) collective-permute-start(bf16[16,2048]{1,0:T(8,128)(2,1)} %trunk.1), channel_id=1, source_target_pairs={{0,4},{1,5},{2,6},{3,7},{4,0},{5,1},{6,2},{7,3},{8,12},{9,13},{10,... | collective-permute-start | bytes 196616 | tf_op jit(solution)/shard_map/ppermute | solution.py:199
  6.3 6.3 %collective-permute-start.2 = (bf16[16,2048]{1,0:T(8,128)(2,1)}, bf16[16,2048]{1,0:T(8,128)(2,1)S(1)}, u32[]{:S(2)}, u32[]{:S(2)}) collective-permute-start(bf16[16,2048]{1,0:T(8,128)(2,1)} %trunk.1), channel_id=1, source_target_pairs={{0,6},{1,7},{2,4},{3,5},{4,2},{5,3},{6,0},{7,1},{8,14},{9,15},{10,... | collective-permute-start | bytes 196616 | tf_op jit(solution)/shard_map/ppermute | solution.py:199
  13.2 20.7 %collective-permute-start.9 = (bf16[2048,128]{1,0:T(8,128)(2,1)S(1)}, bf16[2048,128]{1,0:T(8,128)(2,1)S(1)}, u32[]{:S(2)}, u32[]{:S(2)}) collective-permute-start(bf16[2048,128]{1,0:T(8,128)(2,1)S(1)} %get-tuple-element.51), channel_id=1, source_target_pairs={{0,0},{1,16},{2,2},{3,18},{4,4},{5,20},{6,6},{7,22},{8,8},{9,24},{... | collective-permute-start | bytes 1572872 | tf_op jit(solution)/shard_map/ppermute | solution.py:199
  13.9 21.1 %collective-permute-start.11 = (bf16[2048,128]{1,0:T(8,128)(2,1)S(1)}, bf16[2048,128]{1,0:T(8,128)(2,1)S(1)}, u32[]{:S(2)}, u32[]{:S(2)}) collective-permute-start(bf16[2048,128]{1,0:T(8,128)(2,1)S(1)} %get-tuple-element.50), channel_id=1, source_target_pairs={{0,8},{1,24},{2,10},{3,26},{4,12},{5,28},{6,14},{7,30},{8,0},{9,16... | collective-permute-start | bytes 1572872 | tf_op jit(solution)/shard_map/ppermute | solution.py:199
  16.2 15.0 %collective-permute-start.5 = (bf16[128,1024]{1,0:T(8,128)(2,1)S(1)}, bf16[128,1024]{1,0:T(8,128)(2,1)S(1)}, u32[]{:S(2)}, u32[]{:S(2)}) collective-permute-start(bf16[128,1024]{1,0:T(8,128)(2,1)S(1)} %shard_map.97), channel_id=1, source_target_pairs={{0,8},{1,24},{2,10},{3,26},{12,4},{13,20},{14,6},{15,22},{16,9},{1... | collective-permute-start | bytes 786440 | tf_op jit(solution)/shard_map/ppermute | solution.py:199
  31.5 8.8 %collective-permute-start.6 = (f32[128,256]{1,0:T(8,128)S(1)}, f32[128,256]{1,0:T(8,128)S(1)}, u32[]{:S(2)}, u32[]{:S(2)}) collective-permute-start(f32[128,256]{1,0:T(8,128)S(1)} %get-tuple-element.27), channel_id=1, source_target_pairs={{0,1},{1,0},{2,3},{3,2},{4,5},{5,4},{6,7},{7,6},{8,9},{9,8},{10,11... | collective-permute-start | bytes 393224 | tf_op jit(solution)/shard_map/ppermute | solution.py:199
  35.3 5.0 %collective-permute-start.12 = (f32[128,128]{1,0:T(8,128)S(1)}, f32[128,128]{1,0:T(8,128)S(1)}, u32[]{:S(2)}, u32[]{:S(2)}) collective-permute-start(f32[128,128]{1,0:T(8,128)S(1)} %shard_map.100), channel_id=1, source_target_pairs={{0,8},{1,24},{2,10},{3,26},{4,12},{5,28},{6,14},{7,30},{8,0},{9,16... | collective-permute-start | bytes 196616 | tf_op jit(solution)/shard_map/ppermute | solution.py:199
  40.3 6.3 %collective-permute-start.7 = (f16[128,256]{1,0:T(8,128)(2,1)S(1)}, f16[128,256]{1,0:T(8,128)(2,1)S(1)}, u32[]{:S(2)}, u32[]{:S(2)}) collective-permute-start(f16[128,256]{1,0:T(8,128)(2,1)S(1)} %fusion), channel_id=1, source_target_pairs={{0,2},{1,5},{2,0},{3,7},{4,6},{5,1},{6,4},{7,3},{8,10},{9,13},{10,... | collective-permute-start | bytes 196616 | tf_op jit(solution)/shard_map/ppermute | solution.py:199
  40.4 6.1 %collective-permute-start.8 = (f16[128,128]{1,0:T(8,128)(2,1)S(1)}, f16[128,128]{1,0:T(8,128)(2,1)S(1)}, u32[]{:S(2)}, u32[]{:S(2)}) collective-permute-start(f16[128,128]{1,0:T(8,128)(2,1)S(1)} %slice_select_fusion.1), channel_id=1, source_target_pairs={{0,6},{1,7},{2,4},{3,5},{4,2},{5,3},{6,0},{7,1},{8,14},{9,15},{10,... | collective-permute-start | bytes 98312 | tf_op jit(solution)/shard_map/ppermute | solution.py:199
  44.1 6.8 %collective-permute-start.14 = (bf16[64,4096]{1,0:T(8,128)(2,1)S(1)}, bf16[64,4096]{1,0:T(8,128)(2,1)S(1)}, u32[]{:S(2)}, u32[]{:S(2)}) collective-permute-start(bf16[64,4096]{1,0:T(8,128)(2,1)S(1)} %get-tuple-element.48), channel_id=1, source_target_pairs={{0,1},{1,0},{2,3},{3,2},{4,5},{5,4},{6,7},{7,6},{8,9},{9,8},{10,11... | collective-permute-start | bytes 1572872 | tf_op jit(solution)/shard_map/ppermute | solution.py:199
  51.9 5.4 %collective-permute-start.15 = (bf16[8,4224]{1,0:T(8,128)(2,1)S(1)}, bf16[8,4224]{1,0:T(8,128)(2,1)S(1)}, u32[]{:S(2)}, u32[]{:S(2)}) collective-permute-start(bf16[8,4224]{1,0:T(8,128)(2,1)S(1)} %get-tuple-element.31.first), channel_id=1, source_target_pairs={{0,2},{1,3},{2,0},{3,1},{4,6},{5,7},{6,4},{7,5},{8,10},{9,11},{10,... | collective-permute-start | bytes 202760 | tf_op jit(solution)/shard_map/ppermute | solution.py:199
  51.9 8.9 %collective-permute-start.16 = (bf16[8,4224]{1,0:T(8,128)(2,1)S(1)}, bf16[8,4224]{1,0:T(8,128)(2,1)S(1)}, u32[]{:S(2)}, u32[]{:S(2)}) collective-permute-start(bf16[8,4224]{1,0:T(8,128)(2,1)S(1)} %get-tuple-element.31.first), channel_id=1, source_target_pairs={{0,4},{1,5},{2,6},{3,7},{4,0},{5,1},{6,2},{7,3},{8,12},{9,13},{10,... | collective-permute-start | bytes 202760 | tf_op jit(solution)/shard_map/ppermute | solution.py:199
  53.8 7.0 %collective-permute-start.17 = (bf16[8,4224]{1,0:T(8,128)(2,1)S(1)}, bf16[8,4224]{1,0:T(8,128)(2,1)S(1)}, u32[]{:S(2)}, u32[]{:S(2)}) collective-permute-start(bf16[8,4224]{1,0:T(8,128)(2,1)S(1)} %get-tuple-element.31.first), channel_id=1, source_target_pairs={{0,6},{1,7},{2,4},{3,5},{4,2},{5,3},{6,0},{7,1},{8,14},{9,15},{10,... | collective-permute-start | bytes 202760 | tf_op jit(solution)/shard_map/ppermute | solution.py:199
  63.8 6.1 %collective-permute-start.24 = (bf16[128,128]{1,0:T(8,128)(2,1)S(1)}, bf16[128,128]{1,0:T(8,128)(2,1)S(1)}, u32[]{:S(2)}, u32[]{:S(2)}) collective-permute-start(bf16[128,128]{1,0:T(8,128)(2,1)S(1)} %slice_select_fusion), channel_id=1, source_target_pairs={{0,6},{1,7},{2,4},{3,5},{4,2},{5,3},{6,0},{7,1},{8,14},{9,15},{10,... | collective-permute-start | bytes 98312 | tf_op jit(solution)/shard_map/ppermute | solution.py:199
  65.9 5.2 %collective-permute-start.23 = (bf16[128,256]{1,0:T(8,128)(2,1)S(1)}, bf16[128,256]{1,0:T(8,128)(2,1)S(1)}, u32[]{:S(2)}, u32[]{:S(2)}) collective-permute-start(bf16[128,256]{1,0:T(8,128)(2,1)S(1)} %convert_element_type.39), channel_id=1, source_target_pairs={{0,2},{1,5},{2,0},{3,7},{4,6},{5,1},{6,4},{7,3},{8,10},{9,13},{10,... | collective-permute-start | bytes 196616 | tf_op jit(solution)/shard_map/ppermute | solution.py:199
  71.3 7.8 %collective-permute-start.19 = (bf16[32,3072]{1,0:T(8,128)(2,1)S(1)}, bf16[32,3072]{1,0:T(8,128)(2,1)S(1)}, u32[]{:S(2)}, u32[]{:S(2)}) collective-permute-start(bf16[32,3072]{1,0:T(8,128)(2,1)S(1)} %get-tuple-element.54), channel_id=1, source_target_pairs={{0,8},{1,9},{2,10},{3,11},{4,12},{5,13},{6,14},{7,15},{8,0},{9,1},... | collective-permute-start | bytes 589832 | tf_op jit(solution)/shard_map/ppermute | solution.py:199
  72.0 11.6 %collective-permute-start.20 = (bf16[32,3072]{1,0:T(8,128)(2,1)S(1)}, bf16[32,3072]{1,0:T(8,128)(2,1)S(1)}, u32[]{:S(2)}, u32[]{:S(2)}) collective-permute-start(bf16[32,3072]{1,0:T(8,128)(2,1)S(1)} %get-tuple-element.53), channel_id=1, source_target_pairs={{0,16},{1,17},{2,18},{3,19},{4,20},{5,21},{6,22},{7,23},{8,24},{9,... | collective-permute-start | bytes 589832 | tf_op jit(solution)/shard_map/ppermute | solution.py:199
  73.2 11.1 %collective-permute-start.21 = (bf16[32,3072]{1,0:T(8,128)(2,1)S(1)}, bf16[32,3072]{1,0:T(8,128)(2,1)S(1)}, u32[]{:S(2)}, u32[]{:S(2)}) collective-permute-start(bf16[32,3072]{1,0:T(8,128)(2,1)S(1)} %get-tuple-element.52), channel_id=1, source_target_pairs={{0,24},{1,25},{2,26},{3,27},{4,28},{5,29},{6,30},{7,31},{8,16},{9,... | collective-permute-start | bytes 589832 | tf_op jit(solution)/shard_map/ppermute | solution.py:199
  75.4 9.3 %collective-permute-start.26 = (bf16[32,1024]{1,0:T(8,128)(2,1)S(1)}, bf16[32,1024]{1,0:T(8,128)(2,1)S(1)}, u32[]{:S(2)}, u32[]{:S(2)}) collective-permute-start(bf16[32,1024]{1,0:T(8,128)(2,1)S(1)} %get-tuple-element.57), channel_id=1, source_target_pairs={{0,8},{1,9},{2,10},{3,11},{4,12},{5,13},{6,14},{7,15},{8,0},{9,1},... | collective-permute-start | bytes 196616 | tf_op jit(solution)/shard_map/ppermute | solution.py:199
  76.2 8.6 %collective-permute-start.27 = (bf16[32,1024]{1,0:T(8,128)(2,1)S(1)}, bf16[32,1024]{1,0:T(8,128)(2,1)S(1)}, u32[]{:S(2)}, u32[]{:S(2)}) collective-permute-start(bf16[32,1024]{1,0:T(8,128)(2,1)S(1)} %get-tuple-element.56), channel_id=1, source_target_pairs={{0,16},{1,17},{2,18},{3,19},{4,20},{5,21},{6,22},{7,23},{8,24},{9,... | collective-permute-start | bytes 196616 | tf_op jit(solution)/shard_map/ppermute | solution.py:199
  79.1 7.5 %collective-permute-start.28 = (bf16[32,1024]{1,0:T(8,128)(2,1)S(1)}, bf16[32,1024]{1,0:T(8,128)(2,1)S(1)}, u32[]{:S(2)}, u32[]{:S(2)}) collective-permute-start(bf16[32,1024]{1,0:T(8,128)(2,1)S(1)} %get-tuple-element.55), channel_id=1, source_target_pairs={{0,24},{1,25},{2,26},{3,27},{4,28},{5,29},{6,30},{7,31},{8,16},{9,... | collective-permute-start | bytes 196616 | tf_op jit(solution)/shard_map/ppermute | solution.py:199
  84.3 7.0 %collective-permute-start.22 = (bf16[32,2048]{1,0:T(8,128)(2,1)S(1)}, bf16[32,2048]{1,0:T(8,128)(2,1)S(1)}, u32[]{:S(2)}, u32[]{:S(2)}) collective-permute-start(bf16[32,2048]{1,0:T(8,128)(2,1)S(1)} %get-tuple-element.38), channel_id=1, source_target_pairs={{0,2},{1,6},{2,3},{3,7},{4,0},{5,4},{6,1},{7,5},{8,10},{9,14},{10,... | collective-permute-start | bytes 393224 | tf_op jit(solution)/shard_map/ppermute | solution.py:199
  86.6 4.7 %collective-permute-start.29 = (bf16[32,2048]{1,0:T(8,128)(2,1)S(1)}, bf16[32,2048]{1,0:T(8,128)(2,1)S(1)}, u32[]{:S(2)}, u32[]{:S(2)}) collective-permute-start(bf16[32,2048]{1,0:T(8,128)(2,1)S(1)} %shard_map.107), channel_id=1, source_target_pairs={{0,0},{1,4},{2,1},{3,5},{4,2},{5,6},{6,3},{7,7},{8,8},{9,12},{10,9... | collective-permute-start | bytes 393224 | tf_op jit(solution)/shard_map/ppermute | solution.py:199
  (15 other events, 51.9 us)

commit v4 on v3

--- a/solution.py
+++ b/solution.py
@@ -451,7 +451,7 @@
 
 def backward_kernel(
     pairs, segments, mine, swapped, queries, kv_values, attention, capped,
-    query_grad, kv_grad, rewards_out, factors, *, full_width,
+    weight, query_grad, kv_grad, rewards_out, factors, far, *, full_width,
 ):
     bf16 = jnp.bfloat16
     width = full_width
@@ -485,19 +485,16 @@
     ratio = capped[...] / softcap_limit
     raw_grad = (score_grad * (1.0 - ratio * ratio) * (1.0 / math.sqrt(HD))).astype(bf16)
     order = member_order(here(), attn.shape[0])
-    query_grad[...] = matmul(order, matmul(raw_grad, keys).astype(bf16)).astype(bf16)
+    turned = matmul(order, matmul(raw_grad, keys).astype(bf16)).astype(bf16)
+    query_grad[...] = turned
+    block = far.shape[1] // 3
+    for step in (1, 2, 3):
+        start = pl.multiple_of(((here()[1] // 2) ^ step) * block, block)
+        far[:, (step - 1) * block : step * block] = matmul_nt(
+            turned, weight[pl.ds(start, block), :]
+        ).astype(far.dtype)
     kv_grad[:, :HD] = matmul_tn(raw_grad, queries[...])
     kv_grad[:, HD:] = matmul_tn(attn.astype(bf16), out_grad)
-
-
-def far_kernel(grad, weight, far):
-    place = here()
-    width = far.shape[1] // 3
-    for step in (1, 2, 3):
-        start = pl.multiple_of(((place[1] // 2) ^ step) * width, width)
-        far[:, (step - 1) * width : step * width] = matmul_nt(
-            grad[...], weight[pl.ds(start, width), :]
-        ).astype(far.dtype)
 
 
 def near_kernel(
@@ -652,21 +649,20 @@
         pair_order[1::2][:, None] == seq_ids
     ).astype(f32)
     pairs = jnp.concatenate([pairs, jnp.zeros_like(pairs)], axis=0)
-    query_grad, kv_grad, rewards, factors = local_call(
+    query_grad, kv_grad, rewards, factors, far_grad = local_call(
         functools.partial(backward_kernel, full_width=float(2 * half_width)),
         [
             ((tokens, HD), bf16),
             ((tokens, 2 * HD), f32),
             ((1, SEQS), f32),
             ((2, SEQS, HD), f32),
+            ((tokens, 3 * block_width), bf16),
         ],
         pairs, segments, report, core_swap(report), queries, kv_values, attention, capped,
+        query_piece,
     )
 
     kv_mine, kv_swapped = height_total(kv_grad, core, bf16)
-    (far_grad,) = local_call(
-        far_kernel, [((tokens, 3 * block_width), bf16)], query_grad, query_piece
-    )
     far_got = [
         send(far_grad[d * member_rows : (d + 1) * member_rows], lambda m, z, k, d=d: (m ^ d, z, k))
         for d in (1, 2, 3)

time: 95 us -> 95.1 us (level)
    pallas_call x12 -> x11, Pallas kernels: 4.75 us -> 4.47 us  [local_call(): pl.pallas_call(kernel, out_shape=[jax.ShapeDtypeStruct(shape, dtype) for...]
where the time goes in v4:
time: 95.1 us; the launch traced here: 94.5 us
  waiting for transfers between devices  41.7 us (44%)
  starting transfers between devices  41.5 us (44%)
  Pallas kernels  5.04 us (5%)
  local copies, waits for them, and re-layouts  4.48 us (5%)
  between operations  0.96 us (1%)
    ppermute x31, waiting for transfers between devices, send(): return lax.ppermute(block, ('member', 'shard'), route_pairs(target))  41.7 us
    ppermute x31, starting transfers between devices, send(): return lax.ppermute(block, ('member', 'shard'), route_pairs(target))  41.5 us
    pallas_call x11, Pallas kernels, local_call(): pl.pallas_call(kernel, out_shape=[jax.ShapeDtypeStruct(shape, dtype) for...  4.47 us
    unnamed x16, local copies, waits for them, and re-layouts  4.06 us
  transfers between devices with their start and end apart: 31, of which 18 were waited for; matrix products, arithmetic and copies ran while one was open for 1% of the time, Pallas kernels for 2%

profile of v4, /device:TPU:0, one launch (start us, length us, event | category | flops | bytes accessed | tf_op | source)
XLA Modules:
  0.0 94.5 jit_solution(18179227684628703972)
XLA Ops:
  0.6 3.1 %collective-permute-start = (bf16[16,2048]{1,0:T(8,128)(2,1)}, bf16[16,2048]{1,0:T(8,128)(2,1)S(1)}, u32[]{:S(2)}, u32[]{:S(2)}) collective-permute-start(bf16[16,2048]{1,0:T(8,128)(2,1)} %trunk.1), channel_id=1, source_target_pairs={{0,2},{1,3},{2,0},{3,1},{4,6},{5,7},{6,4},{7,5},{8,10},{9,11},{10,... | collective-permute-start | bytes 196616 | tf_op jit(solution)/shard_map/ppermute | solution.py:199
  3.8 2.6 %collective-permute-start.1 = (bf16[16,2048]{1,0:T(8,128)(2,1)}, bf16[16,2048]{1,0:T(8,128)(2,1)S(1)}, u32[]{:S(2)}, u32[]{:S(2)}) collective-permute-start(bf16[16,2048]{1,0:T(8,128)(2,1)} %trunk.1), channel_id=1, source_target_pairs={{0,4},{1,5},{2,6},{3,7},{4,0},{5,1},{6,2},{7,3},{8,12},{9,13},{10,... | collective-permute-start | bytes 196616 | tf_op jit(solution)/shard_map/ppermute | solution.py:199
  11.2 1.4 %collective-permute-done.2.refs_3_ = bf16[16,2048]{1,0:T(8,128)(2,1)S(1)} collective-permute-done((bf16[16,2048]{1,0:T(8,128)(2,1)}, bf16[16,2048]{1,0:T(8,128)(2,1)S(1)}, u32[]{:S(2)}, u32[]{:S(2)}) %collective-permute-start.2) | collective-permute-done | bytes 65568 | tf_op jit(solution)/shard_map/ppermute | solution.py:199
  13.9 1.6 %collective-permute-start.11 = (bf16[2048,128]{1,0:T(8,128)(2,1)S(1)}, bf16[2048,128]{1,0:T(8,128)(2,1)S(1)}, u32[]{:S(2)}, u32[]{:S(2)}) collective-permute-start(bf16[2048,128]{1,0:T(8,128)(2,1)S(1)} %get-tuple-element.52), channel_id=1, source_target_pairs={{0,8},{1,24},{2,10},{3,26},{4,12},{5,28},{6,14},{7,30},{8,0},{9,16... | collective-permute-start | bytes 1572872 | tf_op jit(solution)/shard_map/ppermute | solution.py:199
  16.2 2.6 %collective-permute-start.5 = (bf16[128,1024]{1,0:T(8,128)(2,1)S(1)}, bf16[128,1024]{1,0:T(8,128)(2,1)S(1)}, u32[]{:S(2)}, u32[]{:S(2)}) collective-permute-start(bf16[128,1024]{1,0:T(8,128)(2,1)S(1)} %shard_map.97), channel_id=1, source_target_pairs={{0,8},{1,24},{2,10},{3,26},{12,4},{13,20},{14,6},{15,22},{16,9},{1... | collective-permute-start | bytes 786440 | tf_op jit(solution)/shard_map/ppermute | solution.py:199
  18.7 12.4 %collective-permute-done.5.second = bf16[128,1024]{1,0:T(8,128)(2,1)S(1)} collective-permute-done((bf16[128,1024]{1,0:T(8,128)(2,1)S(1)}, bf16[128,1024]{1,0:T(8,128)(2,1)S(1)}, u32[]{:S(2)}, u32[]{:S(2)}) %collective-permute-start.5) | collective-permute-done | bytes 262176 | tf_op jit(solution)/shard_map/ppermute | solution.py:199
  31.5 2.4 %collective-permute-start.6 = (f32[128,256]{1,0:T(8,128)S(1)}, f32[128,256]{1,0:T(8,128)S(1)}, u32[]{:S(2)}, u32[]{:S(2)}) collective-permute-start(f32[128,256]{1,0:T(8,128)S(1)} %get-tuple-element.28), channel_id=1, source_target_pairs={{0,1},{1,0},{2,3},{3,2},{4,5},{5,4},{6,7},{7,6},{8,9},{9,8},{10,11... | collective-permute-start | bytes 393224 | tf_op jit(solution)/shard_map/ppermute | solution.py:199
  35.3 2.7 %collective-permute-start.12 = (f32[128,128]{1,0:T(8,128)S(1)}, f32[128,128]{1,0:T(8,128)S(1)}, u32[]{:S(2)}, u32[]{:S(2)}) collective-permute-start(f32[128,128]{1,0:T(8,128)S(1)} %shard_map.100), channel_id=1, source_target_pairs={{0,8},{1,24},{2,10},{3,26},{4,12},{5,28},{6,14},{7,30},{8,0},{9,16... | collective-permute-start | bytes 196616 | tf_op jit(solution)/shard_map/ppermute | solution.py:199
  38.0 2.2 %collective-permute-done.12 = f32[128,128]{1,0:T(8,128)S(1)} collective-permute-done((f32[128,128]{1,0:T(8,128)S(1)}, f32[128,128]{1,0:T(8,128)S(1)}, u32[]{:S(2)}, u32[]{:S(2)}) %collective-permute-start.12) | collective-permute-done | bytes 65568 | tf_op jit(solution)/shard_map/ppermute | solution.py:199
  40.4 3.6 %collective-permute-start.8 = (f16[128,128]{1,0:T(8,128)(2,1)S(1)}, f16[128,128]{1,0:T(8,128)(2,1)S(1)}, u32[]{:S(2)}, u32[]{:S(2)}) collective-permute-start(f16[128,128]{1,0:T(8,128)(2,1)S(1)} %slice_select_fusion.1), channel_id=1, source_target_pairs={{0,6},{1,7},{2,4},{3,5},{4,2},{5,3},{6,0},{7,1},{8,14},{9,15},{10,... | collective-permute-start | bytes 98312 | tf_op jit(solution)/shard_map/ppermute | solution.py:199
  44.1 1.5 %collective-permute-start.14 = (bf16[64,4096]{1,0:T(8,128)(2,1)S(1)}, bf16[64,4096]{1,0:T(8,128)(2,1)S(1)}, u32[]{:S(2)}, u32[]{:S(2)}) collective-permute-start(bf16[64,4096]{1,0:T(8,128)(2,1)S(1)} %get-tuple-element.50), channel_id=1, source_target_pairs={{0,1},{1,0},{2,3},{3,2},{4,5},{5,4},{6,7},{7,6},{8,9},{9,8},{10,11... | collective-permute-start | bytes 1572872 | tf_op jit(solution)/shard_map/ppermute | solution.py:199
  46.6 3.2 %collective-permute-start.13 = (f32[128,384]{1,0:T(8,128)S(1)}, f32[128,384]{1,0:T(8,128)S(1)}, u32[]{:S(2)}, u32[]{:S(2)}) collective-permute-start(f32[128,384]{1,0:T(8,128)S(1)} %pad_maximum_fusion.mine), channel_id=1, source_target_pairs={{0,1},{1,0},{2,3},{3,2},{4,5},{5,4},{6,7},{7,6},{8,9},{9,8},{10,11... | collective-permute-start | bytes 589832 | tf_op jit(solution)/shard_map/ppermute | solution.py:199
  51.9 1.9 %collective-permute-start.16 = (bf16[8,4224]{1,0:T(8,128)(2,1)S(1)}, bf16[8,4224]{1,0:T(8,128)(2,1)S(1)}, u32[]{:S(2)}, u32[]{:S(2)}) collective-permute-start(bf16[8,4224]{1,0:T(8,128)(2,1)S(1)} %get-tuple-element.32.first), channel_id=1, source_target_pairs={{0,4},{1,5},{2,6},{3,7},{4,0},{5,1},{6,2},{7,3},{8,12},{9,13},{10,... | collective-permute-start | bytes 202760 | tf_op jit(solution)/shard_map/ppermute | solution.py:199
  53.8 2.5 %collective-permute-start.17 = (bf16[8,4224]{1,0:T(8,128)(2,1)S(1)}, bf16[8,4224]{1,0:T(8,128)(2,1)S(1)}, u32[]{:S(2)}, u32[]{:S(2)}) collective-permute-start(bf16[8,4224]{1,0:T(8,128)(2,1)S(1)} %get-tuple-element.32.first), channel_id=1, source_target_pairs={{0,6},{1,7},{2,4},{3,5},{4,2},{5,3},{6,0},{7,1},{8,14},{9,15},{10,... | collective-permute-start | bytes 202760 | tf_op jit(solution)/shard_map/ppermute | solution.py:199
  57.4 3.4 %collective-permute-done.16.third = bf16[8,4224]{1,0:T(8,128)(2,1)S(1)} collective-permute-done((bf16[8,4224]{1,0:T(8,128)(2,1)S(1)}, bf16[8,4224]{1,0:T(8,128)(2,1)S(1)}, u32[]{:S(2)}, u32[]{:S(2)}) %collective-permute-start.16) | collective-permute-done | bytes 67616 | tf_op jit(solution)/shard_map/ppermute | solution.py:199
  62.5 1.4 %shard_map.103 = (bf16[128,128]{1,0:T(8,128)(2,1)S(1)}, f32[128,256]{1,0:T(8,128)S(1)}, f32[1,8]{1,0:T(1,128)}, f32[2,8,128]{2,1,0:T(8,128)S(1)}, bf16[128,3072]{1,0:T(8,128)(2,1)S(1)}) custom-call(f32[8,8]{1,0:T(8,128)S(1)} %concatenate.12.pairs, s32[1,128]{1,0:T(1,128)S(1)} %get-tuple-element.25.segments, f32[24,128]{1,0:T(8,128)S(1)} %get-tuple-element.33.mine, ...), custom_call_target="tpu_custom_call" | custom-call | tf_op jit(solution)/shard_map/pallas_call | solution.py:266
  63.9 2.1 %collective-permute-start.24 = (bf16[128,128]{1,0:T(8,128)(2,1)S(1)}, bf16[128,128]{1,0:T(8,128)(2,1)S(1)}, u32[]{:S(2)}, u32[]{:S(2)}) collective-permute-start(bf16[128,128]{1,0:T(8,128)(2,1)S(1)} %slice_select_fusion), channel_id=1, source_target_pairs={{0,6},{1,7},{2,4},{3,5},{4,2},{5,3},{6,0},{7,1},{8,14},{9,15},{10,... | collective-permute-start | bytes 98312 | tf_op jit(solution)/shard_map/ppermute | solution.py:199
  66.4 3.6 %collective-permute-done.24 = bf16[128,128]{1,0:T(8,128)(2,1)S(1)} collective-permute-done((bf16[128,128]{1,0:T(8,128)(2,1)S(1)}, bf16[128,128]{1,0:T(8,128)(2,1)S(1)}, u32[]{:S(2)}, u32[]{:S(2)}) %collective-permute-start.24) | collective-permute-done | bytes 32800 | tf_op jit(solution)/shard_map/ppermute | solution.py:199
  73.3 1.7 %collective-permute-start.21 = (bf16[32,3072]{1,0:T(8,128)(2,1)S(1)}, bf16[32,3072]{1,0:T(8,128)(2,1)S(1)}, u32[]{:S(2)}, u32[]{:S(2)}) collective-permute-start(bf16[32,3072]{1,0:T(8,128)(2,1)S(1)} %get-tuple-element.54), channel_id=1, source_target_pairs={{0,24},{1,25},{2,26},{3,27},{4,28},{5,29},{6,30},{7,31},{8,16},{9,... | collective-permute-start | bytes 589832 | tf_op jit(solution)/shard_map/ppermute | solution.py:199
  77.4 1.8 %collective-permute-done.19.first = bf16[32,3072]{1,0:T(8,128)(2,1)S(1)} collective-permute-done((bf16[32,3072]{1,0:T(8,128)(2,1)S(1)}, bf16[32,3072]{1,0:T(8,128)(2,1)S(1)}, u32[]{:S(2)}, u32[]{:S(2)}) %collective-permute-start.19) | collective-permute-done | bytes 196640 | tf_op jit(solution)/shard_map/ppermute | solution.py:199
  80.5 3.3 %collective-permute-done.20.second = bf16[32,3072]{1,0:T(8,128)(2,1)S(1)} collective-permute-done((bf16[32,3072]{1,0:T(8,128)(2,1)S(1)}, bf16[32,3072]{1,0:T(8,128)(2,1)S(1)}, u32[]{:S(2)}, u32[]{:S(2)}) %collective-permute-start.20) | collective-permute-done | bytes 196640 | tf_op jit(solution)/shard_map/ppermute | solution.py:199
  84.9 1.8 %collective-permute-done.28.third = bf16[32,1024]{1,0:T(8,128)(2,1)S(1)} collective-permute-done((bf16[32,1024]{1,0:T(8,128)(2,1)S(1)}, bf16[32,1024]{1,0:T(8,128)(2,1)S(1)}, u32[]{:S(2)}, u32[]{:S(2)}) %collective-permute-start.28) | collective-permute-done | bytes 65568 | tf_op jit(solution)/shard_map/ppermute | solution.py:199
  87.4 4.0 %collective-permute-done.22.first = bf16[32,2048]{1,0:T(8,128)(2,1)S(1)} collective-permute-done((bf16[32,2048]{1,0:T(8,128)(2,1)S(1)}, bf16[32,2048]{1,0:T(8,128)(2,1)S(1)}, u32[]{:S(2)}, u32[]{:S(2)}) %collective-permute-start.22) | collective-permute-done | bytes 131104 | tf_op jit(solution)/shard_map/ppermute | solution.py:199
  91.5 1.5 %collective-permute-start.30 = (bf16[32,1024]{1,0:T(8,128)(2,1)S(1)}, bf16[32,1024]{1,0:T(8,128)(2,1)S(1)}, u32[]{:S(2)}, u32[]{:S(2)}) collective-permute-start(bf16[32,1024]{1,0:T(8,128)(2,1)S(1)} %get-tuple-element.46), channel_id=1, source_target_pairs={{0,1},{1,0},{2,3},{3,2},{4,5},{5,4},{6,7},{7,6},{8,9},{9,8},{10,11... | collective-permute-start | bytes 196616 | tf_op jit(solution)/shard_map/ppermute | solution.py:199
  (86 shorter events, 25.2 us)
Async XLA Ops:
  0.6 10.0 %collective-permute-start = (bf16[16,2048]{1,0:T(8,128)(2,1)}, bf16[16,2048]{1,0:T(8,128)(2,1)S(1)}, u32[]{:S(2)}, u32[]{:S(2)}) collective-permute-start(bf16[16,2048]{1,0:T(8,128)(2,1)} %trunk.1), channel_id=1, source_target_pairs={{0,2},{1,3},{2,0},{3,1},{4,6},{5,7},{6,4},{7,5},{8,10},{9,11},{10,... | collective-permute-start | bytes 196616 | tf_op jit(solution)/shard_map/ppermute | solution.py:199
  3.8 7.5 %collective-permute-start.1 = (bf16[16,2048]{1,0:T(8,128)(2,1)}, bf16[16,2048]{1,0:T(8,128)(2,1)S(1)}, u32[]{:S(2)}, u32[]{:S(2)}) collective-permute-start(bf16[16,2048]{1,0:T(8,128)(2,1)} %trunk.1), channel_id=1, source_target_pairs={{0,4},{1,5},{2,6},{3,7},{4,0},{5,1},{6,2},{7,3},{8,12},{9,13},{10,... | collective-permute-start | bytes 196616 | tf_op jit(solution)/shard_map/ppermute | solution.py:199
  6.3 6.3 %collective-permute-start.2 = (bf16[16,2048]{1,0:T(8,128)(2,1)}, bf16[16,2048]{1,0:T(8,128)(2,1)S(1)}, u32[]{:S(2)}, u32[]{:S(2)}) collective-permute-start(bf16[16,2048]{1,0:T(8,128)(2,1)} %trunk.1), channel_id=1, source_target_pairs={{0,6},{1,7},{2,4},{3,5},{4,2},{5,3},{6,0},{7,1},{8,14},{9,15},{10,... | collective-permute-start | bytes 196616 | tf_op jit(solution)/shard_map/ppermute | solution.py:199
  13.2 20.7 %collective-permute-start.9 = (bf16[2048,128]{1,0:T(8,128)(2,1)S(1)}, bf16[2048,128]{1,0:T(8,128)(2,1)S(1)}, u32[]{:S(2)}, u32[]{:S(2)}) collective-permute-start(bf16[2048,128]{1,0:T(8,128)(2,1)S(1)} %get-tuple-element.53), channel_id=1, source_target_pairs={{0,0},{1,16},{2,2},{3,18},{4,4},{5,20},{6,6},{7,22},{8,8},{9,24},{... | collective-permute-start | bytes 1572872 | tf_op jit(solution)/shard_map/ppermute | solution.py:199
  13.9 21.1 %collective-permute-start.11 = (bf16[2048,128]{1,0:T(8,128)(2,1)S(1)}, bf16[2048,128]{1,0:T(8,128)(2,1)S(1)}, u32[]{:S(2)}, u32[]{:S(2)}) collective-permute-start(bf16[2048,128]{1,0:T(8,128)(2,1)S(1)} %get-tuple-element.52), channel_id=1, source_target_pairs={{0,8},{1,24},{2,10},{3,26},{4,12},{5,28},{6,14},{7,30},{8,0},{9,16... | collective-permute-start | bytes 1572872 | tf_op jit(solution)/shard_map/ppermute | solution.py:199
  16.2 15.0 %collective-permute-start.5 = (bf16[128,1024]{1,0:T(8,128)(2,1)S(1)}, bf16[128,1024]{1,0:T(8,128)(2,1)S(1)}, u32[]{:S(2)}, u32[]{:S(2)}) collective-permute-start(bf16[128,1024]{1,0:T(8,128)(2,1)S(1)} %shard_map.97), channel_id=1, source_target_pairs={{0,8},{1,24},{2,10},{3,26},{12,4},{13,20},{14,6},{15,22},{16,9},{1... | collective-permute-start | bytes 786440 | tf_op jit(solution)/shard_map/ppermute | solution.py:199
  31.5 8.8 %collective-permute-start.6 = (f32[128,256]{1,0:T(8,128)S(1)}, f32[128,256]{1,0:T(8,128)S(1)}, u32[]{:S(2)}, u32[]{:S(2)}) collective-permute-start(f32[128,256]{1,0:T(8,128)S(1)} %get-tuple-element.28), channel_id=1, source_target_pairs={{0,1},{1,0},{2,3},{3,2},{4,5},{5,4},{6,7},{7,6},{8,9},{9,8},{10,11... | collective-permute-start | bytes 393224 | tf_op jit(solution)/shard_map/ppermute | solution.py:199
  35.3 5.0 %collective-permute-start.12 = (f32[128,128]{1,0:T(8,128)S(1)}, f32[128,128]{1,0:T(8,128)S(1)}, u32[]{:S(2)}, u32[]{:S(2)}) collective-permute-start(f32[128,128]{1,0:T(8,128)S(1)} %shard_map.100), channel_id=1, source_target_pairs={{0,8},{1,24},{2,10},{3,26},{4,12},{5,28},{6,14},{7,30},{8,0},{9,16... | collective-permute-start | bytes 196616 | tf_op jit(solution)/shard_map/ppermute | solution.py:199
  40.3 6.3 %collective-permute-start.7 = (f16[128,256]{1,0:T(8,128)(2,1)S(1)}, f16[128,256]{1,0:T(8,128)(2,1)S(1)}, u32[]{:S(2)}, u32[]{:S(2)}) collective-permute-start(f16[128,256]{1,0:T(8,128)(2,1)S(1)} %fusion), channel_id=1, source_target_pairs={{0,2},{1,5},{2,0},{3,7},{4,6},{5,1},{6,4},{7,3},{8,10},{9,13},{10,... | collective-permute-start | bytes 196616 | tf_op jit(solution)/shard_map/ppermute | solution.py:199
  40.4 6.1 %collective-permute-start.8 = (f16[128,128]{1,0:T(8,128)(2,1)S(1)}, f16[128,128]{1,0:T(8,128)(2,1)S(1)}, u32[]{:S(2)}, u32[]{:S(2)}) collective-permute-start(f16[128,128]{1,0:T(8,128)(2,1)S(1)} %slice_select_fusion.1), channel_id=1, source_target_pairs={{0,6},{1,7},{2,4},{3,5},{4,2},{5,3},{6,0},{7,1},{8,14},{9,15},{10,... | collective-permute-start | bytes 98312 | tf_op jit(solution)/shard_map/ppermute | solution.py:199
  44.1 6.8 %collective-permute-start.14 = (bf16[64,4096]{1,0:T(8,128)(2,1)S(1)}, bf16[64,4096]{1,0:T(8,128)(2,1)S(1)}, u32[]{:S(2)}, u32[]{:S(2)}) collective-permute-start(bf16[64,4096]{1,0:T(8,128)(2,1)S(1)} %get-tuple-element.50), channel_id=1, source_target_pairs={{0,1},{1,0},{2,3},{3,2},{4,5},{5,4},{6,7},{7,6},{8,9},{9,8},{10,11... | collective-permute-start | bytes 1572872 | tf_op jit(solution)/shard_map/ppermute | solution.py:199
  51.9 5.4 %collective-permute-start.15 = (bf16[8,4224]{1,0:T(8,128)(2,1)S(1)}, bf16[8,4224]{1,0:T(8,128)(2,1)S(1)}, u32[]{:S(2)}, u32[]{:S(2)}) collective-permute-start(bf16[8,4224]{1,0:T(8,128)(2,1)S(1)} %get-tuple-element.32.first), channel_id=1, source_target_pairs={{0,2},{1,3},{2,0},{3,1},{4,6},{5,7},{6,4},{7,5},{8,10},{9,11},{10,... | collective-permute-start | bytes 202760 | tf_op jit(solution)/shard_map/ppermute | solution.py:199
  51.9 8.9 %collective-permute-start.16 = (bf16[8,4224]{1,0:T(8,128)(2,1)S(1)}, bf16[8,4224]{1,0:T(8,128)(2,1)S(1)}, u32[]{:S(2)}, u32[]{:S(2)}) collective-permute-start(bf16[8,4224]{1,0:T(8,128)(2,1)S(1)} %get-tuple-element.32.first), channel_id=1, source_target_pairs={{0,4},{1,5},{2,6},{3,7},{4,0},{5,1},{6,2},{7,3},{8,12},{9,13},{10,... | collective-permute-start | bytes 202760 | tf_op jit(solution)/shard_map/ppermute | solution.py:199
  53.8 7.0 %collective-permute-start.17 = (bf16[8,4224]{1,0:T(8,128)(2,1)S(1)}, bf16[8,4224]{1,0:T(8,128)(2,1)S(1)}, u32[]{:S(2)}, u32[]{:S(2)}) collective-permute-start(bf16[8,4224]{1,0:T(8,128)(2,1)S(1)} %get-tuple-element.32.first), channel_id=1, source_target_pairs={{0,6},{1,7},{2,4},{3,5},{4,2},{5,3},{6,0},{7,1},{8,14},{9,15},{10,... | collective-permute-start | bytes 202760 | tf_op jit(solution)/shard_map/ppermute | solution.py:199
  63.9 6.1 %collective-permute-start.24 = (bf16[128,128]{1,0:T(8,128)(2,1)S(1)}, bf16[128,128]{1,0:T(8,128)(2,1)S(1)}, u32[]{:S(2)}, u32[]{:S(2)}) collective-permute-start(bf16[128,128]{1,0:T(8,128)(2,1)S(1)} %slice_select_fusion), channel_id=1, source_target_pairs={{0,6},{1,7},{2,4},{3,5},{4,2},{5,3},{6,0},{7,1},{8,14},{9,15},{10,... | collective-permute-start | bytes 98312 | tf_op jit(solution)/shard_map/ppermute | solution.py:199
  66.0 5.2 %collective-permute-start.23 = (bf16[128,256]{1,0:T(8,128)(2,1)S(1)}, bf16[128,256]{1,0:T(8,128)(2,1)S(1)}, u32[]{:S(2)}, u32[]{:S(2)}) collective-permute-start(bf16[128,256]{1,0:T(8,128)(2,1)S(1)} %convert_element_type.39), channel_id=1, source_target_pairs={{0,2},{1,5},{2,0},{3,7},{4,6},{5,1},{6,4},{7,3},{8,10},{9,13},{10,... | collective-permute-start | bytes 196616 | tf_op jit(solution)/shard_map/ppermute | solution.py:199
  71.4 7.8 %collective-permute-start.19 = (bf16[32,3072]{1,0:T(8,128)(2,1)S(1)}, bf16[32,3072]{1,0:T(8,128)(2,1)S(1)}, u32[]{:S(2)}, u32[]{:S(2)}) collective-permute-start(bf16[32,3072]{1,0:T(8,128)(2,1)S(1)} %get-tuple-element.56), channel_id=1, source_target_pairs={{0,8},{1,9},{2,10},{3,11},{4,12},{5,13},{6,14},{7,15},{8,0},{9,1},... | collective-permute-start | bytes 589832 | tf_op jit(solution)/shard_map/ppermute | solution.py:199
  72.1 11.6 %collective-permute-start.20 = (bf16[32,3072]{1,0:T(8,128)(2,1)S(1)}, bf16[32,3072]{1,0:T(8,128)(2,1)S(1)}, u32[]{:S(2)}, u32[]{:S(2)}) collective-permute-start(bf16[32,3072]{1,0:T(8,128)(2,1)S(1)} %get-tuple-element.55), channel_id=1, source_target_pairs={{0,16},{1,17},{2,18},{3,19},{4,20},{5,21},{6,22},{7,23},{8,24},{9,... | collective-permute-start | bytes 589832 | tf_op jit(solution)/shard_map/ppermute | solution.py:199
  73.3 11.1 %collective-permute-start.21 = (bf16[32,3072]{1,0:T(8,128)(2,1)S(1)}, bf16[32,3072]{1,0:T(8,128)(2,1)S(1)}, u32[]{:S(2)}, u32[]{:S(2)}) collective-permute-start(bf16[32,3072]{1,0:T(8,128)(2,1)S(1)} %get-tuple-element.54), channel_id=1, source_target_pairs={{0,24},{1,25},{2,26},{3,27},{4,28},{5,29},{6,30},{7,31},{8,16},{9,... | collective-permute-start | bytes 589832 | tf_op jit(solution)/shard_map/ppermute | solution.py:199
  75.5 9.3 %collective-permute-start.26 = (bf16[32,1024]{1,0:T(8,128)(2,1)S(1)}, bf16[32,1024]{1,0:T(8,128)(2,1)S(1)}, u32[]{:S(2)}, u32[]{:S(2)}) collective-permute-start(bf16[32,1024]{1,0:T(8,128)(2,1)S(1)} %get-tuple-element.59), channel_id=1, source_target_pairs={{0,8},{1,9},{2,10},{3,11},{4,12},{5,13},{6,14},{7,15},{8,0},{9,1},... | collective-permute-start | bytes 196616 | tf_op jit(solution)/shard_map/ppermute | solution.py:199
  76.3 8.6 %collective-permute-start.27 = (bf16[32,1024]{1,0:T(8,128)(2,1)S(1)}, bf16[32,1024]{1,0:T(8,128)(2,1)S(1)}, u32[]{:S(2)}, u32[]{:S(2)}) collective-permute-start(bf16[32,1024]{1,0:T(8,128)(2,1)S(1)} %get-tuple-element.58), channel_id=1, source_target_pairs={{0,16},{1,17},{2,18},{3,19},{4,20},{5,21},{6,22},{7,23},{8,24},{9,... | collective-permute-start | bytes 196616 | tf_op jit(solution)/shard_map/ppermute | solution.py:199
  79.2 7.5 %collective-permute-start.28 = (bf16[32,1024]{1,0:T(8,128)(2,1)S(1)}, bf16[32,1024]{1,0:T(8,128)(2,1)S(1)}, u32[]{:S(2)}, u32[]{:S(2)}) collective-permute-start(bf16[32,1024]{1,0:T(8,128)(2,1)S(1)} %get-tuple-element.57), channel_id=1, source_target_pairs={{0,24},{1,25},{2,26},{3,27},{4,28},{5,29},{6,30},{7,31},{8,16},{9,... | collective-permute-start | bytes 196616 | tf_op jit(solution)/shard_map/ppermute | solution.py:199
  84.4 7.0 %collective-permute-start.22 = (bf16[32,2048]{1,0:T(8,128)(2,1)S(1)}, bf16[32,2048]{1,0:T(8,128)(2,1)S(1)}, u32[]{:S(2)}, u32[]{:S(2)}) collective-permute-start(bf16[32,2048]{1,0:T(8,128)(2,1)S(1)} %get-tuple-element.39), channel_id=1, source_target_pairs={{0,2},{1,6},{2,3},{3,7},{4,0},{5,4},{6,1},{7,5},{8,10},{9,14},{10,... | collective-permute-start | bytes 393224 | tf_op jit(solution)/shard_map/ppermute | solution.py:199
  86.7 4.7 %collective-permute-start.29 = (bf16[32,2048]{1,0:T(8,128)(2,1)S(1)}, bf16[32,2048]{1,0:T(8,128)(2,1)S(1)}, u32[]{:S(2)}, u32[]{:S(2)}) collective-permute-start(bf16[32,2048]{1,0:T(8,128)(2,1)S(1)} %shard_map.106), channel_id=1, source_target_pairs={{0,0},{1,4},{2,1},{3,5},{4,2},{5,6},{6,3},{7,7},{8,8},{9,12},{10,9... | collective-permute-start | bytes 393224 | tf_op jit(solution)/shard_map/ppermute | solution.py:199
  (15 other events, 51.9 us)
